TPU v7x, 512 devices: a whole 4x4x16 slice. The times are simulated.
512 devices in a mesh: group: 16 (over z), shard: 32 (over y, x, core).
Axes of the slice: x: 4, y: 4, z: 16, core: 2. Of those that a mesh axis runs over, the one named last changes fastest.
Arguments:
- hot_row: int32 [4096, 39], P(('group', 'shard')), may hold values from 0 to 2047
- cold_row: int32 [4096, 39], P(('group', 'shard')), may hold values from 0 to 4095
- cold_owner: int32 [4096, 39], P(('group', 'shard')), may hold values from 0 to 31, as said below
- is_cold: int32 [4096, 39], P(('group', 'shard')), may hold values from 0 to 1
- grad_logit: float32 [4096], P(('group', 'shard')), may hold values from -12 to 12
- hot_table: bfloat16 [2048, 128], replicated, may hold values from -6 to 6
- cold_table: bfloat16 [131072, 128], P('shard'), may hold values from -6 to 6
- first_weight: bfloat16 [100, 1521], replicated, may hold values from -0.15625 to 0.15625
- second_weight: bfloat16 [100, 3900], replicated, may hold values from -0.09375 to 0.09375
- third_weight: bfloat16 [100, 3900], replicated, may hold values from -0.09375 to 0.09375
- out_weight: float32 [3, 100], replicated, may hold values from -0.375 to 0.375
Outputs:
- hot_grad: bfloat16 [2048, 128], replicated
- cold_grad: bfloat16 [131072, 128], P('shard')
- logits: float32 [4096], P(('group', 'shard'))
Inputs may be any that keep to these rules, and one draw needn't show every extreme that they name: `cold_owner`: among the 312 lookups of one device, at most 9 with is_cold 1 name the same owner; for each index of group, one owner receives exactly 9 such lookups from every device of that group index.
All inputs are finite; a program needn't handle non-finite values.
Results may differ from a plain program's by a relative error of at most 0.014.
Values may be sent and summed in bfloat16 or wider, within the bound.
No kernel may reach another device: no remote copies, remote signals or barrier semaphores. Data moves between devices by JAX's collectives and lax.ppermute only.
A program may use at most 64 MiB of HBM per device.

v0:
```python
import jax
import jax.numpy as jnp
from jax import lax
from jax.sharding import PartitionSpec as P


def sample_pass(embedded, grad_logit, layer_weights, out_weight):
    batch_rows, fields, breadth = embedded.shape
    base_wide = embedded.astype(jnp.float32)
    previous = embedded
    layer_inputs = []
    logit_sum = jnp.zeros((batch_rows,), jnp.float32)
    for section_index in range(len(layer_weights)):
        weight = layer_weights[section_index]
        below_maps = previous.shape[1]
        outer_rows = (
            previous.astype(jnp.float32)[:, :, None, :] * base_wide[:, None, :, :]
        ).astype(jnp.bfloat16)
        outer_rows = outer_rows.reshape(batch_rows, below_maps * fields, breadth)
        current = jnp.einsum(
            "hk,bke->bhe", weight, outer_rows, preferred_element_type=jnp.float32
        ).astype(jnp.bfloat16)
        pooled = jnp.sum(current.astype(jnp.float32), axis=2)
        logit_sum = logit_sum + jnp.sum(pooled * out_weight[section_index][None, :], axis=1)
        layer_inputs.append(previous)
        previous = current
    grad_embedded = jnp.zeros((batch_rows, fields, breadth), jnp.float32)
    carried = jnp.zeros((batch_rows, out_weight.shape[1], breadth), jnp.float32)
    for section_index in reversed(range(len(layer_weights))):
        weight = layer_weights[section_index]
        lower_state = layer_inputs[section_index]
        below_maps = lower_state.shape[1]
        grad_state = carried + grad_logit[:, None, None] * out_weight[section_index][None, :, None]
        grad_low = grad_state.astype(jnp.bfloat16)
        grad_outer = jnp.einsum("hk,bhe->bke", weight, grad_low, preferred_element_type=jnp.float32)
        grad_outer = grad_outer.reshape(batch_rows, below_maps, fields, breadth)
        grad_embedded = grad_embedded + jnp.sum(
            grad_outer * lower_state.astype(jnp.float32)[:, :, None, :], axis=1
        )
        carried = jnp.sum(grad_outer * base_wide[:, None, :, :], axis=2)
    grad_embedded = grad_embedded + carried
    return (logit_sum, grad_embedded)


def local(
    hot_row,
    cold_row,
    cold_owner,
    is_cold,
    grad_logit,
    hot_table,
    cold_table,
    first_weight,
    second_weight,
    third_weight,
    out_weight,
):
    samples, fields = hot_row.shape
    breadth = hot_table.shape[1]
    owners = lax.axis_size("shard")
    lookups = samples * fields
    capacity = lookups // owners
    owner_flat = cold_owner.reshape(lookups)
    cold_flag = is_cold.reshape(lookups) == 1
    wanted = jnp.logical_and(
        owner_flat[:, None] == jnp.arange(owners, dtype=jnp.int32)[None, :], cold_flag[:, None]
    ).astype(jnp.int32)
    earlier = jnp.cumsum(wanted, axis=0) - wanted
    position = jnp.sum(earlier * wanted, axis=1)
    target = jnp.where(cold_flag, owner_flat * capacity + position, owners * capacity)
    asked_rows = jnp.where(cold_flag, cold_row.reshape(lookups), -1)
    request = jnp.full((owners * capacity + 1,), -1, jnp.int32).at[target].set(asked_rows)
    request = request[: owners * capacity].reshape(owners, capacity)
    requested = lax.all_to_all(request, "shard", split_axis=0, concat_axis=0, tiled=True)
    present = requested >= 0
    table_rows = jnp.take(cold_table, jnp.maximum(requested, 0), axis=0)
    table_rows = jnp.where(present[:, :, None], table_rows, jnp.zeros_like(table_rows))
    returned = lax.all_to_all(table_rows, "shard", split_axis=0, concat_axis=0, tiled=True)
    fetched_flat = jnp.concatenate(
        [returned.reshape(owners * capacity, breadth), jnp.zeros((1, breadth), jnp.bfloat16)],
        axis=0,
    )
    cold_values = jnp.take(fetched_flat, target, axis=0)
    hot_values = jnp.take(hot_table, hot_row.reshape(lookups), axis=0)
    embedded = jnp.where(cold_flag[:, None], cold_values, hot_values).reshape(
        samples, fields, breadth
    )
    layer_weights = (first_weight, second_weight, third_weight)

    def one_sample(sample_pair):
        logit_one, grad_one = sample_pass(
            sample_pair[0][None], sample_pair[1][None], layer_weights, out_weight
        )
        return (logit_one[0], grad_one[0])

    logits, gradients = lax.map(one_sample, (embedded, grad_logit))
    gradients = gradients.reshape(lookups, breadth)
    cold_terms = jnp.where(cold_flag[:, None], gradients, 0.0)
    hot_terms = jnp.where(cold_flag[:, None], 0.0, gradients)
    outgoing = jnp.zeros((owners * capacity + 1, breadth), jnp.float32).at[target].add(cold_terms)
    outgoing = outgoing[: owners * capacity].reshape(owners, capacity, breadth)
    incoming = lax.all_to_all(
        outgoing.astype(jnp.bfloat16), "shard", split_axis=0, concat_axis=0, tiled=True
    ).astype(outgoing.dtype)
    shard_rows = cold_table.shape[0]
    safe_ids = jnp.maximum(requested, 0)
    cold_local = jax.ops.segment_sum(
        incoming.reshape(-1, breadth), safe_ids.reshape(-1), num_segments=shard_rows
    )
    cold_total = lax.psum(cold_local.astype(jnp.bfloat16), "group")
    hot_local = jax.ops.segment_sum(
        hot_terms, hot_row.reshape(lookups), num_segments=hot_table.shape[0]
    )
    hot_grad = lax.psum(hot_local, ("group", "shard")).astype(jnp.bfloat16)
    return (hot_grad, cold_total, logits)


def solution(mesh):
    return jax.shard_map(
        local,
        mesh=mesh,
        in_specs=(
            P(("group", "shard"), None),
            P(("group", "shard"), None),
            P(("group", "shard"), None),
            P(("group", "shard"), None),
            P(("group", "shard")),
            P(),
            P("shard", None),
            P(),
            P(),
            P(),
            P(),
        ),
        out_specs=(P(), P("shard", None), P(("group", "shard"))),
        check_vma=False,
    )
```

profile of v0, /device:TPU:6, one launch (start us, length us, event | category | flops | bytes accessed | tf_op | source)
XLA Modules:
  0.0 380.3 jit_solution(5741558667474088209)
XLA Ops:
  11.8 2.9 scatter_custom_fusion
  15.4 9.3 %all-to-all-start = ((s32[32,1,9]{2,1,0:T(1,128)}), s32[32,1,9]{2,1,0:T(1,128)S(1)}, u32[]{:S(2)}, u32[]{:S(2)}) async-start(s32[32,1,9]{2,1,0:T(1,128)} %bitcast.28), calls=%async_computation | async-start | bytes 32768 | tf_op jit(solution)/shard_map/all_to_all | solution.py:74
  26.4 2.3 gather_fusion.2
  33.2 5.9 %all-to-all-start.1 = ((bf16[32,9,128]{2,1,0:T(8,128)(2,1)}), bf16[32,9,128]{2,1,0:T(8,128)(2,1)S(1)}, u32[]{:S(2)}, u32[]{:S(2)}) async-start(bf16[32,9,128]{2,1,0:T(8,128)(2,1)} %select_select_fusion), calls=%async_computation.1 | async-start | bytes 262144 | tf_op jit(solution)/shard_map/all_to_all | solution.py:78
  39.1 6.0 %all-to-all-done.1 = bf16[32,9,128]{2,1,0:T(8,128)(2,1)S(1)} async-done(((bf16[32,9,128]{2,1,0:T(8,128)(2,1)}), bf16[32,9,128]{2,1,0:T(8,128)(2,1)S(1)}, u32[]{:S(2)}, u32[]{:S(2)}) %all-to-all-start.1) | async-done | bytes 73760 | tf_op jit(solution)/shard_map/all_to_all | solution.py:78
  47.5 165.5 %while.12 = (s32[]{:T(128)}, f32[8]{0:T(128)}, f32[8,39,128]{2,1,0:T(8,128)}, bf16[8,39,128]{2,1,0:T(8,128)(2,1)}, bf16[100,1521]{1,0:T(8,128)(2,1)S(1)}, /*inde...) while((s32[]{:T(128)}, f32[8]{0:T(128)}, ...), condition=%wide.region_17.18_spmd, body=%wide.region_4.17_spmd.sunk | while | flops 484535232 | bytes 39531044 | solution.py:96
  51.4 1.7 fusion.66
  55.7 1.8 convolution_bitcast_fusion.6
  60.3 1.8 convolution_bitcast_fusion.7
  72.1 1.7 fusion.66
  76.4 1.8 convolution_bitcast_fusion.6
  81.0 1.8 convolution_bitcast_fusion.7
  97.1 1.8 convolution_bitcast_fusion.6
  101.7 1.8 convolution_bitcast_fusion.7
  113.4 1.7 fusion.66
  117.8 1.8 convolution_bitcast_fusion.6
  122.4 1.8 convolution_bitcast_fusion.7
  138.5 1.8 convolution_bitcast_fusion.6
  143.1 1.8 convolution_bitcast_fusion.7
  159.2 1.8 convolution_bitcast_fusion.6
  163.7 1.8 convolution_bitcast_fusion.7
  179.8 1.8 convolution_bitcast_fusion.6
  184.4 1.8 convolution_bitcast_fusion.7
  200.5 1.8 convolution_bitcast_fusion.6
  205.1 1.8 convolution_bitcast_fusion.7
  213.9 2.1 scatter_custom_fusion.2
  216.1 11.5 %all_to_all.19 = bf16[32,9,128]{2,1,0:T(8,128)(2,1)S(1)} all-to-all(bf16[32,9,128]{2,1,0:T(8,128)(2,1)S(1)} %convert_element_type.112), channel_id=1, replica_groups=mesh['group'=16,'shard'=32] {'shard'}, dimensions={0} | all-to-all | bytes 147456 | tf_op jit(solution)/shard_map/all_to_all | solution.py:102
  227.6 2.4 scatter_custom_fusion.3
  231.2 2.0 scatter_custom_fusion.1
  233.2 111.5 %all-reduce.6 = bf16[2048,128]{1,0:T(8,128)(2,1)} all-reduce(f32[2048,128]{1,0:T(8,128)S(1)} %scatter_custom_fusion.1), channel_id=1, replica_groups=mesh['group'=16,'shard'=32] {'group','shard'}, use_global_device_ids=true, to_apply=%region_19.20 | all-reduce | flops 262144 | bytes 1572864 | tf_op jit(solution)/shard_map/psum | solution.py:114
  344.7 26.5 %all-reduce.5.cloned.1.call-done = bf16[4096,128]{1,0:T(8,128)(2,1)} async-done(((bf16[4096,128]{1,0:T(8,128)(2,1)}), bf16[4096,128]{1,0:T(8,128)(2,1)}) %all-reduce.5.cloned.1.call-update) | async-done | bytes 1048592 | tf_op jit(solution)/shard_map/psum | solution.py:110
  371.2 2.3 copy.47
  (312 shorter events, 131.3 us)
Async XLA Ops:
  7.2 23.5 %copy-start = (bf16[4096,128]{1,0:T(8,128)(2,1)S(1)}, bf16[4096,128]{1,0:T(8,128)(2,1)}, u32[]{:S(2)}) copy-start(bf16[4096,128]{1,0:T(8,128)(2,1)} %param.19) | copy-start | bytes 3145732
  8.0 22.6 %copy-start.7 = (pred[312]{0:T(512)(128)(4,1)}, pred[312]{0:T(512)(128)(4,1)S(1)}, u32[]{:S(2)}) copy-start(pred[312]{0:T(512)(128)(4,1)S(1)} %eq.48) | copy-start | bytes 940
  11.8 34.8 %copy-start.9 = (s32[312]{0:T(512)}, s32[312]{0:T(512)S(1)}, u32[]{:S(2)}) copy-start(s32[312]{0:T(512)S(1)} %fusion.26) | copy-start | bytes 3748
  15.4 14.9 %all-to-all-start = ((s32[32,1,9]{2,1,0:T(1,128)}), s32[32,1,9]{2,1,0:T(1,128)S(1)}, u32[]{:S(2)}, u32[]{:S(2)}) async-start(s32[32,1,9]{2,1,0:T(1,128)} %bitcast.28), calls=%async_computation | async-start | bytes 32768 | tf_op jit(solution)/shard_map/all_to_all | solution.py:74
  26.4 21.1 %copy-start.3 = (bf16[100,1521]{1,0:T(8,128)(2,1)S(1)}, bf16[100,1521]{1,0:T(8,128)(2,1)}, u32[]{:S(2)}) copy-start(bf16[100,1521]{1,0:T(8,128)(2,1)} %param.20) | copy-start | bytes 912604
  26.4 21.1 %copy-start.6 = (f32[3,100]{1,0:T(4,128)S(1)}, f32[3,100]{1,0:T(4,128)}, u32[]{:S(2)}) copy-start(f32[3,100]{1,0:T(4,128)} %param.23) | copy-start | bytes 3604
  30.6 8.5 %copy-start.10 = (s32[288]{0:T(512)}, s32[288]{0:T(512)S(1)}, u32[]{:S(2)}) copy-start(s32[288]{0:T(512)S(1)} %reshape.473) | copy-start | bytes 3460
  33.2 12.0 %all-to-all-start.1 = ((bf16[32,9,128]{2,1,0:T(8,128)(2,1)}), bf16[32,9,128]{2,1,0:T(8,128)(2,1)S(1)}, u32[]{:S(2)}, u32[]{:S(2)}) async-start(bf16[32,9,128]{2,1,0:T(8,128)(2,1)} %select_select_fusion), calls=%async_computation.1 | async-start | bytes 262144 | tf_op jit(solution)/shard_map/all_to_all | solution.py:78
  39.1 332.1 %all-reduce.5.cloned.1.call-start = ((), (), s32[]{:S(2)}) async-start(), calls=%async_computation.3 | async-start | bytes 2097152 | tf_op jit(solution)/shard_map/psum | solution.py:110
  51.4 4.4 %copy-start.2 = (bf16[100,3900]{1,0:T(8,128)(2,1)S(1)}, bf16[100,3900]{1,0:T(8,128)(2,1)}, u32[]{:S(2)}) copy-start(bf16[100,3900]{1,0:T(8,128)(2,1)} %get-tuple-element.208) | copy-start | bytes 2340004 | tf_op jit(solution)/shard_map/while
  59.2 1.1 copy-start.1
  64.4 3.1 copy-start.11
  72.1 4.4 %copy-start.2 = (bf16[100,3900]{1,0:T(8,128)(2,1)S(1)}, bf16[100,3900]{1,0:T(8,128)(2,1)}, u32[]{:S(2)}) copy-start(bf16[100,3900]{1,0:T(8,128)(2,1)} %get-tuple-element.208) | copy-start | bytes 2340004 | tf_op jit(solution)/shard_map/while
  79.9 1.1 copy-start.1
  85.1 3.1 copy-start.11
  92.7 4.4 %copy-start.2 = (bf16[100,3900]{1,0:T(8,128)(2,1)S(1)}, bf16[100,3900]{1,0:T(8,128)(2,1)}, u32[]{:S(2)}) copy-start(bf16[100,3900]{1,0:T(8,128)(2,1)} %get-tuple-element.208) | copy-start | bytes 2340004 | tf_op jit(solution)/shard_map/while
  100.5 1.1 copy-start.1
  105.8 3.1 copy-start.11
  113.4 4.4 %copy-start.2 = (bf16[100,3900]{1,0:T(8,128)(2,1)S(1)}, bf16[100,3900]{1,0:T(8,128)(2,1)}, u32[]{:S(2)}) copy-start(bf16[100,3900]{1,0:T(8,128)(2,1)} %get-tuple-element.208) | copy-start | bytes 2340004 | tf_op jit(solution)/shard_map/while
  121.2 1.1 copy-start.1
  126.4 3.1 copy-start.11
  134.1 4.4 %copy-start.2 = (bf16[100,3900]{1,0:T(8,128)(2,1)S(1)}, bf16[100,3900]{1,0:T(8,128)(2,1)}, u32[]{:S(2)}) copy-start(bf16[100,3900]{1,0:T(8,128)(2,1)} %get-tuple-element.208) | copy-start | bytes 2340004 | tf_op jit(solution)/shard_map/while
  141.9 1.1 copy-start.1
  147.1 3.1 copy-start.11
  154.8 4.4 %copy-start.2 = (bf16[100,3900]{1,0:T(8,128)(2,1)S(1)}, bf16[100,3900]{1,0:T(8,128)(2,1)}, u32[]{:S(2)}) copy-start(bf16[100,3900]{1,0:T(8,128)(2,1)} %get-tuple-element.208) | copy-start | bytes 2340004 | tf_op jit(solution)/shard_map/while
  162.6 1.1 copy-start.1
  167.8 3.1 copy-start.11
  175.5 4.4 %copy-start.2 = (bf16[100,3900]{1,0:T(8,128)(2,1)S(1)}, bf16[100,3900]{1,0:T(8,128)(2,1)}, u32[]{:S(2)}) copy-start(bf16[100,3900]{1,0:T(8,128)(2,1)} %get-tuple-element.208) | copy-start | bytes 2340004 | tf_op jit(solution)/shard_map/while
  188.5 3.1 copy-start.11
  196.1 4.4 %copy-start.2 = (bf16[100,3900]{1,0:T(8,128)(2,1)S(1)}, bf16[100,3900]{1,0:T(8,128)(2,1)}, u32[]{:S(2)}) copy-start(bf16[100,3900]{1,0:T(8,128)(2,1)} %get-tuple-element.208) | copy-start | bytes 2340004 | tf_op jit(solution)/shard_map/while
  209.2 3.1 copy-start.11
  230.0 1.2 copy-start.8
  (19 other events, 13.4 us)
Sparse Core Ops, SparseCore 0:
  231.3 139.8 all-reduce.4
where the time goes:
time: 383 us; the launch traced here: 380 us
  blocking collectives  123 us (32%)
  local copies, waits for them, and re-layouts  63.4 us (17%)
  matrix products  62.2 us (16%)
  other arithmetic  52.6 us (14%)
  waiting for transfers between devices  34 us (9%)
  loops' own time  15.5 us (4%)
  starting transfers between devices  15.3 us (4%)
  between operations  14.3 us (4%)
    psum x1, blocking collectives, local(): hot_grad = lax.psum(hot_local, ('group', 'shard')).astype(jnp.bfloat16)  112 us
    dot_general x24, matrix products, sample_pass(): jnp.einsum('hk,bhe->bke', weight, grad_low, preferred_element_type=jnp.fl...  33 us
    dot_general x24, matrix products, sample_pass(): jnp.einsum('hk,bke->bhe', weight, outer_rows, preferred_element_type=jnp....  29.2 us
    psum x1, waiting for transfers between devices, local(): cold_total = lax.psum(cold_local.astype(jnp.bfloat16), 'group')  26.5 us
    reshape x24, local copies, waits for them, and re-layouts, sample_pass(): grad_outer = grad_outer.reshape(batch_rows, below_maps, fields, breadth)  25.9 us
    another operation x1, loops' own time, local(): logits, gradients = lax.map(one_sample, (embedded, grad_logit))  15.5 us
    reduce_sum x24, other arithmetic, sample_pass(): jnp.sum(grad_outer * lower_state.astype(jnp.float32)[:, :, None, :], axis=1)  15.3 us
    all_to_all x1, blocking collectives, local(): lax.all_to_all(outgoing.astype(jnp.bfloat16), 'shard', split_axis=0, conc...  11.5 us
  transfers between devices with their start and end apart: 3, of which 3 were waited for; matrix products, arithmetic and copies ran while one was open for 2% of the time, Pallas kernels for 0%

commit v1 on v0

v1 whole, which is shorter than its diff:
```python
import functools

import jax
import jax.numpy as jnp
from jax import lax
from jax.experimental import pallas as pl
from jax.experimental.pallas import tpu as pltpu
from jax.sharding import PartitionSpec as P

CAP = 9
SLOT = 16
FP = 40
VMEM = pl.BlockSpec(memory_space=pltpu.VMEM)
SMEM = pl.BlockSpec(memory_space=pltpu.SMEM)
F32 = jnp.float32
BF16 = jnp.bfloat16
I32 = jnp.int32


def iota(shape, dim):
    return lax.broadcasted_iota(I32, shape, dim)


def route_kernel(owners, hot_ref, row_ref, owner_ref, cold_ref, ask_ref, slot_ref, want_ref, pad_ref):
    samples, fields = hot_ref.shape
    total = samples * FP
    code = jnp.where(cold_ref[...] == 1, owner_ref[...], -1)
    pad_ref[...] = jnp.full(pad_ref.shape, -1.0, F32)
    pad_ref[0:samples, 0:fields] = code.astype(F32)
    pad_ref[samples : 2 * samples, 0:fields] = row_ref[...].astype(F32)
    pad_ref[2 * samples : 3 * samples, 0:fields] = jnp.where(
        cold_ref[...] == 1, -1, hot_ref[...]
    ).astype(F32)
    turned = pad_ref[...].T
    lane = iota((FP, 128), 1).astype(F32)
    for s in range(samples):
        want_ref[s * FP : (s + 1) * FP, :] = jnp.where(
            turned[0:FP, s : s + 1] == lane, 1.0, 0.0
        )
    wanted = want_ref[...]
    below = (iota((total, total), 0) > iota((total, total), 1)).astype(F32).astype(BF16)
    earlier = jnp.dot(below, wanted.astype(BF16), preferred_element_type=F32)
    position = jnp.sum(earlier * wanted, axis=1, keepdims=True)
    lane_all = iota((total, 128), 1).astype(F32)
    owner_col = jnp.sum(wanted * lane_all, axis=1, keepdims=True)
    is_cold = jnp.sum(wanted, axis=1, keepdims=True)
    slot = jnp.where(is_cold > 0.0, owner_col * SLOT + position, -1.0)
    slot_ref[...] = jnp.broadcast_to(slot, (total, 128)).astype(I32)
    row_col = jnp.concatenate(
        [turned[0:FP, samples + s : samples + s + 1] for s in range(samples)], axis=0
    ).astype(I32)
    at = jnp.broadcast_to(position, (total, 128)) == lane_all
    high = jnp.where(at, (row_col >> 6).astype(F32), 0.0).astype(BF16)
    low = jnp.where(at, (row_col & 63).astype(F32), 0.0).astype(BF16)
    there = jnp.where(at, 1.0, 0.0).astype(BF16)
    turned_want = wanted.T[0:owners, :].astype(BF16)
    asked = jnp.dot(
        turned_want, jnp.concatenate([high, low, there], axis=1), preferred_element_type=F32
    )
    row = asked[:, 0:128] * 64.0 + asked[:, 128:256]
    ask_ref[...] = jnp.where(asked[:, 256:384] > 0.0, row, 0.0).astype(I32)


def cin_kernel(
    gl_ref,
    hot_ref,
    cold_ref,
    slot_ref,
    back_ref,
    table_ref,
    out_weight_ref,
    f1_ref,
    f2_ref,
    f3_ref,
    b1_ref,
    b2_ref,
    b3_ref,
    logit_ref,
    outgoing_ref,
    pad_ref,
    pick_ref,
    emb_ref,
    embb_ref,
    x2_ref,
    x3_ref,
    x4_ref,
    outer_ref,
    carry_ref,
    part_ref,
    pool_ref,
    grad_ref,
):
    samples, fields = hot_ref.shape
    total = samples * FP
    breadth = table_ref.shape[1]
    lanes = samples * breadth
    hot_rows = table_ref.shape[0]
    slots = back_ref.shape[0]
    pad_ref[...] = jnp.full(pad_ref.shape, -1.0, F32)
    pad_ref[0:samples, 0:fields] = jnp.where(cold_ref[...] == 1, -1, hot_ref[...]).astype(F32)
    turned = pad_ref[...].T.astype(I32)
    slot = slot_ref[...]

    for s in range(samples):
        ids = turned[0:FP, s : s + 1]
        pick_ref[s * FP : (s + 1) * FP, 0:hot_rows] = (
            jnp.where(ids == iota((FP, hot_rows), 1), 1.0, 0.0).astype(BF16)
        )
    pick_ref[:, hot_rows : hot_rows + slots] = (
        jnp.where(
            jnp.concatenate([slot] * (slots // 128), axis=1) == iota((total, slots), 1), 1.0, 0.0
        ).astype(BF16)
    )
    rows = jnp.dot(pick_ref[:, 0:hot_rows], table_ref[...], preferred_element_type=F32) + jnp.dot(
        pick_ref[:, hot_rows : hot_rows + slots], back_ref[...], preferred_element_type=F32
    )
    emb_ref[...] = jnp.zeros(emb_ref.shape, F32)
    for s in range(samples):
        emb_ref[0:FP, s * breadth : (s + 1) * breadth] = rows[s * FP : (s + 1) * FP, :]
    embb_ref[...] = emb_ref[...].astype(BF16)

    pool_ref[...] = jnp.zeros(pool_ref.shape, F32)
    states = (embb_ref, x2_ref, x3_ref, x4_ref)
    for k, w_ref in enumerate((f1_ref, f2_ref, f3_ref)):
        source = states[k]
        height = source.shape[0]

        def fill(f, _, source=source, height=height):
            line = jnp.broadcast_to(emb_ref[pl.ds(f, 1), :], (16, lanes)).astype(BF16)
            for r in range(0, height, 16):
                at = pl.multiple_of(f * height + r, 16)
                outer_ref[pl.ds(at, 16), :] = source[r : r + 16, :] * line
            return 0

        lax.fori_loop(0, fields, fill, 0)
        depth = fields * height
        weight = w_ref[...]
        for n in range(0, lanes, 256):
            value = jnp.dot(
                weight, outer_ref[0:depth, n : n + 256], preferred_element_type=F32
            ).astype(BF16)
            states[k + 1][:, n : n + 256] = value
            pool_ref[:, n : n + 256] += value.astype(F32) * out_weight_ref[:, k : k + 1]

    for s in range(samples):
        logit_ref[s] = jnp.sum(pool_ref[:, s * breadth : (s + 1) * breadth])

    part_ref[...] = jnp.zeros(part_ref.shape, F32)
    tall = carry_ref.shape[0]
    grad_ref[...] = jnp.zeros(grad_ref.shape, BF16)
    for k, w_ref in reversed(tuple(enumerate((b1_ref, b2_ref, b3_ref)))):
        source = states[k]
        height = source.shape[0]
        for s in range(samples):
            at = slice(s * breadth, (s + 1) * breadth)
            value = jnp.broadcast_to(gl_ref[s] * out_weight_ref[:, k : k + 1], (tall, breadth))
            if k < 2:
                value = value + carry_ref[:, at]
            grad_ref[0:tall, at] = value.astype(BF16)
        carry_ref[0:height, :] = jnp.zeros((height, lanes), F32)

        def back(f, _, source=source, height=height, w_ref=w_ref):
            at = pl.multiple_of(f * height, 16)
            at8 = pl.multiple_of(f * 8, 8)
            for n in range(0, lanes, 256):
                cols = slice(n, n + 256)
                outer = jnp.dot(
                    w_ref[pl.ds(at, height), :], grad_ref[:, cols], preferred_element_type=F32
                )
                carry_ref[0:height, cols] += outer * emb_ref[pl.ds(f, 1), cols]
                mixed = outer * source[:, cols].astype(F32)
                total_rows = mixed[0:8]
                for r in range(8, height, 8):
                    total_rows = total_rows + mixed[r : r + 8]
                part_ref[pl.ds(at8, 8), cols] += total_rows
            return 0

        lax.fori_loop(0, fields, back, 0)

    grads = carry_ref[0:FP, :] + jnp.sum(part_ref[...].reshape(FP, 8, lanes), axis=1)
    stacked = jnp.concatenate(
        [grads[:, s * breadth : (s + 1) * breadth] for s in range(samples)], axis=0
    ).astype(BF16)
    owners = outgoing_ref.shape[0]
    share = hot_rows // owners
    slot_line = slot.astype(F32).T[0:1].astype(I32)
    hot_col = jnp.concatenate([turned[0:FP, s : s + 1] for s in range(samples)], axis=0)
    hot_wide = jnp.broadcast_to(hot_col, (total, 128)).astype(F32).T[0:1].astype(I32)
    line = jnp.where(jnp.broadcast_to(slot_line, (slots, total)) == iota((slots, total), 0), 1.0, 0.0)
    sent_cold = jnp.dot(line.astype(BF16), stacked, preferred_element_type=F32).astype(BF16)
    line = jnp.where(jnp.broadcast_to(hot_wide, (hot_rows, total)) == iota((hot_rows, total), 0), 1.0, 0.0)
    sent_hot = jnp.dot(line.astype(BF16), stacked, preferred_element_type=F32).astype(BF16)
    outgoing_ref[:, 0:SLOT, :] = sent_cold.reshape(owners, SLOT, breadth)
    outgoing_ref[:, SLOT : SLOT + share, :] = sent_hot.reshape(owners, share, breadth)


def call_route(hot_row, cold_row, cold_owner, is_cold, owners):
    samples, fields = hot_row.shape
    total = samples * FP
    return pl.pallas_call(
        functools.partial(route_kernel, owners),
        out_shape=(
            jax.ShapeDtypeStruct((owners, 128), I32),
            jax.ShapeDtypeStruct((total, 128), I32),
        ),
        in_specs=[VMEM] * 4,
        out_specs=(VMEM, VMEM),
        scratch_shapes=[pltpu.VMEM((total, 128), F32), pltpu.VMEM((128, 128), F32)],
        name="route",
    )(hot_row, cold_row, cold_owner, is_cold)


def forward_form(weight, fields, height):
    rows = weight.shape[0]
    maps = weight.shape[1] // fields
    turned = weight.reshape(rows, maps, fields).transpose(0, 2, 1)
    tall = -(-rows // 16) * 16
    padded = jnp.pad(turned, ((0, tall - rows), (0, 0), (0, height - maps)))
    return padded.reshape(tall, fields * height)


def backward_form(weight, fields, height):
    rows = weight.shape[0]
    maps = weight.shape[1] // fields
    turned = weight.reshape(rows, maps, fields).transpose(2, 1, 0)
    padded = jnp.pad(turned, ((0, 0), (0, height - maps), (0, 128 - rows)))
    return padded.reshape(fields * height, 128)


def call_cin(grad_logit, hot_row, is_cold, slot, back, hot_table, out_weight, forward, backward):
    samples, fields = hot_row.shape
    total = samples * FP
    hot_rows, breadth = hot_table.shape
    lanes = samples * breadth
    maps = out_weight.shape[1]
    tall = -(-maps // 16) * 16
    owners, slots = back.shape[0], back.shape[0] * back.shape[1]
    weights_line = jnp.pad(out_weight.T, ((0, tall - maps), (0, 128 - out_weight.shape[0])))
    return pl.pallas_call(
        cin_kernel,
        out_shape=(
            jax.ShapeDtypeStruct((samples,), F32),
            jax.ShapeDtypeStruct((owners, SLOT + hot_rows // owners, breadth), BF16),
        ),
        in_specs=[SMEM] + [VMEM] * 12,
        out_specs=(SMEM, VMEM),
        scratch_shapes=[
            pltpu.VMEM((128, 128), F32),
            pltpu.VMEM((total, hot_rows + slots), BF16),
            pltpu.VMEM((48, lanes), F32),
            pltpu.VMEM((48, lanes), BF16),
            pltpu.VMEM((tall, lanes), BF16),
            pltpu.VMEM((tall, lanes), BF16),
            pltpu.VMEM((tall, lanes), BF16),
            pltpu.VMEM((fields * tall, lanes), BF16),
            pltpu.VMEM((tall, lanes), F32),
            pltpu.VMEM((FP * 8, lanes), F32),
            pltpu.VMEM((tall, lanes), F32),
            pltpu.VMEM((128, lanes), BF16),
        ],
        compiler_params=pltpu.CompilerParams(vmem_limit_bytes=56 << 20),
        name="cin",
    )(
        grad_logit, hot_row, is_cold, slot, back.reshape(slots, breadth), hot_table,
        weights_line, *forward, *backward,
    )


def local(
    hot_row, cold_row, cold_owner, is_cold, grad_logit, hot_table, cold_table,
    first_weight, second_weight, third_weight, out_weight,
):
    samples, fields = hot_row.shape
    breadth = hot_table.shape[1]
    owners = lax.axis_size("shard")
    weights = (first_weight, second_weight, third_weight)
    heights = (48, 112, 112)
    forward = [forward_form(w, fields, h) for w, h in zip(weights, heights)]
    backward = [backward_form(w, fields, h) for w, h in zip(weights, heights)]
    ask, slot = call_route(hot_row, cold_row, cold_owner, is_cold, owners)
    requested = lax.all_to_all(ask[:, :SLOT], "shard", split_axis=0, concat_axis=0, tiled=True)
    found = jnp.take(cold_table, requested, axis=0)
    returned = lax.all_to_all(found, "shard", split_axis=0, concat_axis=0, tiled=True)
    logits, outgoing = call_cin(
        grad_logit, hot_row, is_cold, slot, returned, hot_table, out_weight, forward, backward
    )
    incoming = lax.all_to_all(outgoing, "shard", split_axis=0, concat_axis=0, tiled=True)
    cold_in = incoming[:, :SLOT].astype(F32)
    cold_local = jax.ops.segment_sum(
        cold_in.reshape(-1, breadth), requested.reshape(-1), num_segments=cold_table.shape[0]
    )
    cold_total = lax.psum(cold_local.astype(BF16), "group")
    hot_part = jnp.sum(incoming[:, SLOT:].astype(F32), axis=0).astype(BF16)
    hot_mine = jnp.sum(lax.all_gather(hot_part, "group").astype(F32), axis=0).astype(BF16)
    hot_grad = lax.all_gather(hot_mine, "shard", axis=0, tiled=True)
    return (hot_grad, cold_total, logits)


def solution(mesh):
    across = P(("group", "shard"), None)
    return jax.shard_map(
        local,
        mesh=mesh,
        in_specs=(
            across, across, across, across, P(("group", "shard")), P(), P("shard", None),
            P(), P(), P(), P(),
        ),
        out_specs=(P(), P("shard", None), P(("group", "shard"))),
        check_vma=False,
    )
```

time: 383 us -> 268 us (0.70)
  the two profiles are of different devices: /device:TPU:6 before, /device:TPU:2 now
where the time goes in v1:
time: 268 us; the launch traced here: 267 us
  waiting for transfers between devices  89.9 us (34%)
  blocking collectives  74.1 us (28%)
  Pallas kernels  38.8 us (14%)
  local copies, waits for them, and re-layouts  30.3 us (11%)
  between operations  14.2 us (5%)
  starting transfers between devices  12.5 us (5%)
  other arithmetic  7.64 us (3%)
    psum x1, waiting for transfers between devices, local(): cold_total = lax.psum(cold_local.astype(BF16), 'group')  79.5 us
    pallas_call x1, Pallas kernels, call_cin(): pl.pallas_call(cin_kernel, out_shape=(jax.ShapeDtypeStruct((samples,), F3...  36.6 us
    all_gather x1, blocking collectives, local(): lax.all_gather(hot_part, 'group').astype(F32)  35.1 us
    all_gather x1, blocking collectives, local(): hot_grad = lax.all_gather(hot_mine, 'shard', axis=0, tiled=True)  23.5 us
    all_to_all x1, blocking collectives, local(): lax.all_to_all(ask[:, :SLOT], 'shard', split_axis=0, concat_axis=0, tiled...  15.6 us
    unnamed x24, local copies, waits for them, and re-layouts  12.8 us
    all_to_all x1, waiting for transfers between devices, local(): lax.all_to_all(outgoing, 'shard', split_axis=0, concat_axis=0, tiled=True)  10.4 us
    all_to_all x1, starting transfers between devices, local(): lax.all_to_all(outgoing, 'shard', split_axis=0, concat_axis=0, tiled=True)  7.5 us
  transfers between devices with their start and end apart: 3, of which 2 were waited for; matrix products, arithmetic and copies ran while one was open for 10% of the time, Pallas kernels for 0%

profile of v1, /device:TPU:2, one launch (start us, length us, event | category | flops | bytes accessed | tf_op | source)
XLA Modules:
  0.0 267.5 jit_solution(16303452807024239100)
XLA Ops:
  7.2 2.2 route.1
  9.4 15.6 %all_to_all.25 = s32[32,1,16]{2,1,0:T(1,128)S(1)} all-to-all(s32[32,1,16]{2,1,0:T(1,128)} %bitcast.47), channel_id=1, replica_groups=mesh['group'=16,'shard'=32] {'shard'}, dimensions={0} | all-to-all | bytes 4096 | tf_op jit(solution)/shard_map/all_to_all | solution.py:281
  25.1 1.3 gather_fusion
  26.4 0.8 broadcast_select_fusion
  27.2 4.9 %all-to-all-start.1 = ((bf16[32,16,128]{2,1,0:T(8,128)(2,1)}), bf16[32,16,128]{2,1,0:T(8,128)(2,1)S(1)}, u32[]{:S(2)}, u32[]{:S(2)}) async-start(bf16[32,16,128]{2,1,0:T(8,128)(2,1)} %broadcast_select_fusion), calls=%async_computation.1 | async-start | bytes 262144 | tf_op jit(solution)/shard_map/all_to_all | solution.py:283
  32.2 1.1 copy.48
  33.6 2.0 copy.57
  35.6 1.4 pad.28.clone
  37.1 1.8 reshape.86.f2_ref
  38.9 2.3 copy.50
  41.1 1.5 reshape.87
  42.6 2.0 copy.58
  44.7 2.4 pad.29.clone
  47.1 2.9 %reshape.88.f3_ref = bf16[112,4368]{1,0:T(8,128)(2,1)} reshape(bf16[112,39,112]{2,1,0:T(8,128)(2,1)} %pad.29.clone) | data formatting | bytes 1956864 | tf_op jit(solution)/shard_map/reshape | solution.py:219
  50.1 1.2 pad.31.clone
  51.5 1.3 pad.32.clone
  53.3 1.0 copy.55.f1_ref
  54.4 0.9 pad.30.clone
  56.0 0.6 copy-done.3
  56.6 36.6 %cin.1 = (f32[8]{0:T(128)}, bf16[32,80,128]{2,1,0:T(8,128)(2,1)}) custom-call(f32[8]{0:T(128)} %gl_ref.1, s32[8,39]{1,0:T(8,128)} %hot_ref.3, s32[8,39]{1,0:T(8,128)} %cold_ref.3, s32[320,128]{1,0:T(8,128)} %get-tuple-element.7.slot_ref, bf16[512,128]{1,0:T(8,128)(2,1)} %bitcast.41, bf16[2048,128]{1,0:T(8,128)(2,1)} %table_ref.1, ...), custom_call_target="tpu_custom_call" | custom-call | tf_op jit(solution)/shard_map/cin/pallas_call | solution.py:239
  93.2 7.5 %all-to-all-start.2 = ((bf16[32,80,128]{2,1,0:T(8,128)(2,1)}), bf16[32,80,128]{2,1,0:T(8,128)(2,1)S(1)}, u32[]{:S(2)}, u32[]{:S(2)}) async-start(bf16[32,80,128]{2,1,0:T(8,128)(2,1)} %get-tuple-element.9), calls=%async_computation.2 | async-start | bytes 1310720 | tf_op jit(solution)/shard_map/all_to_all | solution.py:287
  101.3 0.7 reduce.5
  102.1 10.4 %all-to-all-done.2 = bf16[32,80,128]{2,1,0:T(8,128)(2,1)S(1)} async-done(((bf16[32,80,128]{2,1,0:T(8,128)(2,1)}), bf16[32,80,128]{2,1,0:T(8,128)(2,1)S(1)}, u32[]{:S(2)}, u32[]{:S(2)}) %all-to-all-start.2) | async-done | bytes 655392 | tf_op jit(solution)/shard_map/all_to_all | solution.py:287
  112.5 0.8 copy-done.1
  113.4 3.9 %scatter_custom_fusion = f32[4096,128]{1,0:T(8,128)S(1)} fusion(s32[512]{0:T(512)S(1)} %reshape.106, f32[]{:T(128)} %constant.23.clone.1, bf16[512,128]{1,0:T(8,128)(2,1)S(1)} %bitcast.43), kind=kCustom, calls=%fused_computation.2 | custom fusion | flops 131072 | bytes 2228228 | tf_op jit(solution)/shard_map/scatter-add | solution.py:289
  117.3 1.1 convert_element_type.14
  118.4 1.1 slice_reduce_fusion
  119.5 35.1 %all-gather = bf16[1024,128]{1,0:T(8,128)(2,1)S(1)} all-gather(bf16[64,128]{1,0:T(8,128)(2,1)S(1)} %slice_reduce_fusion), channel_id=2, replica_groups=mesh['group'=16,'shard'=32] {'group'}, dimensions={0}, use_global_device_ids=true | all-gather | bytes 278528 | tf_op jit(solution)/shard_map/all_gather | solution.py:294
  154.6 23.5 %all_gather.11 = bf16[2048,128]{1,0:T(8,128)(2,1)S(1)} all-gather(bf16[64,128]{1,0:T(8,128)(2,1)S(1)} %reduce_sum.25), channel_id=1, replica_groups=mesh['group'=16,'shard'=32] {'shard'}, dimensions={0}, use_global_device_ids=true | all-gather | bytes 540672 | tf_op jit(solution)/shard_map/all_gather | solution.py:295
  178.1 79.5 %all-reduce.9.cloned.1.call-done = bf16[4096,128]{1,0:T(8,128)(2,1)} async-done(((bf16[4096,128]{1,0:T(8,128)(2,1)}), bf16[4096,128]{1,0:T(8,128)(2,1)}) %all-reduce.9.cloned.1.call-update) | async-done | bytes 1048592 | tf_op jit(solution)/shard_map/psum | solution.py:292
  257.6 0.8 copy.64
  258.4 2.3 copy.65
  (31 shorter events, 2.8 us)
Async XLA Ops:
  7.2 17.9 %copy-start = (bf16[4096,128]{1,0:T(8,128)(2,1)S(1)}, bf16[4096,128]{1,0:T(8,128)(2,1)}, u32[]{:S(2)}) copy-start(bf16[4096,128]{1,0:T(8,128)(2,1)} %param.17) | copy-start | bytes 3145732
  7.2 25.0 %copy-start.2 = (bf16[100,3900]{1,0:T(8,128)(2,1)S(1)}, bf16[100,3900]{1,0:T(8,128)(2,1)}, u32[]{:S(2)}) copy-start(bf16[100,3900]{1,0:T(8,128)(2,1)} %param.19) | copy-start | bytes 2340004
  27.2 28.8 %all-to-all-start.1 = ((bf16[32,16,128]{2,1,0:T(8,128)(2,1)}), bf16[32,16,128]{2,1,0:T(8,128)(2,1)S(1)}, u32[]{:S(2)}, u32[]{:S(2)}) async-start(bf16[32,16,128]{2,1,0:T(8,128)(2,1)} %broadcast_select_fusion), calls=%async_computation.1 | async-start | bytes 262144 | tf_op jit(solution)/shard_map/all_to_all | solution.py:283
  51.3 1.4 copy-start.4
  53.2 2.1 copy-start.5
  56.0 0.6 copy-start.3
  93.2 19.3 %all-to-all-start.2 = ((bf16[32,80,128]{2,1,0:T(8,128)(2,1)}), bf16[32,80,128]{2,1,0:T(8,128)(2,1)S(1)}, u32[]{:S(2)}, u32[]{:S(2)}) async-start(bf16[32,80,128]{2,1,0:T(8,128)(2,1)} %get-tuple-element.9), calls=%async_computation.2 | async-start | bytes 1310720 | tf_op jit(solution)/shard_map/all_to_all | solution.py:287
  100.7 156.8 %all-reduce.9.cloned.1.call-start = ((), (), s32[]{:S(2)}) async-start(), calls=%async_computation.3 | async-start | bytes 2097152 | tf_op jit(solution)/shard_map/psum | solution.py:292
  112.5 0.9 copy-start.1
Sparse Core Ops, SparseCore 0:
  118.5 139.0 all-reduce.8

commit v2 on v1

--- a/solution.py
+++ b/solution.py
@@ -266,6 +266,137 @@
     )
 
 
+def merge_kernel(in_ref, ask_ref, out_ref, wide_ref):
+    owners = in_ref.shape[0]
+    share = in_ref.shape[1] - SLOT
+    rows = owners * CAP
+    for o in range(owners):
+        wide_ref[o * CAP : (o + 1) * CAP, :] = in_ref[o, 0:CAP, :].astype(F32)
+    out_ref[0:rows, :] = wide_ref[...].astype(BF16)
+    width = 384
+    slot = iota((128, width), 1)
+    place = (slot * 7282) >> 16
+    rest = slot - place * CAP
+    spread = jnp.where(rest == iota((128, width), 0), 1.0, 0.0).astype(BF16)
+    keep = place[0:owners] == iota((owners, width), 0)
+    ask = jnp.concatenate([ask_ref[...] >> 6, ask_ref[...] & 63], axis=0).astype(F32).astype(BF16)
+    wide = jnp.dot(ask, spread, preferred_element_type=F32)
+    high = jnp.sum(jnp.where(keep, wide[0:owners], 0.0), axis=0, keepdims=True)
+    low = jnp.sum(jnp.where(keep, wide[owners:], 0.0), axis=0, keepdims=True)
+    lines = [v[:, n : n + 128] for v in (high, low) for n in range(0, width, 128)]
+    lines.append(jnp.zeros((2, 128), F32))
+    out_ref[rows : rows + 8, :] = jnp.concatenate(lines, axis=0).astype(BF16)
+    sums = in_ref[0, SLOT : SLOT + share, :].astype(F32)
+    for o in range(1, owners):
+        sums = sums + in_ref[o, SLOT : SLOT + share, :].astype(F32)
+    out_ref[rows + 8 : rows + 8 + share, :] = sums.astype(BF16)
+
+
+def hot_kernel(height, *refs):
+    parts, out_ref = refs[:-1], refs[-1]
+    owners, share, breadth = out_ref.shape
+    sums = jnp.zeros((share, breadth), F32)
+    for part in parts:
+        for top in range(0, part.shape[0], height):
+            sums = sums + part[top + height - share : top + height, :].astype(F32)
+    value = sums.astype(BF16)
+    for o in range(owners):
+        out_ref[o] = value
+
+
+def scatter_kernel(height, rows, *refs):
+    parts, out_ref, stack_ref, line_ref, pick_ref = refs[:-4], *refs[-4:]
+    width = 384
+    count = 0
+    stack_ref[...] = jnp.zeros(stack_ref.shape, BF16)
+    for part in parts:
+        for top in range(0, part.shape[0], height):
+            stack_ref[count * width : count * width + rows, :] = part[top : top + rows, :]
+            ids = part[top + rows : top + rows + 8, :].astype(F32).astype(I32)
+            for n in range(3):
+                at = slice(count * width + n * 128, count * width + (n + 1) * 128)
+                line_ref[:, at] = jnp.broadcast_to(ids[n : n + 1] * 64 + ids[n + 3 : n + 4], (8, 128))
+            count += 1
+    depth = count * width
+    block = pick_ref.shape[0]
+
+    def step(b, _):
+        base = b * block
+        for n in range(0, depth, 128):
+            line = jnp.broadcast_to(line_ref[0:1, n : n + 128], (block, 128))
+            pick_ref[:, n : n + 128] = jnp.where(
+                line == base + iota((block, 128), 0), 1.0, 0.0
+            ).astype(BF16)
+        out_ref[pl.ds(pl.multiple_of(base, block), block), :] = jnp.dot(
+            pick_ref[...], stack_ref[...], preferred_element_type=F32
+        ).astype(BF16)
+        return 0
+
+    lax.fori_loop(0, out_ref.shape[0] // block, step, 0)
+
+
+def call_merge(incoming, requested):
+    owners, tall, breadth = incoming.shape
+    height = owners * CAP + 8 + tall - SLOT
+    return pl.pallas_call(
+        merge_kernel,
+        out_shape=jax.ShapeDtypeStruct((height, breadth), BF16),
+        in_specs=[VMEM, VMEM],
+        out_specs=VMEM,
+        scratch_shapes=[pltpu.VMEM((owners * CAP, breadth), F32)],
+        name="merge",
+    )(incoming, requested)
+
+
+def call_hot(parts, height, owners, share):
+    breadth = parts[0].shape[1]
+    return pl.pallas_call(
+        functools.partial(hot_kernel, height),
+        out_shape=jax.ShapeDtypeStruct((owners, share, breadth), BF16),
+        in_specs=[VMEM] * len(parts),
+        out_specs=VMEM,
+        name="hot_sum",
+    )(*parts)
+
+
+def call_scatter(parts, height, rows, table_rows):
+    breadth = parts[0].shape[1]
+    count = sum(part.shape[0] for part in parts) // height
+    block = 256
+    return pl.pallas_call(
+        functools.partial(scatter_kernel, height, rows),
+        out_shape=jax.ShapeDtypeStruct((table_rows, breadth), BF16),
+        in_specs=[VMEM] * len(parts),
+        out_specs=VMEM,
+        scratch_shapes=[
+            pltpu.VMEM((count * 384, breadth), BF16),
+            pltpu.VMEM((8, count * 384), I32),
+            pltpu.VMEM((block, count * 384), BF16),
+        ],
+        name="cold_scatter",
+    )(*parts)
+
+
+def exchange(block):
+    groups = lax.axis_size("group")
+    half = groups // 2
+
+    def move(x, hop):
+        return lax.ppermute(x, "group", [(i, (i + hop) % groups) for i in range(groups)])
+
+    pair = jnp.concatenate([block, move(block, half)], axis=0)
+    parts = [pair]
+    up = down = pair
+    for hop in range(1, half):
+        if hop % 2 == 1:
+            up = move(up, 1)
+            parts.append(up)
+        else:
+            down = move(down, -1)
+            parts.append(down)
+    return parts
+
+
 def local(
     hot_row, cold_row, cold_owner, is_cold, grad_logit, hot_table, cold_table,
     first_weight, second_weight, third_weight, out_weight,
@@ -278,21 +409,24 @@
     forward = [forward_form(w, fields, h) for w, h in zip(weights, heights)]
     backward = [backward_form(w, fields, h) for w, h in zip(weights, heights)]
     ask, slot = call_route(hot_row, cold_row, cold_owner, is_cold, owners)
-    requested = lax.all_to_all(ask[:, :SLOT], "shard", split_axis=0, concat_axis=0, tiled=True)
+    ask_in = lax.all_to_all(ask, "shard", split_axis=0, concat_axis=0, tiled=True)
+    requested = ask_in[:, :SLOT]
     found = jnp.take(cold_table, requested, axis=0)
     returned = lax.all_to_all(found, "shard", split_axis=0, concat_axis=0, tiled=True)
     logits, outgoing = call_cin(
         grad_logit, hot_row, is_cold, slot, returned, hot_table, out_weight, forward, backward
     )
     incoming = lax.all_to_all(outgoing, "shard", split_axis=0, concat_axis=0, tiled=True)
-    cold_in = incoming[:, :SLOT].astype(F32)
-    cold_local = jax.ops.segment_sum(
-        cold_in.reshape(-1, breadth), requested.reshape(-1), num_segments=cold_table.shape[0]
-    )
-    cold_total = lax.psum(cold_local.astype(BF16), "group")
-    hot_part = jnp.sum(incoming[:, SLOT:].astype(F32), axis=0).astype(BF16)
-    hot_mine = jnp.sum(lax.all_gather(hot_part, "group").astype(F32), axis=0).astype(BF16)
-    hot_grad = lax.all_gather(hot_mine, "shard", axis=0, tiled=True)
+    block = call_merge(incoming, ask_in)
+    rows = owners * CAP
+    share = hot_table.shape[0] // owners
+    height = block.shape[0]
+    parts = exchange(block)
+    hot_out = lax.all_to_all(
+        call_hot(parts, height, owners, share), "shard", split_axis=0, concat_axis=0, tiled=True
+    )
+    cold_total = call_scatter(parts, height, rows, cold_table.shape[0])
+    hot_grad = hot_out.reshape(hot_table.shape)
     return (hot_grad, cold_total, logits)
 
 

time: 268 us -> 206 us (0.77)
  the two profiles are of different devices: /device:TPU:2 before, /device:TPU:1 now
where the time goes in v2:
time: 206 us; the launch traced here: 205 us
  Pallas kernels  68.8 us (33%)
  starting transfers between devices  55 us (27%)
  blocking collectives  37.8 us (18%)
  local copies, waits for them, and re-layouts  27.3 us (13%)
  waiting for transfers between devices  13.3 us (6%)
    ppermute x8, starting transfers between devices, move(): lax.ppermute(x, 'group', [(i, (i + hop) % groups) for i in range(groups)])  41.6 us
    pallas_call x1, Pallas kernels, call_cin(): pl.pallas_call(cin_kernel, out_shape=(jax.ShapeDtypeStruct((samples,), F3...  36.5 us
    pallas_call x1, Pallas kernels, call_scatter(): pl.pallas_call(functools.partial(scatter_kernel, height, rows), out_shape...  25.9 us
    all_to_all x1, blocking collectives, local(): lax.all_to_all(outgoing, 'shard', split_axis=0, concat_axis=0, tiled=True)  20.5 us
    all_to_all x1, blocking collectives, local(): lax.all_to_all(ask, 'shard', split_axis=0, concat_axis=0, tiled=True)  17.3 us
    ppermute x8, waiting for transfers between devices, move(): lax.ppermute(x, 'group', [(i, (i + hop) % groups) for i in range(groups)])  13.3 us
    unnamed x39, local copies, waits for them, and re-layouts  10.4 us
    all_to_all x1, starting transfers between devices, local(): lax.all_to_all(call_hot(parts, height, owners, share), 'shard', split_axi...  9.2 us
  transfers between devices with their start and end apart: 10, of which 5 were waited for; matrix products, arithmetic and copies ran while one was open for 12% of the time, Pallas kernels for 13%

profile of v2, /device:TPU:1, one launch (start us, length us, event | category | flops | bytes accessed | tf_op | source)
XLA Modules:
  0.0 204.9 jit_solution(3649053808735733044)
XLA Ops:
  0.7 2.2 %route.1 = (s32[32,128]{1,0:T(8,128)}, s32[320,128]{1,0:T(8,128)}) custom-call(s32[8,39]{1,0:T(8,128)} %hot_ref.3, s32[8,39]{1,0:T(8,128)} %row_ref.1, s32[8,39]{1,0:T(8,128)} %owner_ref.1, s32[8,39]{1,0:T(8,128)} %cold_ref.3), custom_call_target="tpu_custom_call" | custom-call | tf_op jit(solution)/shard_map/route/pallas_call | solution.py:200
  2.9 17.3 %all_to_all.26 = s32[32,1,128]{2,1,0:T(1,128)S(1)} all-to-all(s32[32,1,128]{2,1,0:T(1,128)} %bitcast.41), channel_id=1, replica_groups=mesh['group'=16,'shard'=32] {'shard'}, dimensions={0} | all-to-all | bytes 32768 | tf_op jit(solution)/shard_map/all_to_all | solution.py:412
  20.3 1.3 gather_fusion
  22.4 4.1 %all-to-all-start.1 = ((bf16[32,16,128]{2,1,0:T(8,128)(2,1)}), bf16[32,16,128]{2,1,0:T(8,128)(2,1)S(1)}, u32[]{:S(2)}, u32[]{:S(2)}) async-start(bf16[32,16,128]{2,1,0:T(8,128)(2,1)} %broadcast_select_fusion), calls=%async_computation.1 | async-start | bytes 262144 | tf_op jit(solution)/shard_map/all_to_all | solution.py:415
  28.0 2.0 copy.45
  30.1 1.4 pad.28.clone
  31.5 1.8 reshape.53.f2_ref
  33.3 2.3 %copy.38 = bf16[100,3900]{0,1:T(8,128)(2,1)} copy(bf16[100,3900]{1,0:T(8,128)(2,1)} %param.20) | data formatting | bytes 1560000 | tf_op args[9]
  35.6 1.5 reshape.54
  37.1 2.0 copy.46
  39.1 2.5 %pad.29.clone = bf16[112,39,112]{2,1,0:T(8,128)(2,1)} pad(bf16[100,39,100]{2,1,0:T(8,128)(2,1)} %copy.46, bf16[]{:T(256)} %constant.20.clone.1), padding=0_12x0_0x0_12 | pad | bytes 1758434 | tf_op jit(solution)/shard_map/jit(_pad)/pad | solution.py:218
  41.6 2.9 %reshape.55.f3_ref = bf16[112,4368]{1,0:T(8,128)(2,1)} reshape(bf16[112,39,112]{2,1,0:T(8,128)(2,1)} %pad.29.clone) | data formatting | bytes 1956864 | tf_op jit(solution)/shard_map/reshape | solution.py:219
  44.6 1.2 pad.31.clone
  46.0 1.2 pad.32.clone
  51.1 36.5 %cin.1 = (f32[8]{0:T(128)}, bf16[32,80,128]{2,1,0:T(8,128)(2,1)}) custom-call(f32[8]{0:T(128)} %gl_ref.1, s32[8,39]{1,0:T(8,128)} %hot_ref.3, s32[8,39]{1,0:T(8,128)} %cold_ref.3, s32[320,128]{1,0:T(8,128)} %get-tuple-element.7.slot_ref, bf16[512,128]{1,0:T(8,128)(2,1)} %bitcast.35, bf16[2048,128]{1,0:T(8,128)(2,1)} %table_ref.1, ...), custom_call_target="tpu_custom_call" | custom-call | tf_op jit(solution)/shard_map/cin/pallas_call | solution.py:239
  87.7 20.5 %all_to_all.27.in_ref = bf16[32,80,128]{2,1,0:T(8,128)(2,1)} all-to-all(bf16[32,80,128]{2,1,0:T(8,128)(2,1)} %get-tuple-element.9), channel_id=1, replica_groups=mesh['group'=16,'shard'=32] {'shard'}, dimensions={0} | all-to-all | bytes 1310720 | tf_op jit(solution)/shard_map/all_to_all | solution.py:419
  108.1 1.9 merge.1
  110.0 13.6 %collective-permute-start = (bf16[360,128]{1,0:T(8,128)(2,1)}, bf16[360,128]{1,0:T(8,128)(2,1)S(1)}, u32[]{:S(2)}, u32[]{:S(2)}) collective-permute-start(bf16[360,128]{1,0:T(8,128)(2,1)} %merge.1), channel_id=1, source_target_pairs={{0,256},{32,288},{64,320},{96,352},{128,384},{160,416},{192,448},{... | collective-permute-start | bytes 276488 | tf_op jit(solution)/shard_map/ppermute | solution.py:385
  123.6 2.8 %collective-permute-done = bf16[360,128]{1,0:T(8,128)(2,1)S(1)} collective-permute-done((bf16[360,128]{1,0:T(8,128)(2,1)}, bf16[360,128]{1,0:T(8,128)(2,1)S(1)}, u32[]{:S(2)}, u32[]{:S(2)}) %collective-permute-start) | collective-permute-done | bytes 92192 | tf_op jit(solution)/shard_map/ppermute | solution.py:385
  127.3 4.6 %collective-permute-start.1 = (bf16[720,128]{1,0:T(8,128)(2,1)S(1)}, bf16[720,128]{1,0:T(8,128)(2,1)S(1)}, u32[]{:S(2)}, u32[]{:S(2)}) collective-permute-start(bf16[720,128]{1,0:T(8,128)(2,1)S(1)} %pad_maximum_fusion.refs_0_), channel_id=1, source_target_pairs={{0,32},{32,64},{64,96},{96,128},{128,160},{160,192},{192,224},{224... | collective-permute-start | bytes 552968 | tf_op jit(solution)/shard_map/ppermute | solution.py:385
  131.9 8.6 %collective-permute-start.2 = (bf16[720,128]{1,0:T(8,128)(2,1)S(1)}, bf16[720,128]{1,0:T(8,128)(2,1)S(1)}, u32[]{:S(2)}, u32[]{:S(2)}) collective-permute-start(bf16[720,128]{1,0:T(8,128)(2,1)S(1)} %pad_maximum_fusion.refs_0_), channel_id=1, source_target_pairs={{0,480},{32,0},{64,32},{96,64},{128,96},{160,128},{192,160},{224,1... | collective-permute-start | bytes 552968 | tf_op jit(solution)/shard_map/ppermute | solution.py:385
  140.5 2.4 %collective-permute-done.1.refs_1_ = bf16[720,128]{1,0:T(8,128)(2,1)S(1)} collective-permute-done((bf16[720,128]{1,0:T(8,128)(2,1)S(1)}, bf16[720,128]{1,0:T(8,128)(2,1)S(1)}, u32[]{:S(2)}, u32[]{:S(2)}) %collective-permute-start.1) | collective-permute-done | bytes 184352 | tf_op jit(solution)/shard_map/ppermute | solution.py:385
  142.9 1.9 collective-permute-start.3
  144.9 4.6 %collective-permute-start.4 = (bf16[720,128]{1,0:T(8,128)(2,1)S(1)}, bf16[720,128]{1,0:T(8,128)(2,1)S(1)}, u32[]{:S(2)}, u32[]{:S(2)}) collective-permute-start(bf16[720,128]{1,0:T(8,128)(2,1)S(1)} %collective-permute-done.2.refs_2_), channel_id=1, source_target_pairs={{0,480},{32,0},{64,32},{96,64},{128,96},{160,128},{192,160},{224,1... | collective-permute-start | bytes 552968 | tf_op jit(solution)/shard_map/ppermute | solution.py:385
  149.4 1.6 collective-permute-done.3.refs_3_
  151.0 1.9 collective-permute-start.5
  152.9 4.6 %collective-permute-start.6 = (bf16[720,128]{1,0:T(8,128)(2,1)S(1)}, bf16[720,128]{1,0:T(8,128)(2,1)S(1)}, u32[]{:S(2)}, u32[]{:S(2)}) collective-permute-start(bf16[720,128]{1,0:T(8,128)(2,1)S(1)} %collective-permute-done.4.refs_4_), channel_id=1, source_target_pairs={{0,480},{32,0},{64,32},{96,64},{128,96},{160,128},{192,160},{224,1... | collective-permute-start | bytes 552968 | tf_op jit(solution)/shard_map/ppermute | solution.py:385
  158.5 1.9 collective-permute-start.7
  160.4 5.5 %collective-permute-done.7.refs_7_ = bf16[720,128]{1,0:T(8,128)(2,1)S(1)} collective-permute-done((bf16[720,128]{1,0:T(8,128)(2,1)S(1)}, bf16[720,128]{1,0:T(8,128)(2,1)S(1)}, u32[]{:S(2)}, u32[]{:S(2)}) %collective-permute-start.7) | collective-permute-done | bytes 184352 | tf_op jit(solution)/shard_map/ppermute | solution.py:385
  166.7 2.3 %hot_sum.1 = bf16[32,64,128]{2,1,0:T(8,128)(2,1)} custom-call(bf16[720,128]{1,0:T(8,128)(2,1)} %copy-done.1, bf16[720,128]{1,0:T(8,128)(2,1)} %copy-done.3, bf16[720,128]{1,0:T(8,128)(2,1)} %copy-done.4, bf16[720,128]{1,0:T(8,128)(2,1)} %copy-done.5, bf16[720,128]{1,0:T(8,128)(2,1)} %copy-done.6, bf16[720,128]{1,0:T(8,128)(2,1)} %copy-done.7, ...), custom_call_target="tpu_custom_call" | custom-call | tf_op jit(solution)/shard_map/hot_sum/pallas_call | solution.py:353
  169.0 9.2 %all-to-all-start.3 = ((bf16[32,64,128]{2,1,0:T(8,128)(2,1)}), bf16[32,64,128]{2,1,0:T(8,128)(2,1)S(1)}, u32[]{:S(2)}, u32[]{:S(2)}) async-start(bf16[32,64,128]{2,1,0:T(8,128)(2,1)} %hot_sum.1), calls=%async_computation.3 | async-start | bytes 1048576 | tf_op jit(solution)/shard_map/all_to_all | solution.py:425
  178.2 25.9 %cold_scatter.1 = bf16[4096,128]{1,0:T(8,128)(2,1)} custom-call(bf16[720,128]{1,0:T(8,128)(2,1)} %copy-done.1, bf16[720,128]{1,0:T(8,128)(2,1)} %copy-done.3, bf16[720,128]{1,0:T(8,128)(2,1)} %copy-done.4, bf16[720,128]{1,0:T(8,128)(2,1)} %copy-done.5, bf16[720,128]{1,0:T(8,128)(2,1)} %copy-done.6, bf16[720,128]{1,0:T(8,128)(2,1)} %copy-done.7, ...), custom_call_target="tpu_custom_call" | custom-call | tf_op jit(solution)/shard_map/cold_scatter/pallas_call | solution.py:366
  (54 shorter events, 9.9 us)
Async XLA Ops:
  0.6 19.6 %copy-start = (bf16[4096,128]{1,0:T(8,128)(2,1)S(1)}, bf16[4096,128]{1,0:T(8,128)(2,1)}, u32[]{:S(2)}) copy-start(bf16[4096,128]{1,0:T(8,128)(2,1)} %param.17) | copy-start | bytes 3145732
  0.6 25.9 %copy-start.2 = (bf16[100,3900]{1,0:T(8,128)(2,1)S(1)}, bf16[100,3900]{1,0:T(8,128)(2,1)}, u32[]{:S(2)}) copy-start(bf16[100,3900]{1,0:T(8,128)(2,1)} %param.19) | copy-start | bytes 2340004
  20.2 7.5 %copy-start.12 = (s32[32,1,128]{2,1,0:T(1,128)}, s32[32,1,128]{2,1,0:T(1,128)S(1)}, u32[]{:S(2)}) copy-start(s32[32,1,128]{2,1,0:T(1,128)S(1)} %all_to_all.26) | copy-start | bytes 49156
  22.4 28.0 %all-to-all-start.1 = ((bf16[32,16,128]{2,1,0:T(8,128)(2,1)}), bf16[32,16,128]{2,1,0:T(8,128)(2,1)S(1)}, u32[]{:S(2)}, u32[]{:S(2)}) async-start(bf16[32,16,128]{2,1,0:T(8,128)(2,1)} %broadcast_select_fusion), calls=%async_computation.1 | async-start | bytes 262144 | tf_op jit(solution)/shard_map/all_to_all | solution.py:415
  45.9 1.2 copy-start.11
  47.8 1.9 copy-start.13
  50.5 0.6 copy-start.10
  110.0 16.4 %collective-permute-start = (bf16[360,128]{1,0:T(8,128)(2,1)}, bf16[360,128]{1,0:T(8,128)(2,1)S(1)}, u32[]{:S(2)}, u32[]{:S(2)}) collective-permute-start(bf16[360,128]{1,0:T(8,128)(2,1)} %merge.1), channel_id=1, source_target_pairs={{0,256},{32,288},{64,320},{96,352},{128,384},{160,416},{192,448},{... | collective-permute-start | bytes 276488 | tf_op jit(solution)/shard_map/ppermute | solution.py:385
  127.3 38.7 %copy-start.1 = (bf16[720,128]{1,0:T(8,128)(2,1)}, bf16[720,128]{1,0:T(8,128)(2,1)S(1)}, u32[]{:S(2)}) copy-start(bf16[720,128]{1,0:T(8,128)(2,1)S(1)} %pad_maximum_fusion.refs_0_) | copy-start | bytes 552964
  127.3 15.6 %collective-permute-start.1 = (bf16[720,128]{1,0:T(8,128)(2,1)S(1)}, bf16[720,128]{1,0:T(8,128)(2,1)S(1)}, u32[]{:S(2)}, u32[]{:S(2)}) collective-permute-start(bf16[720,128]{1,0:T(8,128)(2,1)S(1)} %pad_maximum_fusion.refs_0_), channel_id=1, source_target_pairs={{0,32},{32,64},{64,96},{96,128},{128,160},{160,192},{192,224},{224... | collective-permute-start | bytes 552968 | tf_op jit(solution)/shard_map/ppermute | solution.py:385
  131.9 12.9 %collective-permute-start.2 = (bf16[720,128]{1,0:T(8,128)(2,1)S(1)}, bf16[720,128]{1,0:T(8,128)(2,1)S(1)}, u32[]{:S(2)}, u32[]{:S(2)}) collective-permute-start(bf16[720,128]{1,0:T(8,128)(2,1)S(1)} %pad_maximum_fusion.refs_0_), channel_id=1, source_target_pairs={{0,480},{32,0},{64,32},{96,64},{128,96},{160,128},{192,160},{224,1... | collective-permute-start | bytes 552968 | tf_op jit(solution)/shard_map/ppermute | solution.py:385
  142.9 23.0 %copy-start.3 = (bf16[720,128]{1,0:T(8,128)(2,1)}, bf16[720,128]{1,0:T(8,128)(2,1)S(1)}, u32[]{:S(2)}) copy-start(bf16[720,128]{1,0:T(8,128)(2,1)S(1)} %collective-permute-done.1.refs_1_) | copy-start | bytes 552964
  142.9 8.1 %collective-permute-start.3 = (bf16[720,128]{1,0:T(8,128)(2,1)S(1)}, bf16[720,128]{1,0:T(8,128)(2,1)S(1)}, u32[]{:S(2)}, u32[]{:S(2)}) collective-permute-start(bf16[720,128]{1,0:T(8,128)(2,1)S(1)} %collective-permute-done.1.refs_1_), channel_id=1, source_target_pairs={{0,32},{32,64},{64,96},{96,128},{128,160},{160,192},{192,224},{224... | collective-permute-start | bytes 552968 | tf_op jit(solution)/shard_map/ppermute | solution.py:385
  144.8 21.1 %copy-start.4 = (bf16[720,128]{1,0:T(8,128)(2,1)}, bf16[720,128]{1,0:T(8,128)(2,1)S(1)}, u32[]{:S(2)}) copy-start(bf16[720,128]{1,0:T(8,128)(2,1)S(1)} %collective-permute-done.2.refs_2_) | copy-start | bytes 552964
  144.9 8.1 %collective-permute-start.4 = (bf16[720,128]{1,0:T(8,128)(2,1)S(1)}, bf16[720,128]{1,0:T(8,128)(2,1)S(1)}, u32[]{:S(2)}, u32[]{:S(2)}) collective-permute-start(bf16[720,128]{1,0:T(8,128)(2,1)S(1)} %collective-permute-done.2.refs_2_), channel_id=1, source_target_pairs={{0,480},{32,0},{64,32},{96,64},{128,96},{160,128},{192,160},{224,1... | collective-permute-start | bytes 552968 | tf_op jit(solution)/shard_map/ppermute | solution.py:385
  151.0 15.0 %copy-start.5 = (bf16[720,128]{1,0:T(8,128)(2,1)}, bf16[720,128]{1,0:T(8,128)(2,1)S(1)}, u32[]{:S(2)}) copy-start(bf16[720,128]{1,0:T(8,128)(2,1)S(1)} %collective-permute-done.3.refs_3_) | copy-start | bytes 552964
  151.0 7.5 %collective-permute-start.5 = (bf16[720,128]{1,0:T(8,128)(2,1)S(1)}, bf16[720,128]{1,0:T(8,128)(2,1)S(1)}, u32[]{:S(2)}, u32[]{:S(2)}) collective-permute-start(bf16[720,128]{1,0:T(8,128)(2,1)S(1)} %collective-permute-done.3.refs_3_), channel_id=1, source_target_pairs={{0,32},{32,64},{64,96},{96,128},{128,160},{160,192},{192,224},{224... | collective-permute-start | bytes 552968 | tf_op jit(solution)/shard_map/ppermute | solution.py:385
  152.9 13.1 %copy-start.6 = (bf16[720,128]{1,0:T(8,128)(2,1)}, bf16[720,128]{1,0:T(8,128)(2,1)S(1)}, u32[]{:S(2)}) copy-start(bf16[720,128]{1,0:T(8,128)(2,1)S(1)} %collective-permute-done.4.refs_4_) | copy-start | bytes 552964
  152.9 7.5 %collective-permute-start.6 = (bf16[720,128]{1,0:T(8,128)(2,1)S(1)}, bf16[720,128]{1,0:T(8,128)(2,1)S(1)}, u32[]{:S(2)}, u32[]{:S(2)}) collective-permute-start(bf16[720,128]{1,0:T(8,128)(2,1)S(1)} %collective-permute-done.4.refs_4_), channel_id=1, source_target_pairs={{0,480},{32,0},{64,32},{96,64},{128,96},{160,128},{192,160},{224,1... | collective-permute-start | bytes 552968 | tf_op jit(solution)/shard_map/ppermute | solution.py:385
  158.5 7.5 %copy-start.7 = (bf16[720,128]{1,0:T(8,128)(2,1)}, bf16[720,128]{1,0:T(8,128)(2,1)S(1)}, u32[]{:S(2)}) copy-start(bf16[720,128]{1,0:T(8,128)(2,1)S(1)} %collective-permute-done.5.refs_5_) | copy-start | bytes 552964
  158.5 7.5 %collective-permute-start.7 = (bf16[720,128]{1,0:T(8,128)(2,1)S(1)}, bf16[720,128]{1,0:T(8,128)(2,1)S(1)}, u32[]{:S(2)}, u32[]{:S(2)}) collective-permute-start(bf16[720,128]{1,0:T(8,128)(2,1)S(1)} %collective-permute-done.5.refs_5_), channel_id=1, source_target_pairs={{0,32},{32,64},{64,96},{96,128},{128,160},{160,192},{192,224},{224... | collective-permute-start | bytes 552968 | tf_op jit(solution)/shard_map/ppermute | solution.py:385
  160.4 5.6 %copy-start.8 = (bf16[720,128]{1,0:T(8,128)(2,1)}, bf16[720,128]{1,0:T(8,128)(2,1)S(1)}, u32[]{:S(2)}) copy-start(bf16[720,128]{1,0:T(8,128)(2,1)S(1)} %collective-permute-done.6.refs_6_) | copy-start | bytes 552964
  166.0 0.7 copy-start.9
  169.0 35.1 %all-to-all-start.3 = ((bf16[32,64,128]{2,1,0:T(8,128)(2,1)}), bf16[32,64,128]{2,1,0:T(8,128)(2,1)S(1)}, u32[]{:S(2)}, u32[]{:S(2)}) async-start(bf16[32,64,128]{2,1,0:T(8,128)(2,1)} %hot_sum.1), calls=%async_computation.3 | async-start | bytes 1048576 | tf_op jit(solution)/shard_map/all_to_all | solution.py:425

commit v3 on v2

--- a/solution.py
+++ b/solution.py
@@ -10,7 +10,9 @@
 CAP = 9
 SLOT = 16
 FP = 40
+GROUP = 3
 VMEM = pl.BlockSpec(memory_space=pltpu.VMEM)
+HBM = pl.BlockSpec(memory_space=pltpu.HBM)
 SMEM = pl.BlockSpec(memory_space=pltpu.SMEM)
 F32 = jnp.float32
 BF16 = jnp.bfloat16
@@ -67,14 +69,14 @@
     cold_ref,
     slot_ref,
     back_ref,
-    table_ref,
     out_weight_ref,
-    f1_ref,
-    f2_ref,
-    f3_ref,
-    b1_ref,
-    b2_ref,
-    b3_ref,
+    table_hbm,
+    f1_hbm,
+    f2_hbm,
+    f3_hbm,
+    b1_hbm,
+    b2_hbm,
+    b3_hbm,
     logit_ref,
     outgoing_ref,
     pad_ref,
@@ -83,13 +85,30 @@
     embb_ref,
     x2_ref,
     x3_ref,
-    x4_ref,
+    w2_ref,
+    w3_ref,
     outer_ref,
     carry_ref,
     part_ref,
     pool_ref,
     grad_ref,
+    table_ref,
+    f1_ref,
+    f2_ref,
+    f3_ref,
+    b1_ref,
+    b2_ref,
+    b3_ref,
+    sems,
 ):
+    held = (table_ref, f1_ref, f2_ref, f3_ref, b3_ref, b2_ref, b1_ref)
+    kept = (table_hbm, f1_hbm, f2_hbm, f3_hbm, b3_hbm, b2_hbm, b1_hbm)
+    copies = [
+        pltpu.make_async_copy(source, target, sems.at[n])
+        for n, (source, target) in enumerate(zip(kept, held))
+    ]
+    for copy in copies:
+        copy.start()
     samples, fields = hot_ref.shape
     total = samples * FP
     breadth = table_ref.shape[1]
@@ -111,6 +130,7 @@
             jnp.concatenate([slot] * (slots // 128), axis=1) == iota((total, slots), 1), 1.0, 0.0
         ).astype(BF16)
     )
+    copies[0].wait()
     rows = jnp.dot(pick_ref[:, 0:hot_rows], table_ref[...], preferred_element_type=F32) + jnp.dot(
         pick_ref[:, hot_rows : hot_rows + slots], back_ref[...], preferred_element_type=F32
     )
@@ -120,7 +140,8 @@
     embb_ref[...] = emb_ref[...].astype(BF16)
 
     pool_ref[...] = jnp.zeros(pool_ref.shape, F32)
-    states = (embb_ref, x2_ref, x3_ref, x4_ref)
+    states = (embb_ref, x2_ref, x3_ref)
+    wides = (emb_ref, w2_ref, w3_ref)
     for k, w_ref in enumerate((f1_ref, f2_ref, f3_ref)):
         source = states[k]
         height = source.shape[0]
@@ -134,13 +155,17 @@
 
         lax.fori_loop(0, fields, fill, 0)
         depth = fields * height
+        copies[1 + k].wait()
         weight = w_ref[...]
         for n in range(0, lanes, 256):
             value = jnp.dot(
                 weight, outer_ref[0:depth, n : n + 256], preferred_element_type=F32
             ).astype(BF16)
-            states[k + 1][:, n : n + 256] = value
-            pool_ref[:, n : n + 256] += value.astype(F32) * out_weight_ref[:, k : k + 1]
+            wide = value.astype(F32)
+            if k < 2:
+                states[k + 1][:, n : n + 256] = value
+                wides[k + 1][:, n : n + 256] = wide
+            pool_ref[:, n : n + 256] += wide * out_weight_ref[:, k : k + 1]
 
     for s in range(samples):
         logit_ref[s] = jnp.sum(pool_ref[:, s * breadth : (s + 1) * breadth])
@@ -149,7 +174,8 @@
     tall = carry_ref.shape[0]
     grad_ref[...] = jnp.zeros(grad_ref.shape, BF16)
     for k, w_ref in reversed(tuple(enumerate((b1_ref, b2_ref, b3_ref)))):
-        source = states[k]
+        copies[6 - k].wait()
+        source = wides[k]
         height = source.shape[0]
         for s in range(samples):
             at = slice(s * breadth, (s + 1) * breadth)
@@ -159,23 +185,35 @@
             grad_ref[0:tall, at] = value.astype(BF16)
         carry_ref[0:height, :] = jnp.zeros((height, lanes), F32)
 
-        def back(f, _, source=source, height=height, w_ref=w_ref):
-            at = pl.multiple_of(f * height, 16)
-            at8 = pl.multiple_of(f * 8, 8)
+        def back(t, _, source=source, height=height, w_ref=w_ref):
+            at = pl.multiple_of(t * (GROUP * height), 16)
+            at8 = pl.multiple_of(t * (GROUP * 8), 8)
             for n in range(0, lanes, 256):
                 cols = slice(n, n + 256)
                 outer = jnp.dot(
-                    w_ref[pl.ds(at, height), :], grad_ref[:, cols], preferred_element_type=F32
+                    w_ref[pl.ds(at, GROUP * height), :],
+                    grad_ref[:, cols],
+                    preferred_element_type=F32,
                 )
-                carry_ref[0:height, cols] += outer * emb_ref[pl.ds(f, 1), cols]
-                mixed = outer * source[:, cols].astype(F32)
-                total_rows = mixed[0:8]
-                for r in range(8, height, 8):
-                    total_rows = total_rows + mixed[r : r + 8]
-                part_ref[pl.ds(at8, 8), cols] += total_rows
+                sums = [None] * GROUP
+                lines = [
+                    jnp.broadcast_to(emb_ref[pl.ds(t * GROUP + u, 1), cols], (8, 256))
+                    for u in range(GROUP)
+                ]
+                for r in range(0, height, 8):
+                    value = source[r : r + 8, cols]
+                    total_rows = carry_ref[r : r + 8, cols]
+                    for u in range(GROUP):
+                        piece = outer[u * height + r : u * height + r + 8]
+                        total_rows = total_rows + piece * lines[u]
+                        mixed = piece * value
+                        sums[u] = mixed if r == 0 else sums[u] + mixed
+                    carry_ref[r : r + 8, cols] = total_rows
+                for u in range(GROUP):
+                    part_ref[pl.ds(at8 + u * 8, 8), cols] += sums[u]
             return 0
 
-        lax.fori_loop(0, fields, back, 0)
+        lax.fori_loop(0, fields // GROUP, back, 0)
 
     grads = carry_ref[0:FP, :] + jnp.sum(part_ref[...].reshape(FP, 8, lanes), axis=1)
     stacked = jnp.concatenate(
@@ -206,25 +244,66 @@
         in_specs=[VMEM] * 4,
         out_specs=(VMEM, VMEM),
         scratch_shapes=[pltpu.VMEM((total, 128), F32), pltpu.VMEM((128, 128), F32)],
+        compiler_params=pltpu.CompilerParams(vmem_limit_bytes=4 << 20),
         name="route",
     )(hot_row, cold_row, cold_owner, is_cold)
 
 
-def forward_form(weight, fields, height):
-    rows = weight.shape[0]
-    maps = weight.shape[1] // fields
-    turned = weight.reshape(rows, maps, fields).transpose(0, 2, 1)
+def prep_kernel(fields, *refs):
+    count = (len(refs) - 3) // 5
+    weights, outs = refs[0:count], refs[count : 3 * count]
+    held, (line_ref, wide_ref, sems) = refs[3 * count : 5 * count], refs[5 * count :]
+    copies = []
+    for k, w_ref in enumerate(weights):
+        f_ref, b_ref = held[2 * k : 2 * k + 2]
+        rows, cols = w_ref.shape
+        pitch = b_ref.shape[0] // fields
+        line_ref[...] = jnp.zeros(line_ref.shape, F32)
+        line_ref[0:rows, 0:cols] = w_ref[...].astype(F32)
+        for c in range(0, fields * pitch, 128):
+            if c < cols:
+                wide_ref[c : c + 128, :] = line_ref[:, c : c + 128].T
+            else:
+                wide_ref[c : c + 128, :] = jnp.zeros((128, 128), F32)
+        for f in range(fields):
+            b_ref[f * pitch : (f + 1) * pitch, :] = wide_ref[
+                pl.ds(f, pitch, stride=fields), :
+            ].astype(BF16)
+        copies.append(pltpu.make_async_copy(b_ref, outs[2 * k + 1], sems.at[2 * k + 1]))
+        copies[-1].start()
+        tall = f_ref.shape[0]
+        for c in range(0, fields * pitch, 128):
+            width = min(128, fields * pitch - c)
+            f_ref[:, c : c + width] = b_ref[c : c + width, :].T[0:tall]
+        copies.append(pltpu.make_async_copy(f_ref, outs[2 * k], sems.at[2 * k]))
+        copies[-1].start()
+    for copy in copies:
+        copy.wait()
+
+
+def call_prep(weights, fields):
+    rows = weights[0].shape[0]
     tall = -(-rows // 16) * 16
-    padded = jnp.pad(turned, ((0, tall - rows), (0, 0), (0, height - maps)))
-    return padded.reshape(tall, fields * height)
-
-
-def backward_form(weight, fields, height):
-    rows = weight.shape[0]
-    maps = weight.shape[1] // fields
-    turned = weight.reshape(rows, maps, fields).transpose(2, 1, 0)
-    padded = jnp.pad(turned, ((0, 0), (0, height - maps), (0, 128 - rows)))
-    return padded.reshape(fields * height, 128)
+    shapes = []
+    for w in weights:
+        pitch = -(-(w.shape[1] // fields) // 16) * 16
+        shapes.append(jax.ShapeDtypeStruct((tall, fields * pitch), BF16))
+        shapes.append(jax.ShapeDtypeStruct((fields * pitch, 128), BF16))
+    deep = max(-(-shape.shape[0] // 128) * 128 for shape in shapes)
+    return pl.pallas_call(
+        functools.partial(prep_kernel, fields),
+        out_shape=tuple(pltpu.HBM(shape.shape, BF16) for shape in shapes),
+        in_specs=[VMEM] * len(weights),
+        out_specs=tuple([HBM] * len(shapes)),
+        scratch_shapes=[pltpu.VMEM(shape.shape, BF16) for shape in shapes]
+        + [
+            pltpu.VMEM((128, deep), F32),
+            pltpu.VMEM((deep, 128), F32),
+            pltpu.SemaphoreType.DMA((len(shapes),)),
+        ],
+        compiler_params=pltpu.CompilerParams(vmem_limit_bytes=14 << 20),
+        name="prep",
+    )(*weights)
 
 
 def call_cin(grad_logit, hot_row, is_cold, slot, back, hot_table, out_weight, forward, backward):
@@ -242,7 +321,7 @@
             jax.ShapeDtypeStruct((samples,), F32),
             jax.ShapeDtypeStruct((owners, SLOT + hot_rows // owners, breadth), BF16),
         ),
-        in_specs=[SMEM] + [VMEM] * 12,
+        in_specs=[SMEM] + [VMEM] * 5 + [HBM] * 7,
         out_specs=(SMEM, VMEM),
         scratch_shapes=[
             pltpu.VMEM((128, 128), F32),
@@ -251,18 +330,22 @@
             pltpu.VMEM((48, lanes), BF16),
             pltpu.VMEM((tall, lanes), BF16),
             pltpu.VMEM((tall, lanes), BF16),
-            pltpu.VMEM((tall, lanes), BF16),
+            pltpu.VMEM((tall, lanes), F32),
+            pltpu.VMEM((tall, lanes), F32),
             pltpu.VMEM((fields * tall, lanes), BF16),
             pltpu.VMEM((tall, lanes), F32),
             pltpu.VMEM((FP * 8, lanes), F32),
             pltpu.VMEM((tall, lanes), F32),
             pltpu.VMEM((128, lanes), BF16),
-        ],
-        compiler_params=pltpu.CompilerParams(vmem_limit_bytes=56 << 20),
+        ]
+        + [pltpu.VMEM(x.shape, BF16) for x in (hot_table, *forward, *backward)]
+        + [pltpu.SemaphoreType.DMA((7,))],
+        compiler_params=pltpu.CompilerParams(vmem_limit_bytes=32 << 20),
         name="cin",
     )(
-        grad_logit, hot_row, is_cold, slot, back.reshape(slots, breadth), hot_table,
-        weights_line, *forward, *backward,
+        grad_logit, hot_row, is_cold, slot, back.reshape(slots, breadth),
+        weights_line,
+        *(pltpu.with_memory_space_constraint(x, pltpu.HBM) for x in (hot_table, *forward, *backward)),
     )
 
 
@@ -275,11 +358,12 @@
     out_ref[0:rows, :] = wide_ref[...].astype(BF16)
     width = 384
     slot = iota((128, width), 1)
+    slot = jnp.where(slot < 256, slot, 256 + (slot & 31))
     place = (slot * 7282) >> 16
     rest = slot - place * CAP
     spread = jnp.where(rest == iota((128, width), 0), 1.0, 0.0).astype(BF16)
     keep = place[0:owners] == iota((owners, width), 0)
-    ask = jnp.concatenate([ask_ref[...] >> 6, ask_ref[...] & 63], axis=0).astype(F32).astype(BF16)
+    ask = jnp.concatenate([ask_ref[...] >> 8, ask_ref[...] & 255], axis=0).astype(F32).astype(BF16)
     wide = jnp.dot(ask, spread, preferred_element_type=F32)
     high = jnp.sum(jnp.where(keep, wide[0:owners], 0.0), axis=0, keepdims=True)
     low = jnp.sum(jnp.where(keep, wide[owners:], 0.0), axis=0, keepdims=True)
@@ -305,34 +389,62 @@
 
 
 def scatter_kernel(height, rows, *refs):
-    parts, out_ref, stack_ref, line_ref, pick_ref = refs[:-4], *refs[-4:]
-    width = 384
-    count = 0
-    stack_ref[...] = jnp.zeros(stack_ref.shape, BF16)
-    for part in parts:
-        for top in range(0, part.shape[0], height):
-            stack_ref[count * width : count * width + rows, :] = part[top : top + rows, :]
-            ids = part[top + rows : top + rows + 8, :].astype(F32).astype(I32)
-            for n in range(3):
-                at = slice(count * width + n * 128, count * width + (n + 1) * 128)
-                line_ref[:, at] = jnp.broadcast_to(ids[n : n + 1] * 64 + ids[n + 3 : n + 4], (8, 128))
-            count += 1
-    depth = count * width
+    parts, out_ref, stack_ref, high_ref, low_ref, pick_ref, wide_ref, rhs_ref = refs[:-7], *refs[-7:]
+    full = rows // 128 * 128
+    tail = rows - full
+    per = 128 // tail
+    sources = [(part, top) for part in parts for top in range(0, part.shape[0], height)]
+    deep = len(sources) * full
+    lane = iota((16, 128), 1)
+    lines = len(sources) // per
+    for n, (part, top) in enumerate(sources):
+        stack_ref[n * full : (n + 1) * full, :] = part[top : top + full, :]
+        at = deep + n * tail
+        stack_ref[at : at + tail, :] = part[top + full : top + rows, :]
+    for half, line_ref in ((0, high_ref), (3, low_ref)):
+        for n, (part, top) in enumerate(sources):
+            ids = part[top + rows : top + rows + 8, :].astype(F32)
+            for c in range(full // 128):
+                at = n * full + c * 128
+                line_ref[:, at : at + 128] = jnp.broadcast_to(
+                    ids[half + c : half + c + 1], (16, 128)
+                ).astype(BF16)
+        for t in range(lines):
+            merged = jnp.zeros((16, 128), F32)
+            for u in range(per):
+                part, top = sources[t * per + u]
+                row = part[top + rows : top + rows + 8, :].astype(F32)[half + 2 : half + 3]
+                merged = jnp.where(lane // tail == u, jnp.broadcast_to(row, (16, 128)), merged)
+            at = deep + t * 128
+            line_ref[:, at : at + 128] = merged.astype(BF16)
+    depth = stack_ref.shape[0]
     block = pick_ref.shape[0]
-
-    def step(b, _):
-        base = b * block
+    one = jnp.ones((16, 128), BF16)
+    zero = jnp.zeros((16, 128), BF16)
+    for r in range(0, block, 16):
+        place = (iota((16, 128), 0) + r).astype(F32).astype(BF16)
         for n in range(0, depth, 128):
-            line = jnp.broadcast_to(line_ref[0:1, n : n + 128], (block, 128))
-            pick_ref[:, n : n + 128] = jnp.where(
-                line == base + iota((block, 128), 0), 1.0, 0.0
-            ).astype(BF16)
-        out_ref[pl.ds(pl.multiple_of(base, block), block), :] = jnp.dot(
-            pick_ref[...], stack_ref[...], preferred_element_type=F32
-        ).astype(BF16)
+            pick_ref[r : r + 16, n : n + 128] = jnp.where(low_ref[:, n : n + 128] == place, one, zero)
+    for n in range(0, depth, 128):
+        wide_ref[n : n + 128, :] = (
+            jnp.broadcast_to(high_ref[0:1, n : n + 128].astype(F32), (128, 128)).T.astype(BF16)
+        )
+
+    def step(t, _):
+        for u in range(2):
+            for v in range(2):
+                mine = jnp.full((16, 128), 4 * t + 2 * u + v, I32).astype(F32).astype(BF16)
+                for n in range(0, depth, 16):
+                    rhs_ref[u, n : n + 16, v * 128 : (v + 1) * 128] = jnp.where(
+                        wide_ref[n : n + 16, :] == mine, stack_ref[n : n + 16, :], zero
+                    )
+            value = jnp.dot(pick_ref[...], rhs_ref[u], preferred_element_type=F32).astype(BF16)
+            for v in range(2):
+                at = pl.multiple_of((4 * t + 2 * u + v) * block, block)
+                out_ref[pl.ds(at, block), :] = value[:, v * 128 : (v + 1) * 128]
         return 0
 
-    lax.fori_loop(0, out_ref.shape[0] // block, step, 0)
+    lax.fori_loop(0, out_ref.shape[0] // block // 4, step, 0)
 
 
 def call_merge(incoming, requested):
@@ -344,6 +456,7 @@
         in_specs=[VMEM, VMEM],
         out_specs=VMEM,
         scratch_shapes=[pltpu.VMEM((owners * CAP, breadth), F32)],
+        compiler_params=pltpu.CompilerParams(vmem_limit_bytes=4 << 20),
         name="merge",
     )(incoming, requested)
 
@@ -355,6 +468,7 @@
         out_shape=jax.ShapeDtypeStruct((owners, share, breadth), BF16),
         in_specs=[VMEM] * len(parts),
         out_specs=VMEM,
+        compiler_params=pltpu.CompilerParams(vmem_limit_bytes=4 << 20),
         name="hot_sum",
     )(*parts)
 
@@ -369,10 +483,14 @@
         in_specs=[VMEM] * len(parts),
         out_specs=VMEM,
         scratch_shapes=[
-            pltpu.VMEM((count * 384, breadth), BF16),
-            pltpu.VMEM((8, count * 384), I32),
-            pltpu.VMEM((block, count * 384), BF16),
+            pltpu.VMEM((count * rows, breadth), BF16),
+            pltpu.VMEM((16, count * rows), BF16),
+            pltpu.VMEM((16, count * rows), BF16),
+            pltpu.VMEM((block, count * rows), BF16),
+            pltpu.VMEM((count * rows, breadth), BF16),
+            pltpu.VMEM((2, count * rows, 2 * breadth), BF16),
         ],
+        compiler_params=pltpu.CompilerParams(vmem_limit_bytes=16 << 20),
         name="cold_scatter",
     )(*parts)
 
@@ -404,17 +522,14 @@
     samples, fields = hot_row.shape
     breadth = hot_table.shape[1]
     owners = lax.axis_size("shard")
-    weights = (first_weight, second_weight, third_weight)
-    heights = (48, 112, 112)
-    forward = [forward_form(w, fields, h) for w, h in zip(weights, heights)]
-    backward = [backward_form(w, fields, h) for w, h in zip(weights, heights)]
+    forms = call_prep((first_weight, second_weight, third_weight), fields)
     ask, slot = call_route(hot_row, cold_row, cold_owner, is_cold, owners)
     ask_in = lax.all_to_all(ask, "shard", split_axis=0, concat_axis=0, tiled=True)
     requested = ask_in[:, :SLOT]
     found = jnp.take(cold_table, requested, axis=0)
     returned = lax.all_to_all(found, "shard", split_axis=0, concat_axis=0, tiled=True)
     logits, outgoing = call_cin(
-        grad_logit, hot_row, is_cold, slot, returned, hot_table, out_weight, forward, backward
+        grad_logit, hot_row, is_cold, slot, returned, hot_table, out_weight, forms[0::2], forms[1::2]
     )
     incoming = lax.all_to_all(outgoing, "shard", split_axis=0, concat_axis=0, tiled=True)
     block = call_merge(incoming, ask_in)

time: 206 us -> 153 us (0.74)
  Pallas kernels: 68.8 us -> 35.8 us
  local copies, waits for them, and re-layouts: 27.3 us -> 6 us
  waiting for transfers between devices: 13.3 us -> 20.2 us
  blocking collectives: 37.8 us -> 33 us
    pallas_call x1, Pallas kernels: 25.9 us -> 7.83 us  [call_scatter(): pl.pallas_call(functools.partial(scatter_kernel, height, rows), out_shape...]
    pallas_call x1, Pallas kernels: 36.5 us -> 23.1 us  [call_cin(): pl.pallas_call(cin_kernel, out_shape=(jax.ShapeDtypeStruct((samples,), F3...]
    reshape x6 -> x0, local copies, waits for them, and re-layouts: 7.61 us -> none  [the longest x3 5.62 us: forward_form(): return padded.reshape(tall, fields * height)]
    pad x6 -> x0, local copies, waits for them, and re-layouts: 7.32 us -> none  [the longest x3 4 us: forward_form(): padded = jnp.pad(turned, ((0, tall - rows), (0, 0), (0, height - maps)))]
    unnamed x39 -> x24, local copies, waits for them, and re-layouts: 10.4 us -> 4.57 us
    all_to_all x1, blocking collectives: 20.5 us -> 16.5 us  [local(): lax.all_to_all(outgoing, 'shard', split_axis=0, concat_axis=0, tiled=True)]
    all_to_all x1, waiting for transfers between devices: 0.01 us -> 3.72 us  [local(): lax.all_to_all(found, 'shard', split_axis=0, concat_axis=0, tiled=True)]
    all_to_all x1, waiting for transfers between devices: 0.01 us -> 3.6 us  [local(): lax.all_to_all(call_hot(parts, height, owners, share), 'shard', split_axi...]
  transfers between devices with their start and end apart: 10 -> 10, of which waited for: 5 -> 7; matrix products, arithmetic and copies ran while one was open for 12% -> 1% of each run, Pallas kernels for 13% -> 7%
where the time goes in v3:
time: 153 us
  starting transfers between devices  55.8 us (36%)
  Pallas kernels  35.8 us (23%)
  blocking collectives  33 us (22%)
  waiting for transfers between devices  20.2 us (13%)
  local copies, waits for them, and re-layouts  6 us (4%)
    ppermute x8, starting transfers between devices, move(): lax.ppermute(x, 'group', [(i, (i + hop) % groups) for i in range(groups)])  42.5 us
    pallas_call x1, Pallas kernels, call_cin(): pl.pallas_call(cin_kernel, out_shape=(jax.ShapeDtypeStruct((samples,), F3...  23.1 us
    all_to_all x1, blocking collectives, local(): lax.all_to_all(ask, 'shard', split_axis=0, concat_axis=0, tiled=True)  16.5 us
    all_to_all x1, blocking collectives, local(): lax.all_to_all(outgoing, 'shard', split_axis=0, concat_axis=0, tiled=True)  16.5 us
    ppermute x8, waiting for transfers between devices, move(): lax.ppermute(x, 'group', [(i, (i + hop) % groups) for i in range(groups)])  12.9 us
    all_to_all x1, starting transfers between devices, local(): lax.all_to_all(call_hot(parts, height, owners, share), 'shard', split_axi...  9.21 us
    pallas_call x1, Pallas kernels, call_scatter(): pl.pallas_call(functools.partial(scatter_kernel, height, rows), out_shape...  7.83 us
    unnamed x24, local copies, waits for them, and re-layouts  4.57 us
  transfers between devices with their start and end apart: 10, of which 7 were waited for; matrix products, arithmetic and copies ran while one was open for 1% of the time, Pallas kernels for 7%

profile of v3, /device:TPU:1, one launch (start us, length us, event | category | flops | bytes accessed | tf_op | source)
XLA Modules:
  0.0 152.6 jit_solution(9568763877418109994)
XLA Ops:
  0.7 0.8 copy-done.4
  1.5 0.7 copy-done.6
  2.3 0.7 copy-done.8
  2.9 0.7 copy-done.9
  3.6 0.7 route.1
  4.3 16.5 %all_to_all.26 = s32[32,1,128]{2,1,0:T(1,128)S(1)} all-to-all(s32[32,1,128]{2,1,0:T(1,128)S(1)} %bitcast.12), channel_id=1, replica_groups=mesh['group'=16,'shard'=32] {'shard'}, dimensions={0} | all-to-all | bytes 32768 | tf_op jit(solution)/shard_map/all_to_all | solution.py:527
  21.0 1.3 gather_fusion
  22.3 0.8 broadcast_select_fusion
  23.1 4.1 %all-to-all-start.1 = ((bf16[32,16,128]{2,1,0:T(8,128)(2,1)}), bf16[32,16,128]{2,1,0:T(8,128)(2,1)S(1)}, u32[]{:S(2)}, u32[]{:S(2)}) async-start(bf16[32,16,128]{2,1,0:T(8,128)(2,1)} %broadcast_select_fusion), calls=%async_computation.1 | async-start | bytes 262144 | tf_op jit(solution)/shard_map/all_to_all | solution.py:530
  27.3 0.8 copy.17
  28.2 3.1 %prep.1 = (bf16[112,1872]{1,0:T(8,128)(2,1)}, bf16[1872,128]{1,0:T(8,128)(2,1)}, bf16[112,4368]{1,0:T(8,128)(2,1)}, bf16[4368,128]{1,0:T(8,128)(2,1)}, bf16[112,...) custom-call(bf16[100,1521]{1,0:T(8,128)(2,1)S(1)} %copy-done.3, bf16[100,3900]{1,0:T(8,128)(2,1)S(1)} %copy-done.1, ...), custom_call_target="tpu_custom_call" | custom-call | tf_op jit(solution)/shard_map/prep/pallas_call | solution.py:293
  31.3 3.7 %all-to-all-done.1 = bf16[32,16,128]{2,1,0:T(8,128)(2,1)S(1)} async-done(((bf16[32,16,128]{2,1,0:T(8,128)(2,1)}), bf16[32,16,128]{2,1,0:T(8,128)(2,1)S(1)}, u32[]{:S(2)}, u32[]{:S(2)}) %all-to-all-start.1) | async-done | bytes 131104 | tf_op jit(solution)/shard_map/all_to_all | solution.py:530
  35.0 23.1 %cin.1 = (f32[8]{0:T(128)}, bf16[32,80,128]{2,1,0:T(8,128)(2,1)S(1)}) custom-call(f32[8]{0:T(128)S(1)} %copy-done.10, s32[8,39]{1,0:T(8,128)S(1)} %copy-done.5, s32[8,39]{1,0:T(8,128)S(1)} %copy-done.7, s32[320,128]{1,0:T(8,128)S(1)} %get-tuple-element.13.slot_ref, bf16[512,128]{1,0:T(8,128)(2,1)S(1)} %bitcast.8, f32[112,128]{1,0:T(8,128)S(1)} %pad.4.out_weight_ref, ...), custom_call_target="tpu_custom_call" | custom-call | tf_op jit(solution)/shard_map/cin/pallas_call | solution.py:318
  58.2 16.5 %all_to_all.27.in_ref = bf16[32,80,128]{2,1,0:T(8,128)(2,1)S(1)} all-to-all(bf16[32,80,128]{2,1,0:T(8,128)(2,1)S(1)} %get-tuple-element.21), channel_id=1, replica_groups=mesh['group'=16,'shard'=32] {'shard'}, dimensions={0} | all-to-all | bytes 1310720 | tf_op jit(solution)/shard_map/all_to_all | solution.py:534
  74.8 14.2 %collective-permute-start = (bf16[360,128]{1,0:T(8,128)(2,1)S(1)}, bf16[360,128]{1,0:T(8,128)(2,1)S(1)}, u32[]{:S(2)}, u32[]{:S(2)}) collective-permute-start(bf16[360,128]{1,0:T(8,128)(2,1)S(1)} %merge.1), channel_id=1, source_target_pairs={{0,256},{32,288},{64,320},{96,352},{128,384},{160,416},{192,448},{... | collective-permute-start | bytes 276488 | tf_op jit(solution)/shard_map/ppermute | solution.py:503
  89.1 2.5 %collective-permute-done = bf16[360,128]{1,0:T(8,128)(2,1)S(1)} collective-permute-done((bf16[360,128]{1,0:T(8,128)(2,1)S(1)}, bf16[360,128]{1,0:T(8,128)(2,1)S(1)}, u32[]{:S(2)}, u32[]{:S(2)}) %collective-permute-start) | collective-permute-done | bytes 92192 | tf_op jit(solution)/shard_map/ppermute | solution.py:503
  91.6 4.6 %collective-permute-start.1 = (bf16[720,128]{1,0:T(8,128)(2,1)S(1)}, bf16[720,128]{1,0:T(8,128)(2,1)S(1)}, u32[]{:S(2)}, u32[]{:S(2)}) collective-permute-start(bf16[720,128]{1,0:T(8,128)(2,1)S(1)} %pad_maximum_fusion.refs_0_), channel_id=1, source_target_pairs={{0,32},{32,64},{64,96},{96,128},{128,160},{160,192},{192,224},{224... | collective-permute-start | bytes 552968 | tf_op jit(solution)/shard_map/ppermute | solution.py:503
  96.3 8.6 %collective-permute-start.2 = (bf16[720,128]{1,0:T(8,128)(2,1)S(1)}, bf16[720,128]{1,0:T(8,128)(2,1)S(1)}, u32[]{:S(2)}, u32[]{:S(2)}) collective-permute-start(bf16[720,128]{1,0:T(8,128)(2,1)S(1)} %pad_maximum_fusion.refs_0_), channel_id=1, source_target_pairs={{0,480},{32,0},{64,32},{96,64},{128,96},{160,128},{192,160},{224,1... | collective-permute-start | bytes 552968 | tf_op jit(solution)/shard_map/ppermute | solution.py:503
  104.8 2.4 %collective-permute-done.1.refs_1_ = bf16[720,128]{1,0:T(8,128)(2,1)S(1)} collective-permute-done((bf16[720,128]{1,0:T(8,128)(2,1)S(1)}, bf16[720,128]{1,0:T(8,128)(2,1)S(1)}, u32[]{:S(2)}, u32[]{:S(2)}) %collective-permute-start.1) | collective-permute-done | bytes 184352 | tf_op jit(solution)/shard_map/ppermute | solution.py:503
  107.3 1.9 %collective-permute-start.3 = (bf16[720,128]{1,0:T(8,128)(2,1)S(1)}, bf16[720,128]{1,0:T(8,128)(2,1)S(1)}, u32[]{:S(2)}, u32[]{:S(2)}) collective-permute-start(bf16[720,128]{1,0:T(8,128)(2,1)S(1)} %collective-permute-done.1.refs_1_), channel_id=1, source_target_pairs={{0,32},{32,64},{64,96},{96,128},{128,160},{160,192},{192,224},{224... | collective-permute-start | bytes 552968 | tf_op jit(solution)/shard_map/ppermute | solution.py:503
  109.2 4.6 %collective-permute-start.4 = (bf16[720,128]{1,0:T(8,128)(2,1)S(1)}, bf16[720,128]{1,0:T(8,128)(2,1)S(1)}, u32[]{:S(2)}, u32[]{:S(2)}) collective-permute-start(bf16[720,128]{1,0:T(8,128)(2,1)S(1)} %collective-permute-done.2.refs_2_), channel_id=1, source_target_pairs={{0,480},{32,0},{64,32},{96,64},{128,96},{160,128},{192,160},{224,1... | collective-permute-start | bytes 552968 | tf_op jit(solution)/shard_map/ppermute | solution.py:503
  113.8 1.6 %collective-permute-done.3.refs_3_ = bf16[720,128]{1,0:T(8,128)(2,1)S(1)} collective-permute-done((bf16[720,128]{1,0:T(8,128)(2,1)S(1)}, bf16[720,128]{1,0:T(8,128)(2,1)S(1)}, u32[]{:S(2)}, u32[]{:S(2)}) %collective-permute-start.3) | collective-permute-done | bytes 184352 | tf_op jit(solution)/shard_map/ppermute | solution.py:503
  115.3 1.9 %collective-permute-start.5 = (bf16[720,128]{1,0:T(8,128)(2,1)S(1)}, bf16[720,128]{1,0:T(8,128)(2,1)S(1)}, u32[]{:S(2)}, u32[]{:S(2)}) collective-permute-start(bf16[720,128]{1,0:T(8,128)(2,1)S(1)} %collective-permute-done.3.refs_3_), channel_id=1, source_target_pairs={{0,32},{32,64},{64,96},{96,128},{128,160},{160,192},{192,224},{224... | collective-permute-start | bytes 552968 | tf_op jit(solution)/shard_map/ppermute | solution.py:503
  117.3 4.6 %collective-permute-start.6 = (bf16[720,128]{1,0:T(8,128)(2,1)S(1)}, bf16[720,128]{1,0:T(8,128)(2,1)S(1)}, u32[]{:S(2)}, u32[]{:S(2)}) collective-permute-start(bf16[720,128]{1,0:T(8,128)(2,1)S(1)} %collective-permute-done.4.refs_4_), channel_id=1, source_target_pairs={{0,480},{32,0},{64,32},{96,64},{128,96},{160,128},{192,160},{224,1... | collective-permute-start | bytes 552968 | tf_op jit(solution)/shard_map/ppermute | solution.py:503
  121.8 1.0 collective-permute-done.5.refs_5_
  122.8 2.1 %collective-permute-start.7 = (bf16[720,128]{1,0:T(8,128)(2,1)S(1)}, bf16[720,128]{1,0:T(8,128)(2,1)S(1)}, u32[]{:S(2)}, u32[]{:S(2)}) collective-permute-start(bf16[720,128]{1,0:T(8,128)(2,1)S(1)} %collective-permute-done.5.refs_5_), channel_id=1, source_target_pairs={{0,32},{32,64},{64,96},{96,128},{128,160},{160,192},{192,224},{224... | collective-permute-start | bytes 552968 | tf_op jit(solution)/shard_map/ppermute | solution.py:503
  124.9 5.4 %collective-permute-done.7.refs_7_ = bf16[720,128]{1,0:T(8,128)(2,1)S(1)} collective-permute-done((bf16[720,128]{1,0:T(8,128)(2,1)S(1)}, bf16[720,128]{1,0:T(8,128)(2,1)S(1)}, u32[]{:S(2)}, u32[]{:S(2)}) %collective-permute-start.7) | collective-permute-done | bytes 184352 | tf_op jit(solution)/shard_map/ppermute | solution.py:503
  130.3 0.9 hot_sum.1
  131.2 9.2 %all-to-all-start.3 = ((bf16[32,64,128]{2,1,0:T(8,128)(2,1)}), bf16[32,64,128]{2,1,0:T(8,128)(2,1)S(1)}, u32[]{:S(2)}, u32[]{:S(2)}) async-start(bf16[32,64,128]{2,1,0:T(8,128)(2,1)} %hot_sum.1), calls=%async_computation.3 | async-start | bytes 1048576 | tf_op jit(solution)/shard_map/all_to_all | solution.py:540
  140.4 7.8 %cold_scatter.1 = bf16[4096,128]{1,0:T(8,128)(2,1)} custom-call(bf16[720,128]{1,0:T(8,128)(2,1)S(1)} %pad_maximum_fusion.refs_0_, bf16[720,128]{1,0:T(8,128)(2,1)S(1)} %collective-permute-done.1.refs_1_, bf16[720,128]{1,0:T(8,128)(2,1)S(1)} %collective-permute-done.2.refs_2_, bf16[720,128]{1,0:T(8,128)(2,1)S(1)} %collective-permute-done.3.refs_3_, ...), custom_call_target="tpu_custom_call" | custom-call | tf_op jit(solution)/shard_map/cold_scatter/pallas_call | solution.py:480
  148.2 3.6 %all-to-all-done.3 = bf16[32,64,128]{2,1,0:T(8,128)(2,1)S(1)} async-done(((bf16[32,64,128]{2,1,0:T(8,128)(2,1)}), bf16[32,64,128]{2,1,0:T(8,128)(2,1)S(1)}, u32[]{:S(2)}, u32[]{:S(2)}) %all-to-all-start.3) | async-done | bytes 524320 | tf_op jit(solution)/shard_map/all_to_all | solution.py:540
  151.8 0.8 copy.19
  (28 shorter events, 0.3 us)
Async XLA Ops:
  0.6 20.4 %copy-start = (bf16[4096,128]{1,0:T(8,128)(2,1)S(1)}, bf16[4096,128]{1,0:T(8,128)(2,1)}, u32[]{:S(2)}) copy-start(bf16[4096,128]{1,0:T(8,128)(2,1)} %param.17) | copy-start | bytes 3145732
  0.6 27.5 %copy-start.2 = (bf16[100,3900]{1,0:T(8,128)(2,1)S(1)}, bf16[100,3900]{1,0:T(8,128)(2,1)}, u32[]{:S(2)}) copy-start(bf16[100,3900]{1,0:T(8,128)(2,1)} %refs_2_.1) | copy-start | bytes 2340004
  0.7 27.5 %copy-start.1 = (bf16[100,3900]{1,0:T(8,128)(2,1)S(1)}, bf16[100,3900]{1,0:T(8,128)(2,1)}, u32[]{:S(2)}) copy-start(bf16[100,3900]{1,0:T(8,128)(2,1)} %refs_1_.1) | copy-start | bytes 2340004
  0.7 27.5 %copy-start.3 = (bf16[100,1521]{1,0:T(8,128)(2,1)S(1)}, bf16[100,1521]{1,0:T(8,128)(2,1)}, u32[]{:S(2)}) copy-start(bf16[100,1521]{1,0:T(8,128)(2,1)} %refs_0_.1) | copy-start | bytes 912604
  0.7 0.8 copy-start.4
  1.5 0.7 copy-start.6
  2.2 0.7 copy-start.8
  2.9 0.7 copy-start.9
  23.1 11.9 %all-to-all-start.1 = ((bf16[32,16,128]{2,1,0:T(8,128)(2,1)}), bf16[32,16,128]{2,1,0:T(8,128)(2,1)S(1)}, u32[]{:S(2)}, u32[]{:S(2)}) async-start(bf16[32,16,128]{2,1,0:T(8,128)(2,1)} %broadcast_select_fusion), calls=%async_computation.1 | async-start | bytes 262144 | tf_op jit(solution)/shard_map/all_to_all | solution.py:530
  27.3 7.7 %copy-start.5 = (s32[8,39]{1,0:T(8,128)S(1)}, s32[8,39]{1,0:T(8,128)}, u32[]{:S(2)}) copy-start(s32[8,39]{1,0:T(8,128)} %hot_ref.3) | copy-start | bytes 3748
  27.3 7.7 %copy-start.7 = (s32[8,39]{1,0:T(8,128)S(1)}, s32[8,39]{1,0:T(8,128)}, u32[]{:S(2)}) copy-start(s32[8,39]{1,0:T(8,128)} %cold_ref.3) | copy-start | bytes 3748
  27.3 7.7 %copy-start.10 = (f32[8]{0:T(128)S(1)}, f32[8]{0:T(128)}, u32[]{:S(2)}) copy-start(f32[8]{0:T(128)} %gl_ref.1) | copy-start | bytes 100
  74.8 16.8 %collective-permute-start = (bf16[360,128]{1,0:T(8,128)(2,1)S(1)}, bf16[360,128]{1,0:T(8,128)(2,1)S(1)}, u32[]{:S(2)}, u32[]{:S(2)}) collective-permute-start(bf16[360,128]{1,0:T(8,128)(2,1)S(1)} %merge.1), channel_id=1, source_target_pairs={{0,256},{32,288},{64,320},{96,352},{128,384},{160,416},{192,448},{... | collective-permute-start | bytes 276488 | tf_op jit(solution)/shard_map/ppermute | solution.py:503
  91.6 15.6 %collective-permute-start.1 = (bf16[720,128]{1,0:T(8,128)(2,1)S(1)}, bf16[720,128]{1,0:T(8,128)(2,1)S(1)}, u32[]{:S(2)}, u32[]{:S(2)}) collective-permute-start(bf16[720,128]{1,0:T(8,128)(2,1)S(1)} %pad_maximum_fusion.refs_0_), channel_id=1, source_target_pairs={{0,32},{32,64},{64,96},{96,128},{128,160},{160,192},{192,224},{224... | collective-permute-start | bytes 552968 | tf_op jit(solution)/shard_map/ppermute | solution.py:503
  96.3 12.9 %collective-permute-start.2 = (bf16[720,128]{1,0:T(8,128)(2,1)S(1)}, bf16[720,128]{1,0:T(8,128)(2,1)S(1)}, u32[]{:S(2)}, u32[]{:S(2)}) collective-permute-start(bf16[720,128]{1,0:T(8,128)(2,1)S(1)} %pad_maximum_fusion.refs_0_), channel_id=1, source_target_pairs={{0,480},{32,0},{64,32},{96,64},{128,96},{160,128},{192,160},{224,1... | collective-permute-start | bytes 552968 | tf_op jit(solution)/shard_map/ppermute | solution.py:503
  107.3 8.1 %collective-permute-start.3 = (bf16[720,128]{1,0:T(8,128)(2,1)S(1)}, bf16[720,128]{1,0:T(8,128)(2,1)S(1)}, u32[]{:S(2)}, u32[]{:S(2)}) collective-permute-start(bf16[720,128]{1,0:T(8,128)(2,1)S(1)} %collective-permute-done.1.refs_1_), channel_id=1, source_target_pairs={{0,32},{32,64},{64,96},{96,128},{128,160},{160,192},{192,224},{224... | collective-permute-start | bytes 552968 | tf_op jit(solution)/shard_map/ppermute | solution.py:503
  109.2 8.1 %collective-permute-start.4 = (bf16[720,128]{1,0:T(8,128)(2,1)S(1)}, bf16[720,128]{1,0:T(8,128)(2,1)S(1)}, u32[]{:S(2)}, u32[]{:S(2)}) collective-permute-start(bf16[720,128]{1,0:T(8,128)(2,1)S(1)} %collective-permute-done.2.refs_2_), channel_id=1, source_target_pairs={{0,480},{32,0},{64,32},{96,64},{128,96},{160,128},{192,160},{224,1... | collective-permute-start | bytes 552968 | tf_op jit(solution)/shard_map/ppermute | solution.py:503
  115.3 7.5 %collective-permute-start.5 = (bf16[720,128]{1,0:T(8,128)(2,1)S(1)}, bf16[720,128]{1,0:T(8,128)(2,1)S(1)}, u32[]{:S(2)}, u32[]{:S(2)}) collective-permute-start(bf16[720,128]{1,0:T(8,128)(2,1)S(1)} %collective-permute-done.3.refs_3_), channel_id=1, source_target_pairs={{0,32},{32,64},{64,96},{96,128},{128,160},{160,192},{192,224},{224... | collective-permute-start | bytes 552968 | tf_op jit(solution)/shard_map/ppermute | solution.py:503
  117.3 7.7 %collective-permute-start.6 = (bf16[720,128]{1,0:T(8,128)(2,1)S(1)}, bf16[720,128]{1,0:T(8,128)(2,1)S(1)}, u32[]{:S(2)}, u32[]{:S(2)}) collective-permute-start(bf16[720,128]{1,0:T(8,128)(2,1)S(1)} %collective-permute-done.4.refs_4_), channel_id=1, source_target_pairs={{0,480},{32,0},{64,32},{96,64},{128,96},{160,128},{192,160},{224,1... | collective-permute-start | bytes 552968 | tf_op jit(solution)/shard_map/ppermute | solution.py:503
  122.8 7.5 %collective-permute-start.7 = (bf16[720,128]{1,0:T(8,128)(2,1)S(1)}, bf16[720,128]{1,0:T(8,128)(2,1)S(1)}, u32[]{:S(2)}, u32[]{:S(2)}) collective-permute-start(bf16[720,128]{1,0:T(8,128)(2,1)S(1)} %collective-permute-done.5.refs_5_), channel_id=1, source_target_pairs={{0,32},{32,64},{64,96},{96,128},{128,160},{160,192},{192,224},{224... | collective-permute-start | bytes 552968 | tf_op jit(solution)/shard_map/ppermute | solution.py:503
  131.2 20.7 %all-to-all-start.3 = ((bf16[32,64,128]{2,1,0:T(8,128)(2,1)}), bf16[32,64,128]{2,1,0:T(8,128)(2,1)S(1)}, u32[]{:S(2)}, u32[]{:S(2)}) async-start(bf16[32,64,128]{2,1,0:T(8,128)(2,1)} %hot_sum.1), calls=%async_computation.3 | async-start | bytes 1048576 | tf_op jit(solution)/shard_map/all_to_all | solution.py:540

commit v4 on v3

--- a/solution.py
+++ b/solution.py
@@ -23,16 +23,26 @@
     return lax.broadcasted_iota(I32, shape, dim)
 
 
-def route_kernel(owners, hot_ref, row_ref, owner_ref, cold_ref, ask_ref, slot_ref, want_ref, pad_ref):
-    samples, fields = hot_ref.shape
+def route_kernel(
+    owners, row_hbm, owner_hbm, cold_hbm, ask_ref, slot_ref, want_ref, pad_ref,
+    row_ref, owner_ref, cold_ref, sems,
+):
+    copies = [
+        pltpu.make_async_copy(source, target, sems.at[n])
+        for n, (source, target) in enumerate(
+            ((row_hbm, row_ref), (owner_hbm, owner_ref), (cold_hbm, cold_ref))
+        )
+    ]
+    for copy in copies:
+        copy.start()
+    for copy in copies:
+        copy.wait()
+    samples, fields = row_ref.shape
     total = samples * FP
     code = jnp.where(cold_ref[...] == 1, owner_ref[...], -1)
     pad_ref[...] = jnp.full(pad_ref.shape, -1.0, F32)
     pad_ref[0:samples, 0:fields] = code.astype(F32)
     pad_ref[samples : 2 * samples, 0:fields] = row_ref[...].astype(F32)
-    pad_ref[2 * samples : 3 * samples, 0:fields] = jnp.where(
-        cold_ref[...] == 1, -1, hot_ref[...]
-    ).astype(F32)
     turned = pad_ref[...].T
     lane = iota((FP, 128), 1).astype(F32)
     for s in range(samples):
@@ -66,11 +76,10 @@
 def cin_kernel(
     gl_ref,
     hot_ref,
-    cold_ref,
+    hot_line_ref,
     slot_ref,
     back_ref,
-    out_weight_ref,
-    table_hbm,
+    scale_ref,
     f1_hbm,
     f2_hbm,
     f3_hbm,
@@ -79,8 +88,8 @@
     b3_hbm,
     logit_ref,
     outgoing_ref,
-    pad_ref,
     pick_ref,
+    out_weight_ref,
     emb_ref,
     embb_ref,
     x2_ref,
@@ -92,7 +101,6 @@
     part_ref,
     pool_ref,
     grad_ref,
-    table_ref,
     f1_ref,
     f2_ref,
     f3_ref,
@@ -101,38 +109,35 @@
     b3_ref,
     sems,
 ):
-    held = (table_ref, f1_ref, f2_ref, f3_ref, b3_ref, b2_ref, b1_ref)
-    kept = (table_hbm, f1_hbm, f2_hbm, f3_hbm, b3_hbm, b2_hbm, b1_hbm)
+    held = (f1_ref, f2_ref, f3_ref, b3_ref, b2_ref, b1_ref)
+    kept = (f1_hbm, f2_hbm, f3_hbm, b3_hbm, b2_hbm, b1_hbm)
     copies = [
         pltpu.make_async_copy(source, target, sems.at[n])
         for n, (source, target) in enumerate(zip(kept, held))
     ]
     for copy in copies:
         copy.start()
-    samples, fields = hot_ref.shape
-    total = samples * FP
-    breadth = table_ref.shape[1]
+    samples = gl_ref.shape[0]
+    total, breadth = hot_ref.shape
+    fields = b1_ref.shape[0] // embb_ref.shape[0]
     lanes = samples * breadth
-    hot_rows = table_ref.shape[0]
     slots = back_ref.shape[0]
-    pad_ref[...] = jnp.full(pad_ref.shape, -1.0, F32)
-    pad_ref[0:samples, 0:fields] = jnp.where(cold_ref[...] == 1, -1, hot_ref[...]).astype(F32)
-    turned = pad_ref[...].T.astype(I32)
+    owners = outgoing_ref.shape[0]
+    share = outgoing_ref.shape[1] - SLOT
+    hot_rows = owners * share
     slot = slot_ref[...]
-
-    for s in range(samples):
-        ids = turned[0:FP, s : s + 1]
-        pick_ref[s * FP : (s + 1) * FP, 0:hot_rows] = (
-            jnp.where(ids == iota((FP, hot_rows), 1), 1.0, 0.0).astype(BF16)
-        )
-    pick_ref[:, hot_rows : hot_rows + slots] = (
-        jnp.where(
-            jnp.concatenate([slot] * (slots // 128), axis=1) == iota((total, slots), 1), 1.0, 0.0
+    layers, maps = scale_ref.shape
+    tall = carry_ref.shape[0]
+    out_weight_ref[...] = jnp.zeros(out_weight_ref.shape, F32)
+    out_weight_ref[0:layers, 0:maps] = scale_ref[...]
+    out_weight_ref[...] = out_weight_ref[...].T
+
+    for n in range(0, slots, 128):
+        pick_ref[:, n : n + 128] = jnp.where(
+            slot == iota((total, 128), 1) + n, 1.0, 0.0
         ).astype(BF16)
-    )
-    copies[0].wait()
-    rows = jnp.dot(pick_ref[:, 0:hot_rows], table_ref[...], preferred_element_type=F32) + jnp.dot(
-        pick_ref[:, hot_rows : hot_rows + slots], back_ref[...], preferred_element_type=F32
+    rows = hot_ref[...].astype(F32) + jnp.dot(
+        pick_ref[...], back_ref[...], preferred_element_type=F32
     )
     emb_ref[...] = jnp.zeros(emb_ref.shape, F32)
     for s in range(samples):
@@ -155,7 +160,7 @@
 
         lax.fori_loop(0, fields, fill, 0)
         depth = fields * height
-        copies[1 + k].wait()
+        copies[k].wait()
         weight = w_ref[...]
         for n in range(0, lanes, 256):
             value = jnp.dot(
@@ -165,39 +170,36 @@
             if k < 2:
                 states[k + 1][:, n : n + 256] = value
                 wides[k + 1][:, n : n + 256] = wide
-            pool_ref[:, n : n + 256] += wide * out_weight_ref[:, k : k + 1]
+            pool_ref[:, n : n + 256] += wide * out_weight_ref[0:tall, k : k + 1]
 
     for s in range(samples):
         logit_ref[s] = jnp.sum(pool_ref[:, s * breadth : (s + 1) * breadth])
 
     part_ref[...] = jnp.zeros(part_ref.shape, F32)
-    tall = carry_ref.shape[0]
     grad_ref[...] = jnp.zeros(grad_ref.shape, BF16)
     for k, w_ref in reversed(tuple(enumerate((b1_ref, b2_ref, b3_ref)))):
-        copies[6 - k].wait()
+        copies[5 - k].wait()
         source = wides[k]
         height = source.shape[0]
         for s in range(samples):
             at = slice(s * breadth, (s + 1) * breadth)
-            value = jnp.broadcast_to(gl_ref[s] * out_weight_ref[:, k : k + 1], (tall, breadth))
+            value = jnp.broadcast_to(gl_ref[s] * out_weight_ref[0:tall, k : k + 1], (tall, breadth))
             if k < 2:
                 value = value + carry_ref[:, at]
             grad_ref[0:tall, at] = value.astype(BF16)
         carry_ref[0:height, :] = jnp.zeros((height, lanes), F32)
 
-        def back(t, _, source=source, height=height, w_ref=w_ref):
-            at = pl.multiple_of(t * (GROUP * height), 16)
-            at8 = pl.multiple_of(t * (GROUP * 8), 8)
-            for n in range(0, lanes, 256):
-                cols = slice(n, n + 256)
+        def back(n, _, source=source, height=height, w_ref=w_ref):
+            cols = pl.ds(pl.multiple_of(n * 256, 256), 256)
+            for t in range(0, fields, GROUP):
                 outer = jnp.dot(
-                    w_ref[pl.ds(at, GROUP * height), :],
+                    w_ref[t * height : (t + GROUP) * height, :],
                     grad_ref[:, cols],
                     preferred_element_type=F32,
                 )
                 sums = [None] * GROUP
                 lines = [
-                    jnp.broadcast_to(emb_ref[pl.ds(t * GROUP + u, 1), cols], (8, 256))
+                    jnp.broadcast_to(emb_ref[t + u : t + u + 1, cols], (8, 256))
                     for u in range(GROUP)
                 ]
                 for r in range(0, height, 8):
@@ -210,20 +212,17 @@
                         sums[u] = mixed if r == 0 else sums[u] + mixed
                     carry_ref[r : r + 8, cols] = total_rows
                 for u in range(GROUP):
-                    part_ref[pl.ds(at8 + u * 8, 8), cols] += sums[u]
+                    part_ref[(t + u) * 8 : (t + u + 1) * 8, cols] += sums[u]
             return 0
 
-        lax.fori_loop(0, fields // GROUP, back, 0)
+        lax.fori_loop(0, lanes // 256, back, 0)
 
     grads = carry_ref[0:FP, :] + jnp.sum(part_ref[...].reshape(FP, 8, lanes), axis=1)
     stacked = jnp.concatenate(
         [grads[:, s * breadth : (s + 1) * breadth] for s in range(samples)], axis=0
     ).astype(BF16)
-    owners = outgoing_ref.shape[0]
-    share = hot_rows // owners
     slot_line = slot.astype(F32).T[0:1].astype(I32)
-    hot_col = jnp.concatenate([turned[0:FP, s : s + 1] for s in range(samples)], axis=0)
-    hot_wide = jnp.broadcast_to(hot_col, (total, 128)).astype(F32).T[0:1].astype(I32)
+    hot_wide = hot_line_ref[0:1]
     line = jnp.where(jnp.broadcast_to(slot_line, (slots, total)) == iota((slots, total), 0), 1.0, 0.0)
     sent_cold = jnp.dot(line.astype(BF16), stacked, preferred_element_type=F32).astype(BF16)
     line = jnp.where(jnp.broadcast_to(hot_wide, (hot_rows, total)) == iota((hot_rows, total), 0), 1.0, 0.0)
@@ -232,8 +231,8 @@
     outgoing_ref[:, SLOT : SLOT + share, :] = sent_hot.reshape(owners, share, breadth)
 
 
-def call_route(hot_row, cold_row, cold_owner, is_cold, owners):
-    samples, fields = hot_row.shape
+def call_route(cold_row, cold_owner, is_cold, owners):
+    samples, fields = cold_row.shape
     total = samples * FP
     return pl.pallas_call(
         functools.partial(route_kernel, owners),
@@ -241,12 +240,53 @@
             jax.ShapeDtypeStruct((owners, 128), I32),
             jax.ShapeDtypeStruct((total, 128), I32),
         ),
-        in_specs=[VMEM] * 4,
+        in_specs=[HBM] * 3,
         out_specs=(VMEM, VMEM),
-        scratch_shapes=[pltpu.VMEM((total, 128), F32), pltpu.VMEM((128, 128), F32)],
+        scratch_shapes=[pltpu.VMEM((total, 128), F32), pltpu.VMEM((128, 128), F32)]
+        + [pltpu.VMEM((samples, fields), I32)] * 3
+        + [pltpu.SemaphoreType.DMA((3,))],
         compiler_params=pltpu.CompilerParams(vmem_limit_bytes=4 << 20),
         name="route",
-    )(hot_row, cold_row, cold_owner, is_cold)
+    )(*(pltpu.with_memory_space_constraint(x, pltpu.HBM) for x in (cold_row, cold_owner, is_cold)))
+
+
+def hot_rows_kernel(hot_ref, cold_ref, table_ref, rows_ref, line_ref, pad_ref, pick_ref):
+    samples, fields = hot_ref.shape
+    total = samples * FP
+    hot_rows = table_ref.shape[0]
+    pad_ref[...] = jnp.full(pad_ref.shape, -1.0, F32)
+    pad_ref[0:samples, 0:fields] = jnp.where(cold_ref[...] == 1, -1, hot_ref[...]).astype(F32)
+    turned = pad_ref[...].T
+    for s in range(samples):
+        ids = turned[0:FP, s : s + 1].astype(I32)
+        pick_ref[s * FP : (s + 1) * FP, :] = jnp.where(
+            ids == iota((FP, hot_rows), 1), 1.0, 0.0
+        ).astype(BF16)
+    rows_ref[...] = jnp.dot(
+        pick_ref[...], table_ref[...], preferred_element_type=F32
+    ).astype(BF16)
+    hot_col = jnp.concatenate([turned[0:FP, s : s + 1] for s in range(samples)], axis=0)
+    line_ref[...] = jnp.broadcast_to(hot_col, (total, 128)).T[0:8].astype(I32)
+
+
+def call_hot_rows(hot_row, is_cold, hot_table):
+    samples, fields = hot_row.shape
+    total = samples * FP
+    return pl.pallas_call(
+        hot_rows_kernel,
+        out_shape=(
+            jax.ShapeDtypeStruct((total, hot_table.shape[1]), BF16),
+            jax.ShapeDtypeStruct((8, total), I32),
+        ),
+        in_specs=[VMEM] * 3,
+        out_specs=(VMEM, VMEM),
+        scratch_shapes=[
+            pltpu.VMEM((128, 128), F32),
+            pltpu.VMEM((total, hot_table.shape[0]), BF16),
+        ],
+        compiler_params=pltpu.CompilerParams(vmem_limit_bytes=6 << 20),
+        name="hot_rows",
+    )(hot_row, is_cold, hot_table)
 
 
 def prep_kernel(fields, *refs):
@@ -306,28 +346,27 @@
     )(*weights)
 
 
-def call_cin(grad_logit, hot_row, is_cold, slot, back, hot_table, out_weight, forward, backward):
-    samples, fields = hot_row.shape
-    total = samples * FP
-    hot_rows, breadth = hot_table.shape
+def call_cin(grad_logit, hot_values, hot_line, slot, back, hot_rows, out_weight, forward, backward):
+    total, breadth = hot_values.shape
+    samples = grad_logit.shape[0]
     lanes = samples * breadth
-    maps = out_weight.shape[1]
-    tall = -(-maps // 16) * 16
     owners, slots = back.shape[0], back.shape[0] * back.shape[1]
-    weights_line = jnp.pad(out_weight.T, ((0, tall - maps), (0, 128 - out_weight.shape[0])))
+    tall = forward[0].shape[0]
+    small = -(-(FP) // 16) * 16
+    fields = backward[0].shape[0] // small
     return pl.pallas_call(
         cin_kernel,
         out_shape=(
             jax.ShapeDtypeStruct((samples,), F32),
             jax.ShapeDtypeStruct((owners, SLOT + hot_rows // owners, breadth), BF16),
         ),
-        in_specs=[SMEM] + [VMEM] * 5 + [HBM] * 7,
+        in_specs=[SMEM] + [VMEM] * 5 + [HBM] * 6,
         out_specs=(SMEM, VMEM),
         scratch_shapes=[
+            pltpu.VMEM((total, slots), BF16),
             pltpu.VMEM((128, 128), F32),
-            pltpu.VMEM((total, hot_rows + slots), BF16),
-            pltpu.VMEM((48, lanes), F32),
-            pltpu.VMEM((48, lanes), BF16),
+            pltpu.VMEM((small, lanes), F32),
+            pltpu.VMEM((small, lanes), BF16),
             pltpu.VMEM((tall, lanes), BF16),
             pltpu.VMEM((tall, lanes), BF16),
             pltpu.VMEM((tall, lanes), F32),
@@ -338,14 +377,13 @@
             pltpu.VMEM((tall, lanes), F32),
             pltpu.VMEM((128, lanes), BF16),
         ]
-        + [pltpu.VMEM(x.shape, BF16) for x in (hot_table, *forward, *backward)]
-        + [pltpu.SemaphoreType.DMA((7,))],
+        + [pltpu.VMEM(x.shape, BF16) for x in (*forward, *backward)]
+        + [pltpu.SemaphoreType.DMA((6,))],
         compiler_params=pltpu.CompilerParams(vmem_limit_bytes=32 << 20),
         name="cin",
     )(
-        grad_logit, hot_row, is_cold, slot, back.reshape(slots, breadth),
-        weights_line,
-        *(pltpu.with_memory_space_constraint(x, pltpu.HBM) for x in (hot_table, *forward, *backward)),
+        grad_logit, hot_values, hot_line, slot, back.reshape(slots, breadth), out_weight,
+        *(pltpu.with_memory_space_constraint(x, pltpu.HBM) for x in (*forward, *backward)),
     )
 
 
@@ -355,7 +393,10 @@
     rows = owners * CAP
     for o in range(owners):
         wide_ref[o * CAP : (o + 1) * CAP, :] = in_ref[o, 0:CAP, :].astype(F32)
-    out_ref[0:rows, :] = wide_ref[...].astype(BF16)
+    value = wide_ref[...].astype(BF16)
+    copies = out_ref.shape[0]
+    for c in range(copies):
+        out_ref[c, 0:rows, :] = value
     width = 384
     slot = iota((128, width), 1)
     slot = jnp.where(slot < 256, slot, 256 + (slot & 31))
@@ -369,20 +410,34 @@
     low = jnp.sum(jnp.where(keep, wide[owners:], 0.0), axis=0, keepdims=True)
     lines = [v[:, n : n + 128] for v in (high, low) for n in range(0, width, 128)]
     lines.append(jnp.zeros((2, 128), F32))
-    out_ref[rows : rows + 8, :] = jnp.concatenate(lines, axis=0).astype(BF16)
+    value = jnp.concatenate(lines, axis=0).astype(BF16)
+    for c in range(copies):
+        out_ref[c, rows : rows + 8, :] = value
     sums = in_ref[0, SLOT : SLOT + share, :].astype(F32)
     for o in range(1, owners):
         sums = sums + in_ref[o, SLOT : SLOT + share, :].astype(F32)
-    out_ref[rows + 8 : rows + 8 + share, :] = sums.astype(BF16)
-
-
-def hot_kernel(height, *refs):
+    value = sums.astype(BF16)
+    for c in range(copies):
+        out_ref[c, rows + 8 : rows + 8 + share, :] = value
+
+
+def pack_kernel(rows, in_ref, out_ref):
+    count, height = in_ref.shape[0:2]
+    sums = in_ref[0, rows:height, :].astype(F32)
+    out_ref[0:rows, :] = in_ref[0, 0:rows, :]
+    for c in range(1, count):
+        out_ref[c * rows : (c + 1) * rows, :] = in_ref[c, 0:rows, :]
+        sums = sums + in_ref[c, rows:height, :].astype(F32)
+    out_ref[count * rows :, :] = sums.astype(BF16)
+
+
+def hot_kernel(*refs):
     parts, out_ref = refs[:-1], refs[-1]
     owners, share, breadth = out_ref.shape
     sums = jnp.zeros((share, breadth), F32)
     for part in parts:
-        for top in range(0, part.shape[0], height):
-            sums = sums + part[top + height - share : top + height, :].astype(F32)
+        top = part.shape[0] - share
+        sums = sums + part[top : top + share, :].astype(F32)
     value = sums.astype(BF16)
     for o in range(owners):
         out_ref[o] = value
@@ -393,7 +448,11 @@
     full = rows // 128 * 128
     tail = rows - full
     per = 128 // tail
-    sources = [(part, top) for part in parts for top in range(0, part.shape[0], height)]
+    sources = [
+        (part, top)
+        for part in parts
+        for top in range(0, part.shape[0] // height * height, height)
+    ]
     deep = len(sources) * full
     lane = iota((16, 128), 1)
     lines = len(sources) // per
@@ -447,12 +506,12 @@
     lax.fori_loop(0, out_ref.shape[0] // block // 4, step, 0)
 
 
-def call_merge(incoming, requested):
+def call_merge(incoming, requested, copies):
     owners, tall, breadth = incoming.shape
     height = owners * CAP + 8 + tall - SLOT
     return pl.pallas_call(
         merge_kernel,
-        out_shape=jax.ShapeDtypeStruct((height, breadth), BF16),
+        out_shape=jax.ShapeDtypeStruct((copies, height, breadth), BF16),
         in_specs=[VMEM, VMEM],
         out_specs=VMEM,
         scratch_shapes=[pltpu.VMEM((owners * CAP, breadth), F32)],
@@ -461,21 +520,33 @@
     )(incoming, requested)
 
 
-def call_hot(parts, height, owners, share):
+def call_pack(blocks, rows):
+    count, height, breadth = blocks.shape
+    return pl.pallas_call(
+        functools.partial(pack_kernel, rows),
+        out_shape=jax.ShapeDtypeStruct((count * rows + height - rows, breadth), BF16),
+        in_specs=[VMEM],
+        out_specs=VMEM,
+        compiler_params=pltpu.CompilerParams(vmem_limit_bytes=4 << 20),
+        name="pack",
+    )(blocks)
+
+
+def call_hot(parts, owners, share):
     breadth = parts[0].shape[1]
     return pl.pallas_call(
-        functools.partial(hot_kernel, height),
+        hot_kernel,
         out_shape=jax.ShapeDtypeStruct((owners, share, breadth), BF16),
         in_specs=[VMEM] * len(parts),
         out_specs=VMEM,
-        compiler_params=pltpu.CompilerParams(vmem_limit_bytes=4 << 20),
+        compiler_params=pltpu.CompilerParams(vmem_limit_bytes=6 << 20),
         name="hot_sum",
     )(*parts)
 
 
 def call_scatter(parts, height, rows, table_rows):
     breadth = parts[0].shape[1]
-    count = sum(part.shape[0] for part in parts) // height
+    count = sum(part.shape[0] // height for part in parts)
     block = 256
     return pl.pallas_call(
         functools.partial(scatter_kernel, height, rows),
@@ -495,24 +566,24 @@
     )(*parts)
 
 
-def exchange(block):
+def exchange(blocks, rows):
     groups = lax.axis_size("group")
-    half = groups // 2
+    count = blocks.shape[0]
+    apart = groups // count
 
     def move(x, hop):
         return lax.ppermute(x, "group", [(i, (i + hop) % groups) for i in range(groups)])
 
-    pair = jnp.concatenate([block, move(block, half)], axis=0)
-    parts = [pair]
-    up = down = pair
-    for hop in range(1, half):
-        if hop % 2 == 1:
-            up = move(up, 1)
-            parts.append(up)
-        else:
-            down = move(down, -1)
-            parts.append(down)
-    return parts
+    classes = [[a + apart * i for i in range(count)] for a in range(apart)]
+    mine = call_pack(
+        lax.all_to_all(
+            blocks, "group", split_axis=0, concat_axis=0, axis_index_groups=classes, tiled=True
+        ),
+        rows,
+    )
+    up, down = move(mine, 1), move(mine, -1)
+    half = count // 2 * rows
+    return mine, up, down, move(up[:half], 1), move(down[half:], -1)
 
 
 def local(
@@ -523,24 +594,25 @@
     breadth = hot_table.shape[1]
     owners = lax.axis_size("shard")
     forms = call_prep((first_weight, second_weight, third_weight), fields)
-    ask, slot = call_route(hot_row, cold_row, cold_owner, is_cold, owners)
+    ask, slot = call_route(cold_row, cold_owner, is_cold, owners)
+    hot_values, hot_line = call_hot_rows(hot_row, is_cold, hot_table)
     ask_in = lax.all_to_all(ask, "shard", split_axis=0, concat_axis=0, tiled=True)
     requested = ask_in[:, :SLOT]
     found = jnp.take(cold_table, requested, axis=0)
     returned = lax.all_to_all(found, "shard", split_axis=0, concat_axis=0, tiled=True)
     logits, outgoing = call_cin(
-        grad_logit, hot_row, is_cold, slot, returned, hot_table, out_weight, forms[0::2], forms[1::2]
+        grad_logit, hot_values, hot_line, slot, returned, hot_table.shape[0], out_weight,
+        forms[0::2], forms[1::2],
     )
     incoming = lax.all_to_all(outgoing, "shard", split_axis=0, concat_axis=0, tiled=True)
-    block = call_merge(incoming, ask_in)
     rows = owners * CAP
     share = hot_table.shape[0] // owners
-    height = block.shape[0]
-    parts = exchange(block)
+    parts = exchange(call_merge(incoming, ask_in, 4), rows + 8)
     hot_out = lax.all_to_all(
-        call_hot(parts, height, owners, share), "shard", split_axis=0, concat_axis=0, tiled=True
+        call_hot((*parts[0:3], parts[4]), owners, share),
+        "shard", split_axis=0, concat_axis=0, tiled=True,
     )
-    cold_total = call_scatter(parts, height, rows, cold_table.shape[0])
+    cold_total = call_scatter(parts, rows + 8, rows, cold_table.shape[0])
     hot_grad = hot_out.reshape(hot_table.shape)
     return (hot_grad, cold_total, logits)
 

time: 153 us -> 150 us (0.980)
  blocking collectives: 33 us -> 66 us
  starting transfers between devices: 55.8 us -> 29.8 us
  waiting for transfers between devices: 20.2 us -> 15.4 us
  Pallas kernels: 35.8 us -> 31.4 us
    all_to_all x0 -> x1, blocking collectives: none -> 30.9 us  [exchange(): lax.all_to_all(blocks, 'group', split_axis=0, concat_axis=0, axis_index_g...]
    ppermute x8 -> x4, starting transfers between devices: 42.5 us -> 17.7 us  [move(): lax.ppermute(x, 'group', [(i, (i + hop) % groups) for i in range(groups)])]
    pallas_call x1, Pallas kernels: 23.1 us -> 17.2 us  [call_cin(): pl.pallas_call(cin_kernel, out_shape=(jax.ShapeDtypeStruct((samples,), F3...]
    all_to_all x1, waiting for transfers between devices: 3.6 us -> 0.01 us  [local(): lax.all_to_all(call_hot((*parts[0:3], parts[4]), owners, share), 'shard',...]
    all_to_all x1, waiting for transfers between devices: 3.72 us -> 1.64 us  [local(): lax.all_to_all(found, 'shard', split_axis=0, concat_axis=0, tiled=True)]
    all_to_all x1, blocking collectives: 16.5 us -> 18.5 us  [local(): lax.all_to_all(outgoing, 'shard', split_axis=0, concat_axis=0, tiled=True)]
    ppermute x8 -> x4, waiting for transfers between devices: 12.9 us -> 13.8 us  [move(): lax.ppermute(x, 'group', [(i, (i + hop) % groups) for i in range(groups)])]
    unnamed x24 -> x23, local copies, waits for them, and re-layouts: 4.57 us -> 4 us
  transfers between devices with their start and end apart: 10 -> 6, of which waited for: 7 -> 4; matrix products, arithmetic and copies ran while one was open for 1% -> 0% of each run, Pallas kernels for 7% -> 8%
where the time goes in v4:
time: 150 us
  blocking collectives  66 us (44%)
  Pallas kernels  31.4 us (21%)
  starting transfers between devices  29.8 us (20%)
  waiting for transfers between devices  15.4 us (10%)
  local copies, waits for them, and re-layouts  5.44 us (4%)
    all_to_all x1, blocking collectives, exchange(): lax.all_to_all(blocks, 'group', split_axis=0, concat_axis=0, axis_index_g...  30.9 us
    all_to_all x1, blocking collectives, local(): lax.all_to_all(outgoing, 'shard', split_axis=0, concat_axis=0, tiled=True)  18.5 us
    ppermute x4, starting transfers between devices, move(): lax.ppermute(x, 'group', [(i, (i + hop) % groups) for i in range(groups)])  17.7 us
    pallas_call x1, Pallas kernels, call_cin(): pl.pallas_call(cin_kernel, out_shape=(jax.ShapeDtypeStruct((samples,), F3...  17.2 us
    all_to_all x1, blocking collectives, local(): lax.all_to_all(ask, 'shard', split_axis=0, concat_axis=0, tiled=True)  16.5 us
    ppermute x4, waiting for transfers between devices, move(): lax.ppermute(x, 'group', [(i, (i + hop) % groups) for i in range(groups)])  13.8 us
    all_to_all x1, starting transfers between devices, local(): lax.all_to_all(call_hot((*parts[0:3], parts[4]), owners, share), 'shard',...  7.97 us
    pallas_call x1, Pallas kernels, call_scatter(): pl.pallas_call(functools.partial(scatter_kernel, height, rows), out_shape...  7.83 us
  transfers between devices with their start and end apart: 6, of which 4 were waited for; matrix products, arithmetic and copies ran while one was open for 0% of the time, Pallas kernels for 8%

profile of v4, /device:TPU:1, one launch (start us, length us, event | category | flops | bytes accessed | tf_op | source)
XLA Modules:
  0.0 149.6 jit_solution(7303635579203285102)
XLA Ops:
  0.6 0.0 copy-start
  0.7 1.6 %route.1 = (s32[32,128]{1,0:T(8,128)S(1)}, s32[320,128]{1,0:T(8,128)S(1)}) custom-call(s32[8,39]{1,0:T(8,128)} %row_hbm.1, s32[8,39]{1,0:T(8,128)} %owner_hbm.1, s32[8,39]{1,0:T(8,128)} %cold_hbm.1), custom_call_target="tpu_custom_call" | custom-call | tf_op jit(solution)/shard_map/route/pallas_call | solution.py:237
  2.3 16.5 %all_to_all.31 = s32[32,1,128]{2,1,0:T(1,128)S(1)} all-to-all(s32[32,1,128]{2,1,0:T(1,128)S(1)} %bitcast.11), channel_id=1, replica_groups=mesh['group'=16,'shard'=32] {'shard'}, dimensions={0} | all-to-all | bytes 32768 | tf_op jit(solution)/shard_map/all_to_all | solution.py:599
  18.8 0.1 reshape.23
  18.9 0.0 copy-start.1
  18.9 0.0 copy-start.2
  18.9 1.3 gather_fusion
  20.3 0.8 broadcast_select_fusion
  21.1 4.2 %all-to-all-start.1 = ((bf16[32,16,128]{2,1,0:T(8,128)(2,1)}), bf16[32,16,128]{2,1,0:T(8,128)(2,1)S(1)}, u32[]{:S(2)}, u32[]{:S(2)}) async-start(bf16[32,16,128]{2,1,0:T(8,128)(2,1)} %broadcast_select_fusion), calls=%async_computation.1 | async-start | bytes 262144 | tf_op jit(solution)/shard_map/all_to_all | solution.py:602
  25.2 0.0 copy-start.8
  25.3 0.7 copy-done.8
  25.9 0.6 hot_rows.1
  26.6 0.6 copy-done.5
  27.2 1.0 copy-done.4
  28.2 3.1 %prep.1 = (bf16[112,1872]{1,0:T(8,128)(2,1)}, bf16[1872,128]{1,0:T(8,128)(2,1)}, bf16[112,4368]{1,0:T(8,128)(2,1)}, bf16[4368,128]{1,0:T(8,128)(2,1)}, bf16[112,...) custom-call(bf16[100,1521]{1,0:T(8,128)(2,1)S(1)} %copy-done.4, bf16[100,3900]{1,0:T(8,128)(2,1)S(1)} %copy-done.1, ...), custom_call_target="tpu_custom_call" | custom-call | tf_op jit(solution)/shard_map/prep/pallas_call | solution.py:333
  31.3 1.6 %all-to-all-done.1 = bf16[32,16,128]{2,1,0:T(8,128)(2,1)S(1)} async-done(((bf16[32,16,128]{2,1,0:T(8,128)(2,1)}), bf16[32,16,128]{2,1,0:T(8,128)(2,1)S(1)}, u32[]{:S(2)}, u32[]{:S(2)}) %all-to-all-start.1) | async-done | bytes 131104 | tf_op jit(solution)/shard_map/all_to_all | solution.py:602
  32.9 0.9 copy-done.6
  33.8 17.2 %cin.1 = (f32[8]{0:T(128)}, bf16[32,80,128]{2,1,0:T(8,128)(2,1)S(1)}) custom-call(f32[8]{0:T(128)S(1)} %copy-done.10, bf16[320,128]{1,0:T(8,128)(2,1)S(1)} %copy-done.6, s32[8,320]{1,0:T(8,128)S(1)} %get-tuple-element.16.hot_line_ref, s32[320,128]{1,0:T(8,128)S(1)} %get-tuple-element.17.slot_ref, bf16[512,128]{1,0:T(8,128)(2,1)S(1)} %bitcast.7, ...), custom_call_target="tpu_custom_call" | custom-call | tf_op jit(solution)/shard_map/cin/pallas_call | solution.py:357
  51.0 18.5 %all_to_all.32.in_ref = bf16[32,80,128]{2,1,0:T(8,128)(2,1)S(1)} all-to-all(bf16[32,80,128]{2,1,0:T(8,128)(2,1)S(1)} %get-tuple-element.25), channel_id=1, replica_groups=mesh['group'=16,'shard'=32] {'shard'}, dimensions={0} | all-to-all | bytes 1310720 | tf_op jit(solution)/shard_map/all_to_all | solution.py:607
  69.5 0.2 merge.1
  69.7 30.9 %all_to_all.33.in_ref = bf16[4,360,128]{2,1,0:T(8,128)(2,1)S(1)} all-to-all(bf16[4,360,128]{2,1,0:T(8,128)(2,1)S(1)} %merge.1), channel_id=1, replica_groups={{0,128,256,384},{32,160,288,416},{64,192,320,448},{96,224,352,480},{1,1..., dimensions={0} | all-to-all | bytes 737280 | tf_op jit(solution)/shard_map/all_to_all | solution.py:579
  100.6 5.2 %collective-permute-start.1 = (bf16[1248,128]{1,0:T(8,128)(2,1)S(1)}, bf16[1248,128]{1,0:T(8,128)(2,1)S(1)}, u32[]{:S(2)}, u32[]{:S(2)}) collective-permute-start(bf16[1248,128]{1,0:T(8,128)(2,1)S(1)} %pack.1.refs_0_), channel_id=1, source_target_pairs={{0,480},{32,0},{64,32},{96,64},{128,96},{160,128},{192,160},{224,1... | collective-permute-start | bytes 958472 | tf_op jit(solution)/shard_map/ppermute | solution.py:575
  105.8 7.5 %collective-permute-start = (bf16[1248,128]{1,0:T(8,128)(2,1)S(1)}, bf16[1248,128]{1,0:T(8,128)(2,1)S(1)}, u32[]{:S(2)}, u32[]{:S(2)}) collective-permute-start(bf16[1248,128]{1,0:T(8,128)(2,1)S(1)} %pack.1.refs_0_), channel_id=1, source_target_pairs={{0,32},{32,64},{64,96},{96,128},{128,160},{160,192},{192,224},{224... | collective-permute-start | bytes 958472 | tf_op jit(solution)/shard_map/ppermute | solution.py:575
  113.3 4.4 %collective-permute-done.1.refs_2_ = bf16[1248,128]{1,0:T(8,128)(2,1)S(1)} collective-permute-done((bf16[1248,128]{1,0:T(8,128)(2,1)S(1)}, bf16[1248,128]{1,0:T(8,128)(2,1)S(1)}, u32[]{:S(2)}, u32[]{:S(2)}) %collective-permute-start.1) | collective-permute-done | bytes 319520 | tf_op jit(solution)/shard_map/ppermute | solution.py:575
  117.7 1.9 %collective-permute-start.2 = (bf16[656,128]{1,0:T(8,128)(2,1)S(1)}, bf16[656,128]{1,0:T(8,128)(2,1)S(1)}, u32[]{:S(2)}, u32[]{:S(2)}) collective-permute-start(bf16[656,128]{1,0:T(8,128)(2,1)S(1)} %slice.15), channel_id=1, source_target_pairs={{0,480},{32,0},{64,32},{96,64},{128,96},{160,128},{192,160},{224,1... | collective-permute-start | bytes 503816 | tf_op jit(solution)/shard_map/ppermute | solution.py:575
  119.6 4.2 %collective-permute-done.2.refs_3_.refs_4_ = bf16[656,128]{1,0:T(8,128)(2,1)S(1)} collective-permute-done((bf16[656,128]{1,0:T(8,128)(2,1)S(1)}, bf16[656,128]{1,0:T(8,128)(2,1)S(1)}, u32[]{:S(2)}, u32[]{:S(2)}) %collective-permute-start.2) | collective-permute-done | bytes 167968 | tf_op jit(solution)/shard_map/ppermute | solution.py:575
  123.8 0.9 hot_sum.1
  124.6 8.0 %all-to-all-start.4 = ((bf16[32,64,128]{2,1,0:T(8,128)(2,1)}), bf16[32,64,128]{2,1,0:T(8,128)(2,1)S(1)}, u32[]{:S(2)}, u32[]{:S(2)}) async-start(bf16[32,64,128]{2,1,0:T(8,128)(2,1)} %hot_sum.1), calls=%async_computation.4 | async-start | bytes 1048576 | tf_op jit(solution)/shard_map/all_to_all | solution.py:611
  132.6 3.1 %collective-permute-start.3 = (bf16[592,128]{1,0:T(8,128)(2,1)S(1)}, bf16[592,128]{1,0:T(8,128)(2,1)S(1)}, u32[]{:S(2)}, u32[]{:S(2)}) collective-permute-start(bf16[592,128]{1,0:T(8,128)(2,1)S(1)} %slice.16), channel_id=1, source_target_pairs={{0,32},{32,64},{64,96},{96,128},{128,160},{160,192},{192,224},{224... | collective-permute-start | bytes 454664 | tf_op jit(solution)/shard_map/ppermute | solution.py:575
  135.8 5.2 %collective-permute-done.3.refs_3_ = bf16[592,128]{1,0:T(8,128)(2,1)S(1)} collective-permute-done((bf16[592,128]{1,0:T(8,128)(2,1)S(1)}, bf16[592,128]{1,0:T(8,128)(2,1)S(1)}, u32[]{:S(2)}, u32[]{:S(2)}) %collective-permute-start.3) | collective-permute-done | bytes 151584 | tf_op jit(solution)/shard_map/ppermute | solution.py:575
  141.0 7.8 %cold_scatter.1 = bf16[4096,128]{1,0:T(8,128)(2,1)} custom-call(bf16[1248,128]{1,0:T(8,128)(2,1)S(1)} %pack.1.refs_0_, bf16[1248,128]{1,0:T(8,128)(2,1)S(1)} %collective-permute-done.refs_1_, bf16[1248,128]{1,0:T(8,128)(2,1)S(1)} %collective-permute-done.1.refs_2_, bf16[592,128]{1,0:T(8,128)(2,1)S(1)} %collective-permute-done.3.refs_3_, ...), custom_call_target="tpu_custom_call" | custom-call | tf_op jit(solution)/shard_map/cold_scatter/pallas_call | solution.py:551
  148.8 0.8 copy.16
  (22 shorter events, 0.1 us)
Async XLA Ops:
  0.6 18.3 %copy-start = (bf16[4096,128]{1,0:T(8,128)(2,1)S(1)}, bf16[4096,128]{1,0:T(8,128)(2,1)}, u32[]{:S(2)}) copy-start(bf16[4096,128]{1,0:T(8,128)(2,1)} %param.17) | copy-start | bytes 3145732
  0.6 24.6 %copy-start.7 = (s32[8,39]{1,0:T(8,128)S(1)}, s32[8,39]{1,0:T(8,128)}, u32[]{:S(2)}) copy-start(s32[8,39]{1,0:T(8,128)} %cold_hbm.1) | copy-start | bytes 3748
  0.7 24.6 %copy-start.3 = (bf16[2048,128]{1,0:T(8,128)(2,1)S(1)}, bf16[2048,128]{1,0:T(8,128)(2,1)}, u32[]{:S(2)}) copy-start(bf16[2048,128]{1,0:T(8,128)(2,1)} %table_ref.1) | copy-start | bytes 1572868
  18.9 8.3 %copy-start.1 = (bf16[100,3900]{1,0:T(8,128)(2,1)S(1)}, bf16[100,3900]{1,0:T(8,128)(2,1)}, u32[]{:S(2)}) copy-start(bf16[100,3900]{1,0:T(8,128)(2,1)} %refs_1_.1) | copy-start | bytes 2340004
  18.9 8.3 %copy-start.2 = (bf16[100,3900]{1,0:T(8,128)(2,1)S(1)}, bf16[100,3900]{1,0:T(8,128)(2,1)}, u32[]{:S(2)}) copy-start(bf16[100,3900]{1,0:T(8,128)(2,1)} %refs_2_.1) | copy-start | bytes 2340004
  21.1 11.9 %all-to-all-start.1 = ((bf16[32,16,128]{2,1,0:T(8,128)(2,1)}), bf16[32,16,128]{2,1,0:T(8,128)(2,1)S(1)}, u32[]{:S(2)}, u32[]{:S(2)}) async-start(bf16[32,16,128]{2,1,0:T(8,128)(2,1)} %broadcast_select_fusion), calls=%async_computation.1 | async-start | bytes 262144 | tf_op jit(solution)/shard_map/all_to_all | solution.py:602
  25.2 0.7 copy-start.8
  26.6 0.6 copy-start.5
  27.2 1.0 copy-start.4
  28.2 4.8 %copy-start.9 = (f32[3,100]{1,0:T(4,128)S(1)}, f32[3,100]{1,0:T(4,128)}, u32[]{:S(2)}) copy-start(f32[3,100]{1,0:T(4,128)} %scale_ref.1) | copy-start | bytes 3604
  28.2 4.8 %copy-start.10 = (f32[8]{0:T(128)S(1)}, f32[8]{0:T(128)}, u32[]{:S(2)}) copy-start(f32[8]{0:T(128)} %gl_ref.1) | copy-start | bytes 100
  32.9 0.9 copy-start.6
  100.6 17.0 %collective-permute-start.1 = (bf16[1248,128]{1,0:T(8,128)(2,1)S(1)}, bf16[1248,128]{1,0:T(8,128)(2,1)S(1)}, u32[]{:S(2)}, u32[]{:S(2)}) collective-permute-start(bf16[1248,128]{1,0:T(8,128)(2,1)S(1)} %pack.1.refs_0_), channel_id=1, source_target_pairs={{0,480},{32,0},{64,32},{96,64},{128,96},{160,128},{192,160},{224,1... | collective-permute-start | bytes 958472 | tf_op jit(solution)/shard_map/ppermute | solution.py:575
  105.8 13.8 %collective-permute-start = (bf16[1248,128]{1,0:T(8,128)(2,1)S(1)}, bf16[1248,128]{1,0:T(8,128)(2,1)S(1)}, u32[]{:S(2)}, u32[]{:S(2)}) collective-permute-start(bf16[1248,128]{1,0:T(8,128)(2,1)S(1)} %pack.1.refs_0_), channel_id=1, source_target_pairs={{0,32},{32,64},{64,96},{96,128},{128,160},{160,192},{192,224},{224... | collective-permute-start | bytes 958472 | tf_op jit(solution)/shard_map/ppermute | solution.py:575
  117.7 6.1 %collective-permute-start.2 = (bf16[656,128]{1,0:T(8,128)(2,1)S(1)}, bf16[656,128]{1,0:T(8,128)(2,1)S(1)}, u32[]{:S(2)}, u32[]{:S(2)}) collective-permute-start(bf16[656,128]{1,0:T(8,128)(2,1)S(1)} %slice.15), channel_id=1, source_target_pairs={{0,480},{32,0},{64,32},{96,64},{128,96},{160,128},{192,160},{224,1... | collective-permute-start | bytes 503816 | tf_op jit(solution)/shard_map/ppermute | solution.py:575
  124.6 24.2 %all-to-all-start.4 = ((bf16[32,64,128]{2,1,0:T(8,128)(2,1)}), bf16[32,64,128]{2,1,0:T(8,128)(2,1)S(1)}, u32[]{:S(2)}, u32[]{:S(2)}) async-start(bf16[32,64,128]{2,1,0:T(8,128)(2,1)} %hot_sum.1), calls=%async_computation.4 | async-start | bytes 1048576 | tf_op jit(solution)/shard_map/all_to_all | solution.py:611
  132.6 8.4 %collective-permute-start.3 = (bf16[592,128]{1,0:T(8,128)(2,1)S(1)}, bf16[592,128]{1,0:T(8,128)(2,1)S(1)}, u32[]{:S(2)}, u32[]{:S(2)}) collective-permute-start(bf16[592,128]{1,0:T(8,128)(2,1)S(1)} %slice.16), channel_id=1, source_target_pairs={{0,32},{32,64},{64,96},{96,128},{128,160},{160,192},{192,224},{224... | collective-permute-start | bytes 454664 | tf_op jit(solution)/shard_map/ppermute | solution.py:575

commit v5 on v4

--- a/solution.py
+++ b/solution.py
@@ -75,11 +75,11 @@
 
 def cin_kernel(
     gl_ref,
-    hot_ref,
     hot_line_ref,
     slot_ref,
     back_ref,
     scale_ref,
+    hot_hbm,
     f1_hbm,
     f2_hbm,
     f3_hbm,
@@ -107,10 +107,11 @@
     b1_ref,
     b2_ref,
     b3_ref,
+    hot_ref,
     sems,
 ):
-    held = (f1_ref, f2_ref, f3_ref, b3_ref, b2_ref, b1_ref)
-    kept = (f1_hbm, f2_hbm, f3_hbm, b3_hbm, b2_hbm, b1_hbm)
+    held = (hot_ref, f1_ref, f2_ref, f3_ref, b3_ref, b2_ref, b1_ref)
+    kept = (hot_hbm, f1_hbm, f2_hbm, f3_hbm, b3_hbm, b2_hbm, b1_hbm)
     copies = [
         pltpu.make_async_copy(source, target, sems.at[n])
         for n, (source, target) in enumerate(zip(kept, held))
@@ -136,6 +137,7 @@
         pick_ref[:, n : n + 128] = jnp.where(
             slot == iota((total, 128), 1) + n, 1.0, 0.0
         ).astype(BF16)
+    copies[0].wait()
     rows = hot_ref[...].astype(F32) + jnp.dot(
         pick_ref[...], back_ref[...], preferred_element_type=F32
     )
@@ -160,7 +162,7 @@
 
         lax.fori_loop(0, fields, fill, 0)
         depth = fields * height
-        copies[k].wait()
+        copies[1 + k].wait()
         weight = w_ref[...]
         for n in range(0, lanes, 256):
             value = jnp.dot(
@@ -178,7 +180,7 @@
     part_ref[...] = jnp.zeros(part_ref.shape, F32)
     grad_ref[...] = jnp.zeros(grad_ref.shape, BF16)
     for k, w_ref in reversed(tuple(enumerate((b1_ref, b2_ref, b3_ref)))):
-        copies[5 - k].wait()
+        copies[6 - k].wait()
         source = wides[k]
         height = source.shape[0]
         for s in range(samples):
@@ -250,7 +252,9 @@
     )(*(pltpu.with_memory_space_constraint(x, pltpu.HBM) for x in (cold_row, cold_owner, is_cold)))
 
 
-def hot_rows_kernel(hot_ref, cold_ref, table_ref, rows_ref, line_ref, pad_ref, pick_ref):
+def hot_rows_kernel(
+    hot_ref, cold_ref, table_ref, rows_hbm, line_ref, pad_ref, pick_ref, rows_ref, sem
+):
     samples, fields = hot_ref.shape
     total = samples * FP
     hot_rows = table_ref.shape[0]
@@ -265,8 +269,11 @@
     rows_ref[...] = jnp.dot(
         pick_ref[...], table_ref[...], preferred_element_type=F32
     ).astype(BF16)
+    copy = pltpu.make_async_copy(rows_ref, rows_hbm, sem)
+    copy.start()
     hot_col = jnp.concatenate([turned[0:FP, s : s + 1] for s in range(samples)], axis=0)
     line_ref[...] = jnp.broadcast_to(hot_col, (total, 128)).T[0:8].astype(I32)
+    copy.wait()
 
 
 def call_hot_rows(hot_row, is_cold, hot_table):
@@ -275,14 +282,16 @@
     return pl.pallas_call(
         hot_rows_kernel,
         out_shape=(
-            jax.ShapeDtypeStruct((total, hot_table.shape[1]), BF16),
+            pltpu.HBM((total, hot_table.shape[1]), BF16),
             jax.ShapeDtypeStruct((8, total), I32),
         ),
         in_specs=[VMEM] * 3,
-        out_specs=(VMEM, VMEM),
+        out_specs=(HBM, VMEM),
         scratch_shapes=[
             pltpu.VMEM((128, 128), F32),
             pltpu.VMEM((total, hot_table.shape[0]), BF16),
+            pltpu.VMEM((total, hot_table.shape[1]), BF16),
+            pltpu.SemaphoreType.DMA,
         ],
         compiler_params=pltpu.CompilerParams(vmem_limit_bytes=6 << 20),
         name="hot_rows",
@@ -360,7 +369,7 @@
             jax.ShapeDtypeStruct((samples,), F32),
             jax.ShapeDtypeStruct((owners, SLOT + hot_rows // owners, breadth), BF16),
         ),
-        in_specs=[SMEM] + [VMEM] * 5 + [HBM] * 6,
+        in_specs=[SMEM] + [VMEM] * 4 + [HBM] * 7,
         out_specs=(SMEM, VMEM),
         scratch_shapes=[
             pltpu.VMEM((total, slots), BF16),
@@ -377,13 +386,16 @@
             pltpu.VMEM((tall, lanes), F32),
             pltpu.VMEM((128, lanes), BF16),
         ]
-        + [pltpu.VMEM(x.shape, BF16) for x in (*forward, *backward)]
-        + [pltpu.SemaphoreType.DMA((6,))],
+        + [pltpu.VMEM(x.shape, BF16) for x in (*forward, *backward, hot_values)]
+        + [pltpu.SemaphoreType.DMA((7,))],
         compiler_params=pltpu.CompilerParams(vmem_limit_bytes=32 << 20),
         name="cin",
     )(
-        grad_logit, hot_values, hot_line, slot, back.reshape(slots, breadth), out_weight,
-        *(pltpu.with_memory_space_constraint(x, pltpu.HBM) for x in (*forward, *backward)),
+        grad_logit, hot_line, slot, back.reshape(slots, breadth), out_weight,
+        *(
+            pltpu.with_memory_space_constraint(x, pltpu.HBM)
+            for x in (hot_values, *forward, *backward)
+        ),
     )
 
 
@@ -421,38 +433,36 @@
         out_ref[c, rows + 8 : rows + 8 + share, :] = value
 
 
-def pack_kernel(rows, in_ref, out_ref):
-    count, height = in_ref.shape[0:2]
-    sums = in_ref[0, rows:height, :].astype(F32)
-    out_ref[0:rows, :] = in_ref[0, 0:rows, :]
-    for c in range(1, count):
-        out_ref[c * rows : (c + 1) * rows, :] = in_ref[c, 0:rows, :]
-        sums = sums + in_ref[c, rows:height, :].astype(F32)
-    out_ref[count * rows :, :] = sums.astype(BF16)
-
-
-def hot_kernel(*refs):
+def pack_kernel(rows, *refs):
+    blocks, out_ref = refs[:-1], refs[-1]
+    height = blocks[0].shape[0]
+    last = (len(blocks) - 1) * rows
+    sums = jnp.zeros((height - rows, out_ref.shape[1]), F32)
+    for c, block in enumerate(blocks):
+        at = c * rows if c * rows < last else last + height - rows
+        out_ref[at : at + rows, :] = block[0:rows, :]
+        sums = sums + block[rows:height, :].astype(F32)
+    out_ref[last : last + height - rows, :] = sums.astype(BF16)
+
+
+def hot_kernel(tops, *refs):
     parts, out_ref = refs[:-1], refs[-1]
     owners, share, breadth = out_ref.shape
     sums = jnp.zeros((share, breadth), F32)
-    for part in parts:
-        top = part.shape[0] - share
-        sums = sums + part[top : top + share, :].astype(F32)
+    for part, top in zip(parts, tops):
+        if top is not None:
+            sums = sums + part[top : top + share, :].astype(F32)
     value = sums.astype(BF16)
     for o in range(owners):
         out_ref[o] = value
 
 
-def scatter_kernel(height, rows, *refs):
+def scatter_kernel(places, rows, *refs):
     parts, out_ref, stack_ref, high_ref, low_ref, pick_ref, wide_ref, rhs_ref = refs[:-7], *refs[-7:]
     full = rows // 128 * 128
     tail = rows - full
     per = 128 // tail
-    sources = [
-        (part, top)
-        for part in parts
-        for top in range(0, part.shape[0] // height * height, height)
-    ]
+    sources = [(parts[n], top) for n, top in places]
     deep = len(sources) * full
     lane = iota((16, 128), 1)
     lines = len(sources) // per
@@ -521,21 +531,22 @@
 
 
 def call_pack(blocks, rows):
-    count, height, breadth = blocks.shape
+    height, breadth = blocks[0].shape
+    count = len(blocks)
     return pl.pallas_call(
         functools.partial(pack_kernel, rows),
         out_shape=jax.ShapeDtypeStruct((count * rows + height - rows, breadth), BF16),
-        in_specs=[VMEM],
+        in_specs=[VMEM] * count,
         out_specs=VMEM,
         compiler_params=pltpu.CompilerParams(vmem_limit_bytes=4 << 20),
         name="pack",
-    )(blocks)
-
-
-def call_hot(parts, owners, share):
+    )(*blocks)
+
+
+def call_hot(parts, tops, owners, share):
     breadth = parts[0].shape[1]
     return pl.pallas_call(
-        hot_kernel,
+        functools.partial(hot_kernel, tops),
         out_shape=jax.ShapeDtypeStruct((owners, share, breadth), BF16),
         in_specs=[VMEM] * len(parts),
         out_specs=VMEM,
@@ -544,12 +555,12 @@
     )(*parts)
 
 
-def call_scatter(parts, height, rows, table_rows):
+def call_scatter(parts, places, rows, table_rows):
     breadth = parts[0].shape[1]
-    count = sum(part.shape[0] // height for part in parts)
+    count = len(places)
     block = 256
     return pl.pallas_call(
-        functools.partial(scatter_kernel, height, rows),
+        functools.partial(scatter_kernel, places, rows),
         out_shape=jax.ShapeDtypeStruct((table_rows, breadth), BF16),
         in_specs=[VMEM] * len(parts),
         out_specs=VMEM,
@@ -566,24 +577,23 @@
     )(*parts)
 
 
-def exchange(blocks, rows):
+def exchange(block, rows):
     groups = lax.axis_size("group")
-    count = blocks.shape[0]
-    apart = groups // count
+    share = block.shape[0] - rows
 
     def move(x, hop):
         return lax.ppermute(x, "group", [(i, (i + hop) % groups) for i in range(groups)])
 
-    classes = [[a + apart * i for i in range(count)] for a in range(apart)]
-    mine = call_pack(
-        lax.all_to_all(
-            blocks, "group", split_axis=0, concat_axis=0, axis_index_groups=classes, tiled=True
-        ),
-        rows,
-    )
+    apart = groups // 4
+    far = [move(block, apart), move(block, -apart), move(block, 2 * apart)]
+    mine = call_pack([far[0], block, far[1], far[2]], rows)
     up, down = move(mine, 1), move(mine, -1)
-    half = count // 2 * rows
-    return mine, up, down, move(up[:half], 1), move(down[half:], -1)
+    up_half = move(up[: 2 * rows], 1)
+    down_half = move(down[rows : 3 * rows + share], -1)
+    whole = (0, rows, 2 * rows, 3 * rows + share)
+    sources = [(n, top) for n in range(3) for top in whole]
+    sources += [(n, top) for n in (3, 4) for top in (0, rows)]
+    return (mine, up, down, up_half, down_half), sources
 
 
 def local(
@@ -598,7 +608,8 @@
     hot_values, hot_line = call_hot_rows(hot_row, is_cold, hot_table)
     ask_in = lax.all_to_all(ask, "shard", split_axis=0, concat_axis=0, tiled=True)
     requested = ask_in[:, :SLOT]
-    found = jnp.take(cold_table, requested, axis=0)
+    requested, hot_line = lax.optimization_barrier((requested, hot_line))
+    found = cold_table.at[requested].get(mode="promise_in_bounds")
     returned = lax.all_to_all(found, "shard", split_axis=0, concat_axis=0, tiled=True)
     logits, outgoing = call_cin(
         grad_logit, hot_values, hot_line, slot, returned, hot_table.shape[0], out_weight,
@@ -607,12 +618,14 @@
     incoming = lax.all_to_all(outgoing, "shard", split_axis=0, concat_axis=0, tiled=True)
     rows = owners * CAP
     share = hot_table.shape[0] // owners
-    parts = exchange(call_merge(incoming, ask_in, 4), rows + 8)
+    tall = rows + 8
+    block = call_merge(incoming, ask_in, 1)[0]
+    parts, places = exchange(block, tall)
     hot_out = lax.all_to_all(
-        call_hot((*parts[0:3], parts[4]), owners, share),
+        call_hot(parts, (3 * tall,) * 3 + (None, 2 * tall), owners, share),
         "shard", split_axis=0, concat_axis=0, tiled=True,
     )
-    cold_total = call_scatter(parts, rows + 8, rows, cold_table.shape[0])
+    cold_total = call_scatter(parts, places, rows, cold_table.shape[0])
     hot_grad = hot_out.reshape(hot_table.shape)
     return (hot_grad, cold_total, logits)
 

time: 150 us -> 144 us (0.960)
  blocking collectives: 66 us -> 16.5 us
  starting transfers between devices: 29.8 us -> 57.5 us
  waiting for transfers between devices: 15.4 us -> 29.5 us
  Pallas kernels: 31.4 us -> 33.4 us
    all_to_all x2 -> x0, blocking collectives: 47.5 us -> none  [the longest x1 30.9 us: exchange(): lax.all_to_all(blocks, 'group', split_axis=0, concat_axis=0, axis_index_g...]
    ppermute x4 -> x7, starting transfers between devices: 17.7 us -> 33.9 us  [move(): lax.ppermute(x, 'group', [(i, (i + hop) % groups) for i in range(groups)])]
    all_to_all x1 -> x2, starting transfers between devices: 7.97 us -> 19.2 us  [the longest x1 10.3 us: local(): lax.all_to_all(ask, 'shard', split_axis=0, concat_axis=0, tiled=True)]
    all_to_all x1 -> x2, waiting for transfers between devices: 0.01 us -> 6.91 us  [the longest x1 3.6 us: local(): lax.all_to_all(call_hot(parts, (3 * tall,) * 3 + (None, 2 * tall), owners...]
    ppermute x4 -> x7, waiting for transfers between devices: 13.8 us -> 18.1 us  [move(): lax.ppermute(x, 'group', [(i, (i + hop) % groups) for i in range(groups)])]
    all_to_all x1, waiting for transfers between devices: 1.64 us -> 4.51 us  [local(): lax.all_to_all(found, 'shard', split_axis=0, concat_axis=0, tiled=True)]
    all_to_all x1, blocking collectives: 18.5 us -> 16.5 us  [local(): lax.all_to_all(outgoing, 'shard', split_axis=0, concat_axis=0, tiled=True)]
    unnamed x23 -> x19, local copies, waits for them, and re-layouts: 4 us -> 3.23 us
  transfers between devices with their start and end apart: 6 -> 10, of which waited for: 4 -> 6; matrix products, arithmetic and copies ran while one was open for 0% -> 0% of each run, Pallas kernels for 8% -> 9%
where the time goes in v5:
time: 144 us; the launch traced here: 143 us
  starting transfers between devices  57.5 us (40%)
  Pallas kernels  33.4 us (23%)
  waiting for transfers between devices  29.5 us (20%)
  blocking collectives  16.5 us (11%)
  local copies, waits for them, and re-layouts  5.26 us (4%)
    ppermute x7, starting transfers between devices, move(): lax.ppermute(x, 'group', [(i, (i + hop) % groups) for i in range(groups)])  33.9 us
    ppermute x7, waiting for transfers between devices, move(): lax.ppermute(x, 'group', [(i, (i + hop) % groups) for i in range(groups)])  18.1 us
    pallas_call x1, Pallas kernels, call_cin(): pl.pallas_call(cin_kernel, out_shape=(jax.ShapeDtypeStruct((samples,), F3...  17.9 us
    all_to_all x1, blocking collectives, local(): lax.all_to_all(outgoing, 'shard', split_axis=0, concat_axis=0, tiled=True)  16.5 us
    all_to_all x1, starting transfers between devices, local(): lax.all_to_all(ask, 'shard', split_axis=0, concat_axis=0, tiled=True)  10.3 us
    all_to_all x1, starting transfers between devices, local(): lax.all_to_all(call_hot(parts, (3 * tall,) * 3 + (None, 2 * tall), owners...  8.9 us
    pallas_call x1, Pallas kernels, call_scatter(): pl.pallas_call(functools.partial(scatter_kernel, places, rows), out_shape...  7.83 us
    all_to_all x1, waiting for transfers between devices, local(): lax.all_to_all(found, 'shard', split_axis=0, concat_axis=0, tiled=True)  4.51 us
  transfers between devices with their start and end apart: 10, of which 6 were waited for; matrix products, arithmetic and copies ran while one was open for 0% of the time, Pallas kernels for 9%

profile of v5, /device:TPU:1, one launch (start us, length us, event | category | flops | bytes accessed | tf_op | source)
XLA Modules:
  0.0 143.0 jit_solution(4528158825041361358)
XLA Ops:
  0.6 0.0 copy-start
  0.7 2.2 %route.1 = (s32[32,128]{1,0:T(8,128)}, s32[320,128]{1,0:T(8,128)S(1)}) custom-call(s32[8,39]{1,0:T(8,128)} %row_hbm.1, s32[8,39]{1,0:T(8,128)} %owner_hbm.1, s32[8,39]{1,0:T(8,128)} %cold_ref.1), custom_call_target="tpu_custom_call" | custom-call | tf_op jit(solution)/shard_map/route/pallas_call | solution.py:239
  2.9 10.3 %all-to-all-start = ((s32[32,1,128]{2,1,0:T(1,128)}), s32[32,1,128]{2,1,0:T(1,128)S(1)}, u32[]{:S(2)}, u32[]{:S(2)}) async-start(s32[32,1,128]{2,1,0:T(1,128)} %bitcast.1), calls=%async_computation | async-start | bytes 32768 | tf_op jit(solution)/shard_map/all_to_all | solution.py:609
  13.2 0.0 copy-start.3
  13.2 1.0 copy-done.3
  14.3 0.7 copy-done.5
  15.0 0.7 copy-done.6
  15.7 1.3 hot_rows.1
  16.9 3.3 %all-to-all-done = s32[32,1,128]{2,1,0:T(1,128)S(1)} async-done(((s32[32,1,128]{2,1,0:T(1,128)}), s32[32,1,128]{2,1,0:T(1,128)S(1)}, u32[]{:S(2)}, u32[]{:S(2)}) %all-to-all-start) | async-done | bytes 16416 | tf_op jit(solution)/shard_map/all_to_all | solution.py:609
  20.2 0.1 reshape.18
  20.3 1.9 %gather_fusion = bf16[512,128]{1,0:T(8,128)(2,1)} fusion(bf16[4096,128]{1,0:T(8,128)(2,1)S(1)} %copy-done, s32[1024]{0:T(1024)S(1)} %pad_clamp_fusion), kind=kCustom, calls=%fused_computation | custom fusion | bytes 264192 | tf_op jit(solution)/shard_map/gather | solution.py:612
  22.3 4.3 %all-to-all-start.1 = ((bf16[32,16,128]{2,1,0:T(8,128)(2,1)}), bf16[32,16,128]{2,1,0:T(8,128)(2,1)S(1)}, u32[]{:S(2)}, u32[]{:S(2)}) async-start(bf16[32,16,128]{2,1,0:T(8,128)(2,1)} %bitcast.3), calls=%async_computation.1 | async-start | bytes 262144 | tf_op jit(solution)/shard_map/all_to_all | solution.py:613
  26.6 3.1 %prep.1 = (bf16[112,1872]{1,0:T(8,128)(2,1)}, bf16[1872,128]{1,0:T(8,128)(2,1)}, bf16[112,4368]{1,0:T(8,128)(2,1)}, bf16[4368,128]{1,0:T(8,128)(2,1)}, bf16[112,...) custom-call(bf16[100,1521]{1,0:T(8,128)(2,1)S(1)} %copy-done.4, bf16[100,3900]{1,0:T(8,128)(2,1)S(1)} %copy-done.1, ...), custom_call_target="tpu_custom_call" | custom-call | tf_op jit(solution)/shard_map/prep/pallas_call | solution.py:342
  29.8 4.5 %all-to-all-done.1 = bf16[32,16,128]{2,1,0:T(8,128)(2,1)S(1)} async-done(((bf16[32,16,128]{2,1,0:T(8,128)(2,1)}), bf16[32,16,128]{2,1,0:T(8,128)(2,1)S(1)}, u32[]{:S(2)}, u32[]{:S(2)}) %all-to-all-start.1) | async-done | bytes 131104 | tf_op jit(solution)/shard_map/all_to_all | solution.py:613
  34.3 17.9 %cin.1 = (f32[8]{0:T(128)}, bf16[32,80,128]{2,1,0:T(8,128)(2,1)S(1)}) custom-call(f32[8]{0:T(128)S(1)} %copy-done.8, s32[8,320]{1,0:T(8,128)S(1)} %get-tuple-element.19.hot_line_ref, s32[320,128]{1,0:T(8,128)S(1)} %get-tuple-element.20.slot_ref, bf16[512,128]{1,0:T(8,128)(2,1)S(1)} %bitcast.9, f32[3,100]{1,0:T(4,128)S(1)} %copy-done.7, ...), custom_call_target="tpu_custom_call" | custom-call | tf_op jit(solution)/shard_map/cin/pallas_call | solution.py:366
  52.2 16.5 %all_to_all.26.in_ref = bf16[32,80,128]{2,1,0:T(8,128)(2,1)S(1)} all-to-all(bf16[32,80,128]{2,1,0:T(8,128)(2,1)S(1)} %get-tuple-element.29), channel_id=1, replica_groups=mesh['group'=16,'shard'=32] {'shard'}, dimensions={0} | all-to-all | bytes 1310720 | tf_op jit(solution)/shard_map/all_to_all | solution.py:618
  68.7 0.2 merge.1
  68.8 13.6 %collective-permute-start.2 = (bf16[360,128]{1,0:T(8,128)(2,1)S(1)}, bf16[360,128]{1,0:T(8,128)(2,1)S(1)}, u32[]{:S(2)}, u32[]{:S(2)}) collective-permute-start(bf16[360,128]{1,0:T(8,128)(2,1)S(1)} %bitcast.10), channel_id=1, source_target_pairs={{0,256},{32,288},{64,320},{96,352},{128,384},{160,416},{192,448},{... | collective-permute-start | bytes 276488 | tf_op jit(solution)/shard_map/ppermute | solution.py:585
  82.4 1.9 %collective-permute-start.1 = (bf16[360,128]{1,0:T(8,128)(2,1)S(1)}, bf16[360,128]{1,0:T(8,128)(2,1)S(1)}, u32[]{:S(2)}, u32[]{:S(2)}) collective-permute-start(bf16[360,128]{1,0:T(8,128)(2,1)S(1)} %bitcast.11), channel_id=1, source_target_pairs={{0,384},{32,416},{64,448},{96,480},{128,0},{160,32},{192,64},{224,... | collective-permute-start | bytes 276488 | tf_op jit(solution)/shard_map/ppermute | solution.py:585
  84.4 7.5 %collective-permute-start = (bf16[360,128]{1,0:T(8,128)(2,1)S(1)}, bf16[360,128]{1,0:T(8,128)(2,1)S(1)}, u32[]{:S(2)}, u32[]{:S(2)}) collective-permute-start(bf16[360,128]{1,0:T(8,128)(2,1)S(1)} %bitcast.12), channel_id=1, source_target_pairs={{0,128},{32,160},{64,192},{96,224},{128,256},{160,288},{192,320},{... | collective-permute-start | bytes 276488 | tf_op jit(solution)/shard_map/ppermute | solution.py:585
  91.8 8.0 %collective-permute-done.1.refs_2_ = bf16[360,128]{1,0:T(8,128)(2,1)S(1)} collective-permute-done((bf16[360,128]{1,0:T(8,128)(2,1)S(1)}, bf16[360,128]{1,0:T(8,128)(2,1)S(1)}, u32[]{:S(2)}, u32[]{:S(2)}) %collective-permute-start.1) | collective-permute-done | bytes 92192 | tf_op jit(solution)/shard_map/ppermute | solution.py:585
  99.9 2.5 %collective-permute-start.4 = (bf16[1248,128]{1,0:T(8,128)(2,1)S(1)}, bf16[1248,128]{1,0:T(8,128)(2,1)S(1)}, u32[]{:S(2)}, u32[]{:S(2)}) collective-permute-start(bf16[1248,128]{1,0:T(8,128)(2,1)S(1)} %pack.1.refs_0_), channel_id=1, source_target_pairs={{0,480},{32,0},{64,32},{96,64},{128,96},{160,128},{192,160},{224,1... | collective-permute-start | bytes 958472 | tf_op jit(solution)/shard_map/ppermute | solution.py:585
  102.4 3.2 %collective-permute-start.3 = (bf16[1248,128]{1,0:T(8,128)(2,1)S(1)}, bf16[1248,128]{1,0:T(8,128)(2,1)S(1)}, u32[]{:S(2)}, u32[]{:S(2)}) collective-permute-start(bf16[1248,128]{1,0:T(8,128)(2,1)S(1)} %pack.1.refs_0_), channel_id=1, source_target_pairs={{0,32},{32,64},{64,96},{96,128},{128,160},{160,192},{192,224},{224... | collective-permute-start | bytes 958472 | tf_op jit(solution)/shard_map/ppermute | solution.py:585
  105.6 5.2 %collective-permute-done.4.refs_2_ = bf16[1248,128]{1,0:T(8,128)(2,1)S(1)} collective-permute-done((bf16[1248,128]{1,0:T(8,128)(2,1)S(1)}, bf16[1248,128]{1,0:T(8,128)(2,1)S(1)}, u32[]{:S(2)}, u32[]{:S(2)}) %collective-permute-start.4) | collective-permute-done | bytes 319520 | tf_op jit(solution)/shard_map/ppermute | solution.py:585
  110.7 3.1 %collective-permute-start.6 = (bf16[656,128]{1,0:T(8,128)(2,1)S(1)}, bf16[656,128]{1,0:T(8,128)(2,1)S(1)}, u32[]{:S(2)}, u32[]{:S(2)}) collective-permute-start(bf16[656,128]{1,0:T(8,128)(2,1)S(1)} %slice.16), channel_id=1, source_target_pairs={{0,480},{32,0},{64,32},{96,64},{128,96},{160,128},{192,160},{224,1... | collective-permute-start | bytes 503816 | tf_op jit(solution)/shard_map/ppermute | solution.py:585
  113.8 2.2 %collective-permute-start.5 = (bf16[592,128]{1,0:T(8,128)(2,1)S(1)}, bf16[592,128]{1,0:T(8,128)(2,1)S(1)}, u32[]{:S(2)}, u32[]{:S(2)}) collective-permute-start(bf16[592,128]{1,0:T(8,128)(2,1)S(1)} %slice.15), channel_id=1, source_target_pairs={{0,32},{32,64},{64,96},{96,128},{128,160},{160,192},{192,224},{224... | collective-permute-start | bytes 454664 | tf_op jit(solution)/shard_map/ppermute | solution.py:585
  116.1 4.9 %collective-permute-done.5.refs_3_ = bf16[592,128]{1,0:T(8,128)(2,1)S(1)} collective-permute-done((bf16[592,128]{1,0:T(8,128)(2,1)S(1)}, bf16[592,128]{1,0:T(8,128)(2,1)S(1)}, u32[]{:S(2)}, u32[]{:S(2)}) %collective-permute-start.5) | collective-permute-done | bytes 151584 | tf_op jit(solution)/shard_map/ppermute | solution.py:585
  121.0 0.9 hot_sum.1
  121.8 8.9 %all-to-all-start.3 = ((bf16[32,64,128]{2,1,0:T(8,128)(2,1)}), bf16[32,64,128]{2,1,0:T(8,128)(2,1)S(1)}, u32[]{:S(2)}, u32[]{:S(2)}) async-start(bf16[32,64,128]{2,1,0:T(8,128)(2,1)} %hot_sum.1), calls=%async_computation.3 | async-start | bytes 1048576 | tf_op jit(solution)/shard_map/all_to_all | solution.py:624
  130.7 7.8 %cold_scatter.1 = bf16[4096,128]{1,0:T(8,128)(2,1)} custom-call(bf16[1248,128]{1,0:T(8,128)(2,1)S(1)} %pack.1.refs_0_, bf16[1248,128]{1,0:T(8,128)(2,1)S(1)} %collective-permute-done.3.refs_1_, bf16[1248,128]{1,0:T(8,128)(2,1)S(1)} %collective-permute-done.4.refs_2_, bf16[592,128]{1,0:T(8,128)(2,1)S(1)} %collective-permute-done.5.refs_3_, ...), custom_call_target="tpu_custom_call" | custom-call | tf_op jit(solution)/shard_map/cold_scatter/pallas_call | solution.py:562
  138.6 3.6 %all-to-all-done.3 = bf16[32,64,128]{2,1,0:T(8,128)(2,1)S(1)} async-done(((bf16[32,64,128]{2,1,0:T(8,128)(2,1)}), bf16[32,64,128]{2,1,0:T(8,128)(2,1)S(1)}, u32[]{:S(2)}, u32[]{:S(2)}) %all-to-all-start.3) | async-done | bytes 524320 | tf_op jit(solution)/shard_map/all_to_all | solution.py:624
  142.2 0.8 copy.16
  (22 shorter events, 0.1 us)
Async XLA Ops:
  0.6 19.7 %copy-start = (bf16[4096,128]{1,0:T(8,128)(2,1)S(1)}, bf16[4096,128]{1,0:T(8,128)(2,1)}, u32[]{:S(2)}) copy-start(bf16[4096,128]{1,0:T(8,128)(2,1)} %param.17) | copy-start | bytes 3145732
  0.6 26.0 %copy-start.2 = (bf16[100,3900]{1,0:T(8,128)(2,1)S(1)}, bf16[100,3900]{1,0:T(8,128)(2,1)}, u32[]{:S(2)}) copy-start(bf16[100,3900]{1,0:T(8,128)(2,1)} %refs_2_.1) | copy-start | bytes 2340004
  0.7 26.0 %copy-start.1 = (bf16[100,3900]{1,0:T(8,128)(2,1)S(1)}, bf16[100,3900]{1,0:T(8,128)(2,1)}, u32[]{:S(2)}) copy-start(bf16[100,3900]{1,0:T(8,128)(2,1)} %refs_1_.1) | copy-start | bytes 2340004
  2.9 17.3 %all-to-all-start = ((s32[32,1,128]{2,1,0:T(1,128)}), s32[32,1,128]{2,1,0:T(1,128)S(1)}, u32[]{:S(2)}, u32[]{:S(2)}) async-start(s32[32,1,128]{2,1,0:T(1,128)} %bitcast.1), calls=%async_computation | async-start | bytes 32768 | tf_op jit(solution)/shard_map/all_to_all | solution.py:609
  13.2 1.0 copy-start.3
  14.3 0.7 copy-start.5
  15.0 0.7 copy-start.6
  15.7 11.0 %copy-start.4 = (bf16[100,1521]{1,0:T(8,128)(2,1)S(1)}, bf16[100,1521]{1,0:T(8,128)(2,1)}, u32[]{:S(2)}) copy-start(bf16[100,1521]{1,0:T(8,128)(2,1)} %refs_0_.1) | copy-start | bytes 912604
  22.3 12.0 %copy-start.7 = (f32[3,100]{1,0:T(4,128)S(1)}, f32[3,100]{1,0:T(4,128)}, u32[]{:S(2)}) copy-start(f32[3,100]{1,0:T(4,128)} %scale_ref.1) | copy-start | bytes 3604
  22.3 12.0 %copy-start.8 = (f32[8]{0:T(128)S(1)}, f32[8]{0:T(128)}, u32[]{:S(2)}) copy-start(f32[8]{0:T(128)} %gl_ref.1) | copy-start | bytes 100
  22.3 12.0 %all-to-all-start.1 = ((bf16[32,16,128]{2,1,0:T(8,128)(2,1)}), bf16[32,16,128]{2,1,0:T(8,128)(2,1)S(1)}, u32[]{:S(2)}, u32[]{:S(2)}) async-start(bf16[32,16,128]{2,1,0:T(8,128)(2,1)} %bitcast.3), calls=%async_computation.1 | async-start | bytes 262144 | tf_op jit(solution)/shard_map/all_to_all | solution.py:613
  68.8 23.0 %collective-permute-start.2 = (bf16[360,128]{1,0:T(8,128)(2,1)S(1)}, bf16[360,128]{1,0:T(8,128)(2,1)S(1)}, u32[]{:S(2)}, u32[]{:S(2)}) collective-permute-start(bf16[360,128]{1,0:T(8,128)(2,1)S(1)} %bitcast.10), channel_id=1, source_target_pairs={{0,256},{32,288},{64,320},{96,352},{128,384},{160,416},{192,448},{... | collective-permute-start | bytes 276488 | tf_op jit(solution)/shard_map/ppermute | solution.py:585
  82.4 17.4 %collective-permute-start.1 = (bf16[360,128]{1,0:T(8,128)(2,1)S(1)}, bf16[360,128]{1,0:T(8,128)(2,1)S(1)}, u32[]{:S(2)}, u32[]{:S(2)}) collective-permute-start(bf16[360,128]{1,0:T(8,128)(2,1)S(1)} %bitcast.11), channel_id=1, source_target_pairs={{0,384},{32,416},{64,448},{96,480},{128,0},{160,32},{192,64},{224,... | collective-permute-start | bytes 276488 | tf_op jit(solution)/shard_map/ppermute | solution.py:585
  84.4 15.5 %collective-permute-start = (bf16[360,128]{1,0:T(8,128)(2,1)S(1)}, bf16[360,128]{1,0:T(8,128)(2,1)S(1)}, u32[]{:S(2)}, u32[]{:S(2)}) collective-permute-start(bf16[360,128]{1,0:T(8,128)(2,1)S(1)} %bitcast.12), channel_id=1, source_target_pairs={{0,128},{32,160},{64,192},{96,224},{128,256},{160,288},{192,320},{... | collective-permute-start | bytes 276488 | tf_op jit(solution)/shard_map/ppermute | solution.py:585
  99.9 10.8 %collective-permute-start.4 = (bf16[1248,128]{1,0:T(8,128)(2,1)S(1)}, bf16[1248,128]{1,0:T(8,128)(2,1)S(1)}, u32[]{:S(2)}, u32[]{:S(2)}) collective-permute-start(bf16[1248,128]{1,0:T(8,128)(2,1)S(1)} %pack.1.refs_0_), channel_id=1, source_target_pairs={{0,480},{32,0},{64,32},{96,64},{128,96},{160,128},{192,160},{224,1... | collective-permute-start | bytes 958472 | tf_op jit(solution)/shard_map/ppermute | solution.py:585
  102.4 11.4 %collective-permute-start.3 = (bf16[1248,128]{1,0:T(8,128)(2,1)S(1)}, bf16[1248,128]{1,0:T(8,128)(2,1)S(1)}, u32[]{:S(2)}, u32[]{:S(2)}) collective-permute-start(bf16[1248,128]{1,0:T(8,128)(2,1)S(1)} %pack.1.refs_0_), channel_id=1, source_target_pairs={{0,32},{32,64},{64,96},{96,128},{128,160},{160,192},{192,224},{224... | collective-permute-start | bytes 958472 | tf_op jit(solution)/shard_map/ppermute | solution.py:585
  110.7 10.3 %collective-permute-start.6 = (bf16[656,128]{1,0:T(8,128)(2,1)S(1)}, bf16[656,128]{1,0:T(8,128)(2,1)S(1)}, u32[]{:S(2)}, u32[]{:S(2)}) collective-permute-start(bf16[656,128]{1,0:T(8,128)(2,1)S(1)} %slice.16), channel_id=1, source_target_pairs={{0,480},{32,0},{64,32},{96,64},{128,96},{160,128},{192,160},{224,1... | collective-permute-start | bytes 503816 | tf_op jit(solution)/shard_map/ppermute | solution.py:585
  113.8 7.1 %collective-permute-start.5 = (bf16[592,128]{1,0:T(8,128)(2,1)S(1)}, bf16[592,128]{1,0:T(8,128)(2,1)S(1)}, u32[]{:S(2)}, u32[]{:S(2)}) collective-permute-start(bf16[592,128]{1,0:T(8,128)(2,1)S(1)} %slice.15), channel_id=1, source_target_pairs={{0,32},{32,64},{64,96},{96,128},{128,160},{160,192},{192,224},{224... | collective-permute-start | bytes 454664 | tf_op jit(solution)/shard_map/ppermute | solution.py:585
  121.8 20.3 %all-to-all-start.3 = ((bf16[32,64,128]{2,1,0:T(8,128)(2,1)}), bf16[32,64,128]{2,1,0:T(8,128)(2,1)S(1)}, u32[]{:S(2)}, u32[]{:S(2)}) async-start(bf16[32,64,128]{2,1,0:T(8,128)(2,1)} %hot_sum.1), calls=%async_computation.3 | async-start | bytes 1048576 | tf_op jit(solution)/shard_map/all_to_all | solution.py:624

commit v6 on v5

--- a/solution.py
+++ b/solution.py
@@ -79,13 +79,12 @@
     slot_ref,
     back_ref,
     scale_ref,
+    mix_ref,
     hot_hbm,
     f1_hbm,
     f2_hbm,
-    f3_hbm,
     b1_hbm,
     b2_hbm,
-    b3_hbm,
     logit_ref,
     outgoing_ref,
     pick_ref,
@@ -95,7 +94,7 @@
     x2_ref,
     x3_ref,
     w2_ref,
-    w3_ref,
+    last_ref,
     outer_ref,
     carry_ref,
     part_ref,
@@ -103,15 +102,13 @@
     grad_ref,
     f1_ref,
     f2_ref,
-    f3_ref,
     b1_ref,
     b2_ref,
-    b3_ref,
     hot_ref,
     sems,
 ):
-    held = (hot_ref, f1_ref, f2_ref, f3_ref, b3_ref, b2_ref, b1_ref)
-    kept = (hot_hbm, f1_hbm, f2_hbm, f3_hbm, b3_hbm, b2_hbm, b1_hbm)
+    held = (hot_ref, f1_ref, f2_ref, b2_ref, b1_ref)
+    kept = (hot_hbm, f1_hbm, f2_hbm, b2_hbm, b1_hbm)
     copies = [
         pltpu.make_async_copy(source, target, sems.at[n])
         for n, (source, target) in enumerate(zip(kept, held))
@@ -148,8 +145,8 @@
 
     pool_ref[...] = jnp.zeros(pool_ref.shape, F32)
     states = (embb_ref, x2_ref, x3_ref)
-    wides = (emb_ref, w2_ref, w3_ref)
-    for k, w_ref in enumerate((f1_ref, f2_ref, f3_ref)):
+    wides = (emb_ref, w2_ref)
+    for k, w_ref in enumerate((f1_ref, f2_ref)):
         source = states[k]
         height = source.shape[0]
 
@@ -169,26 +166,41 @@
                 weight, outer_ref[0:depth, n : n + 256], preferred_element_type=F32
             ).astype(BF16)
             wide = value.astype(F32)
-            if k < 2:
-                states[k + 1][:, n : n + 256] = value
+            states[k + 1][:, n : n + 256] = value
+            if k < 1:
                 wides[k + 1][:, n : n + 256] = wide
             pool_ref[:, n : n + 256] += wide * out_weight_ref[0:tall, k : k + 1]
 
-    for s in range(samples):
-        logit_ref[s] = jnp.sum(pool_ref[:, s * breadth : (s + 1) * breadth])
-
+    mix = mix_ref[...]
+    mix_high = mix.astype(BF16)
+    mix_low = (mix - mix_high.astype(F32)).astype(BF16)
+    small = embb_ref.shape[0]
+    turned_high = mix_high.astype(F32).T[0:small, 0:tall].astype(BF16)
+    turned_low = mix_low.astype(F32).T[0:small, 0:tall].astype(BF16)
     part_ref[...] = jnp.zeros(part_ref.shape, F32)
     grad_ref[...] = jnp.zeros(grad_ref.shape, BF16)
-    for k, w_ref in reversed(tuple(enumerate((b1_ref, b2_ref, b3_ref)))):
-        copies[6 - k].wait()
+    for s in range(samples):
+        at = slice(s * breadth, (s + 1) * breadth)
+        below = jnp.dot(turned_high, x3_ref[:, at], preferred_element_type=F32) + jnp.dot(
+            turned_low, x3_ref[:, at], preferred_element_type=F32
+        )
+        logit_ref[s] = jnp.sum(pool_ref[:, at]) + jnp.sum(below * emb_ref[:, at])
+        last_ref[:, at] = below * gl_ref[s]
+        across = jnp.dot(
+            mix_high[:, 0:small], embb_ref[:, at], preferred_element_type=F32
+        ) + jnp.dot(mix_low[:, 0:small], embb_ref[:, at], preferred_element_type=F32)
+        carry_ref[:, at] = across * gl_ref[s]
+
+    for k, w_ref in reversed(tuple(enumerate((b1_ref, b2_ref)))):
+        copies[4 - k].wait()
         source = wides[k]
         height = source.shape[0]
         for s in range(samples):
             at = slice(s * breadth, (s + 1) * breadth)
-            value = jnp.broadcast_to(gl_ref[s] * out_weight_ref[0:tall, k : k + 1], (tall, breadth))
-            if k < 2:
-                value = value + carry_ref[:, at]
-            grad_ref[0:tall, at] = value.astype(BF16)
+            value = jnp.broadcast_to(
+                gl_ref[s] * out_weight_ref[0:tall, k : k + 1], (tall, breadth)
+            )
+            grad_ref[0:tall, at] = (value + carry_ref[:, at]).astype(BF16)
         carry_ref[0:height, :] = jnp.zeros((height, lanes), F32)
 
         def back(n, _, source=source, height=height, w_ref=w_ref):
@@ -219,7 +231,7 @@
 
         lax.fori_loop(0, lanes // 256, back, 0)
 
-    grads = carry_ref[0:FP, :] + jnp.sum(part_ref[...].reshape(FP, 8, lanes), axis=1)
+    grads = carry_ref[0:FP, :] + last_ref[0:FP, :] + jnp.sum(part_ref[...].reshape(FP, 8, lanes), axis=1)
     stacked = jnp.concatenate(
         [grads[:, s * breadth : (s + 1) * breadth] for s in range(samples)], axis=0
     ).astype(BF16)
@@ -299,9 +311,11 @@
 
 
 def prep_kernel(fields, *refs):
-    count = (len(refs) - 3) // 5
-    weights, outs = refs[0:count], refs[count : 3 * count]
-    held, (line_ref, wide_ref, sems) = refs[3 * count : 5 * count], refs[5 * count :]
+    count = (len(refs) - 7) // 5
+    weights, (third_ref, scale_ref) = refs[0:count], refs[count : count + 2]
+    outs, mix_ref = refs[count + 2 : 3 * count + 2], refs[3 * count + 2]
+    held = refs[3 * count + 3 : 5 * count + 3]
+    line_ref, wide_ref, turn_ref, sems = refs[5 * count + 3 :]
     copies = []
     for k, w_ref in enumerate(weights):
         f_ref, b_ref = held[2 * k : 2 * k + 2]
@@ -326,11 +340,30 @@
             f_ref[:, c : c + width] = b_ref[c : c + width, :].T[0:tall]
         copies.append(pltpu.make_async_copy(f_ref, outs[2 * k], sems.at[2 * k]))
         copies[-1].start()
+    rows, cols = third_ref.shape
+    layers, maps = scale_ref.shape
+    turn_ref[...] = jnp.zeros(turn_ref.shape, F32)
+    turn_ref[0:layers, 0:maps] = scale_ref[...]
+    scale = turn_ref[...].T[:, layers - 1 : layers]
+    line_ref[...] = jnp.zeros(line_ref.shape, F32)
+    line_ref[0:rows, 0:cols] = third_ref[...].astype(F32)
+    tall = mix_ref.shape[0]
+    for c in range(0, fields * tall, 128):
+        if c < cols:
+            total = jnp.sum(line_ref[:, c : c + 128] * scale, axis=0, keepdims=True)
+            wide_ref[c : c + 128, :] = jnp.broadcast_to(total, (128, 128)).T
+        else:
+            wide_ref[c : c + 128, :] = jnp.zeros((128, 128), F32)
+    lane = iota((tall, 128), 1)
+    mix = jnp.zeros((tall, 128), F32)
+    for f in range(fields):
+        mix = jnp.where(lane == f, wide_ref[pl.ds(f, tall, stride=fields), :], mix)
+    mix_ref[...] = mix
     for copy in copies:
         copy.wait()
 
 
-def call_prep(weights, fields):
+def call_prep(weights, third, out_weight, fields):
     rows = weights[0].shape[0]
     tall = -(-rows // 16) * 16
     shapes = []
@@ -338,24 +371,28 @@
         pitch = -(-(w.shape[1] // fields) // 16) * 16
         shapes.append(jax.ShapeDtypeStruct((tall, fields * pitch), BF16))
         shapes.append(jax.ShapeDtypeStruct((fields * pitch, 128), BF16))
-    deep = max(-(-shape.shape[0] // 128) * 128 for shape in shapes)
+    deep = -(-fields * tall // 128) * 128
     return pl.pallas_call(
         functools.partial(prep_kernel, fields),
-        out_shape=tuple(pltpu.HBM(shape.shape, BF16) for shape in shapes),
-        in_specs=[VMEM] * len(weights),
-        out_specs=tuple([HBM] * len(shapes)),
+        out_shape=tuple(pltpu.HBM(shape.shape, BF16) for shape in shapes)
+        + (jax.ShapeDtypeStruct((tall, 128), F32),),
+        in_specs=[VMEM] * (len(weights) + 2),
+        out_specs=tuple([HBM] * len(shapes)) + (VMEM,),
         scratch_shapes=[pltpu.VMEM(shape.shape, BF16) for shape in shapes]
         + [
             pltpu.VMEM((128, deep), F32),
             pltpu.VMEM((deep, 128), F32),
+            pltpu.VMEM((128, 128), F32),
             pltpu.SemaphoreType.DMA((len(shapes),)),
         ],
         compiler_params=pltpu.CompilerParams(vmem_limit_bytes=14 << 20),
         name="prep",
-    )(*weights)
-
-
-def call_cin(grad_logit, hot_values, hot_line, slot, back, hot_rows, out_weight, forward, backward):
+    )(*weights, third, out_weight)
+
+
+def call_cin(
+    grad_logit, hot_values, hot_line, slot, back, hot_rows, out_weight, mix, forward, backward
+):
     total, breadth = hot_values.shape
     samples = grad_logit.shape[0]
     lanes = samples * breadth
@@ -369,7 +406,7 @@
             jax.ShapeDtypeStruct((samples,), F32),
             jax.ShapeDtypeStruct((owners, SLOT + hot_rows // owners, breadth), BF16),
         ),
-        in_specs=[SMEM] + [VMEM] * 4 + [HBM] * 7,
+        in_specs=[SMEM] + [VMEM] * 5 + [HBM] * 5,
         out_specs=(SMEM, VMEM),
         scratch_shapes=[
             pltpu.VMEM((total, slots), BF16),
@@ -379,7 +416,7 @@
             pltpu.VMEM((tall, lanes), BF16),
             pltpu.VMEM((tall, lanes), BF16),
             pltpu.VMEM((tall, lanes), F32),
-            pltpu.VMEM((tall, lanes), F32),
+            pltpu.VMEM((small, lanes), F32),
             pltpu.VMEM((fields * tall, lanes), BF16),
             pltpu.VMEM((tall, lanes), F32),
             pltpu.VMEM((FP * 8, lanes), F32),
@@ -387,11 +424,11 @@
             pltpu.VMEM((128, lanes), BF16),
         ]
         + [pltpu.VMEM(x.shape, BF16) for x in (*forward, *backward, hot_values)]
-        + [pltpu.SemaphoreType.DMA((7,))],
-        compiler_params=pltpu.CompilerParams(vmem_limit_bytes=32 << 20),
+        + [pltpu.SemaphoreType.DMA((5,))],
+        compiler_params=pltpu.CompilerParams(vmem_limit_bytes=28 << 20),
         name="cin",
     )(
-        grad_logit, hot_line, slot, back.reshape(slots, breadth), out_weight,
+        grad_logit, hot_line, slot, back.reshape(slots, breadth), out_weight, mix,
         *(
             pltpu.with_memory_space_constraint(x, pltpu.HBM)
             for x in (hot_values, *forward, *backward)
@@ -603,7 +640,7 @@
     samples, fields = hot_row.shape
     breadth = hot_table.shape[1]
     owners = lax.axis_size("shard")
-    forms = call_prep((first_weight, second_weight, third_weight), fields)
+    *forms, mix = call_prep((first_weight, second_weight), third_weight, out_weight, fields)
     ask, slot = call_route(cold_row, cold_owner, is_cold, owners)
     hot_values, hot_line = call_hot_rows(hot_row, is_cold, hot_table)
     ask_in = lax.all_to_all(ask, "shard", split_axis=0, concat_axis=0, tiled=True)
@@ -613,7 +650,7 @@
     returned = lax.all_to_all(found, "shard", split_axis=0, concat_axis=0, tiled=True)
     logits, outgoing = call_cin(
         grad_logit, hot_values, hot_line, slot, returned, hot_table.shape[0], out_weight,
-        forms[0::2], forms[1::2],
+        mix, forms[0::2], forms[1::2],
     )
     incoming = lax.all_to_all(outgoing, "shard", split_axis=0, concat_axis=0, tiled=True)
     rows = owners * CAP

time: 144 us -> 138 us (0.958)
  Pallas kernels: 33.4 us -> 27.3 us
    pallas_call x1, Pallas kernels: 17.9 us -> 12.4 us  [call_cin(): pl.pallas_call(cin_kernel, out_shape=(jax.ShapeDtypeStruct((samples,), F3...]
  transfers between devices with their start and end apart: 10 -> 10, of which waited for: 6 -> 6; matrix products, arithmetic and copies ran while one was open for 0% -> 0% of each run, Pallas kernels for 9% -> 8%
where the time goes in v6:
time: 138 us; the launch traced here: 137 us
  starting transfers between devices  58.5 us (42%)
  waiting for transfers between devices  29 us (21%)
  Pallas kernels  27.3 us (20%)
  blocking collectives  16.5 us (12%)
  local copies, waits for them, and re-layouts  5.24 us (4%)
    ppermute x7, starting transfers between devices, move(): lax.ppermute(x, 'group', [(i, (i + hop) % groups) for i in range(groups)])  33.7 us
    ppermute x7, waiting for transfers between devices, move(): lax.ppermute(x, 'group', [(i, (i + hop) % groups) for i in range(groups)])  17.1 us
    all_to_all x1, blocking collectives, local(): lax.all_to_all(outgoing, 'shard', split_axis=0, concat_axis=0, tiled=True)  16.5 us
    pallas_call x1, Pallas kernels, call_cin(): pl.pallas_call(cin_kernel, out_shape=(jax.ShapeDtypeStruct((samples,), F3...  12.4 us
    all_to_all x1, starting transfers between devices, local(): lax.all_to_all(ask, 'shard', split_axis=0, concat_axis=0, tiled=True)  10.3 us
    all_to_all x1, starting transfers between devices, local(): lax.all_to_all(call_hot(parts, (3 * tall,) * 3 + (None, 2 * tall), owners...  10.2 us
    pallas_call x1, Pallas kernels, call_scatter(): pl.pallas_call(functools.partial(scatter_kernel, places, rows), out_shape...  7.83 us
    all_to_all x1, waiting for transfers between devices, local(): lax.all_to_all(found, 'shard', split_axis=0, concat_axis=0, tiled=True)  5.05 us
  transfers between devices with their start and end apart: 10, of which 6 were waited for; matrix products, arithmetic and copies ran while one was open for 0% of the time, Pallas kernels for 8%

profile of v6, /device:TPU:1, one launch (start us, length us, event | category | flops | bytes accessed | tf_op | source)
XLA Modules:
  0.0 137.4 jit_solution(611563006971312473)
XLA Ops:
  0.6 0.0 copy-start
  0.7 2.2 %route.1 = (s32[32,128]{1,0:T(8,128)}, s32[320,128]{1,0:T(8,128)S(1)}) custom-call(s32[8,39]{1,0:T(8,128)} %row_hbm.1, s32[8,39]{1,0:T(8,128)} %owner_hbm.1, s32[8,39]{1,0:T(8,128)} %cold_ref.1), custom_call_target="tpu_custom_call" | custom-call | tf_op jit(solution)/shard_map/route/pallas_call | solution.py:251
  2.9 10.3 %all-to-all-start = ((s32[32,1,128]{2,1,0:T(1,128)}), s32[32,1,128]{2,1,0:T(1,128)S(1)}, u32[]{:S(2)}, u32[]{:S(2)}) async-start(s32[32,1,128]{2,1,0:T(1,128)} %bitcast.1), calls=%async_computation | async-start | bytes 32768 | tf_op jit(solution)/shard_map/all_to_all | solution.py:646
  13.2 0.0 copy-start.3
  13.2 1.0 copy-done.3
  14.3 0.7 copy-done.5
  15.0 0.7 copy-done.7
  15.7 1.3 hot_rows.1
  16.9 3.3 %all-to-all-done = s32[32,1,128]{2,1,0:T(1,128)S(1)} async-done(((s32[32,1,128]{2,1,0:T(1,128)}), s32[32,1,128]{2,1,0:T(1,128)S(1)}, u32[]{:S(2)}, u32[]{:S(2)}) %all-to-all-start) | async-done | bytes 16416 | tf_op jit(solution)/shard_map/all_to_all | solution.py:646
  20.2 0.1 reshape.18
  20.3 1.9 %gather_fusion = bf16[512,128]{1,0:T(8,128)(2,1)} fusion(bf16[4096,128]{1,0:T(8,128)(2,1)S(1)} %copy-done, s32[1024]{0:T(1024)S(1)} %pad_clamp_fusion), kind=kCustom, calls=%fused_computation | custom fusion | bytes 264192 | tf_op jit(solution)/shard_map/gather | solution.py:649
  22.2 4.3 %all-to-all-start.1 = ((bf16[32,16,128]{2,1,0:T(8,128)(2,1)}), bf16[32,16,128]{2,1,0:T(8,128)(2,1)S(1)}, u32[]{:S(2)}, u32[]{:S(2)}) async-start(bf16[32,16,128]{2,1,0:T(8,128)(2,1)} %bitcast.3), calls=%async_computation.1 | async-start | bytes 262144 | tf_op jit(solution)/shard_map/all_to_all | solution.py:650
  26.6 2.5 %prep.1 = (bf16[112,1872]{1,0:T(8,128)(2,1)}, bf16[1872,128]{1,0:T(8,128)(2,1)}, bf16[112,4368]{1,0:T(8,128)(2,1)}, bf16[4368,128]{1,0:T(8,128)(2,1)}, f32[112,128]{1,0:T(8,128)S(1)}) custom-call(bf16[100,1521]{1,0:T(8,128)(2,1)S(1)} %copy-done.4, bf16[100,3900]{1,0:T(8,128)(2,1)S(1)} %copy-done.1, bf16[100,3900]{1,0:T(8,128)(2,1)S(1)} %copy-done.2, ...), custom_call_target="tpu_custom_call" | custom-call | tf_op jit(solution)/shard_map/prep/pallas_call | solution.py:375
  29.2 5.1 %all-to-all-done.1 = bf16[32,16,128]{2,1,0:T(8,128)(2,1)S(1)} async-done(((bf16[32,16,128]{2,1,0:T(8,128)(2,1)}), bf16[32,16,128]{2,1,0:T(8,128)(2,1)S(1)}, u32[]{:S(2)}, u32[]{:S(2)}) %all-to-all-start.1) | async-done | bytes 131104 | tf_op jit(solution)/shard_map/all_to_all | solution.py:650
  34.3 12.4 %cin.1 = (f32[8]{0:T(128)}, bf16[32,80,128]{2,1,0:T(8,128)(2,1)S(1)}) custom-call(f32[8]{0:T(128)S(1)} %copy-done.8, s32[8,320]{1,0:T(8,128)S(1)} %get-tuple-element.18.hot_line_ref, s32[320,128]{1,0:T(8,128)S(1)} %get-tuple-element.19.slot_ref, bf16[512,128]{1,0:T(8,128)(2,1)S(1)} %bitcast.9, f32[3,100]{1,0:T(4,128)S(1)} %copy-done.6, ...), custom_call_target="tpu_custom_call" | custom-call | tf_op jit(solution)/shard_map/cin/pallas_call | solution.py:403
  46.6 16.5 %all_to_all.26.in_ref = bf16[32,80,128]{2,1,0:T(8,128)(2,1)S(1)} all-to-all(bf16[32,80,128]{2,1,0:T(8,128)(2,1)S(1)} %get-tuple-element.27), channel_id=1, replica_groups=mesh['group'=16,'shard'=32] {'shard'}, dimensions={0} | all-to-all | bytes 1310720 | tf_op jit(solution)/shard_map/all_to_all | solution.py:655
  63.1 0.2 merge.1
  63.3 13.6 %collective-permute-start.2 = (bf16[360,128]{1,0:T(8,128)(2,1)S(1)}, bf16[360,128]{1,0:T(8,128)(2,1)S(1)}, u32[]{:S(2)}, u32[]{:S(2)}) collective-permute-start(bf16[360,128]{1,0:T(8,128)(2,1)S(1)} %bitcast.10), channel_id=1, source_target_pairs={{0,256},{32,288},{64,320},{96,352},{128,384},{160,416},{192,448},{... | collective-permute-start | bytes 276488 | tf_op jit(solution)/shard_map/ppermute | solution.py:622
  76.9 1.9 %collective-permute-start.1 = (bf16[360,128]{1,0:T(8,128)(2,1)S(1)}, bf16[360,128]{1,0:T(8,128)(2,1)S(1)}, u32[]{:S(2)}, u32[]{:S(2)}) collective-permute-start(bf16[360,128]{1,0:T(8,128)(2,1)S(1)} %bitcast.11), channel_id=1, source_target_pairs={{0,384},{32,416},{64,448},{96,480},{128,0},{160,32},{192,64},{224,... | collective-permute-start | bytes 276488 | tf_op jit(solution)/shard_map/ppermute | solution.py:622
  78.8 7.3 %collective-permute-start = (bf16[360,128]{1,0:T(8,128)(2,1)S(1)}, bf16[360,128]{1,0:T(8,128)(2,1)S(1)}, u32[]{:S(2)}, u32[]{:S(2)}) collective-permute-start(bf16[360,128]{1,0:T(8,128)(2,1)S(1)} %bitcast.12), channel_id=1, source_target_pairs={{0,128},{32,160},{64,192},{96,224},{128,256},{160,288},{192,320},{... | collective-permute-start | bytes 276488 | tf_op jit(solution)/shard_map/ppermute | solution.py:622
  86.1 8.1 %collective-permute-done.1.refs_2_ = bf16[360,128]{1,0:T(8,128)(2,1)S(1)} collective-permute-done((bf16[360,128]{1,0:T(8,128)(2,1)S(1)}, bf16[360,128]{1,0:T(8,128)(2,1)S(1)}, u32[]{:S(2)}, u32[]{:S(2)}) %collective-permute-start.1) | collective-permute-done | bytes 92192 | tf_op jit(solution)/shard_map/ppermute | solution.py:622
  94.3 2.7 %collective-permute-start.4 = (bf16[1248,128]{1,0:T(8,128)(2,1)S(1)}, bf16[1248,128]{1,0:T(8,128)(2,1)S(1)}, u32[]{:S(2)}, u32[]{:S(2)}) collective-permute-start(bf16[1248,128]{1,0:T(8,128)(2,1)S(1)} %pack.1.refs_0_), channel_id=1, source_target_pairs={{0,480},{32,0},{64,32},{96,64},{128,96},{160,128},{192,160},{224,1... | collective-permute-start | bytes 958472 | tf_op jit(solution)/shard_map/ppermute | solution.py:622
  96.9 3.0 %collective-permute-start.3 = (bf16[1248,128]{1,0:T(8,128)(2,1)S(1)}, bf16[1248,128]{1,0:T(8,128)(2,1)S(1)}, u32[]{:S(2)}, u32[]{:S(2)}) collective-permute-start(bf16[1248,128]{1,0:T(8,128)(2,1)S(1)} %pack.1.refs_0_), channel_id=1, source_target_pairs={{0,32},{32,64},{64,96},{96,128},{128,160},{160,192},{192,224},{224... | collective-permute-start | bytes 958472 | tf_op jit(solution)/shard_map/ppermute | solution.py:622
  99.9 5.1 %collective-permute-done.4.refs_2_ = bf16[1248,128]{1,0:T(8,128)(2,1)S(1)} collective-permute-done((bf16[1248,128]{1,0:T(8,128)(2,1)S(1)}, bf16[1248,128]{1,0:T(8,128)(2,1)S(1)}, u32[]{:S(2)}, u32[]{:S(2)}) %collective-permute-start.4) | collective-permute-done | bytes 319520 | tf_op jit(solution)/shard_map/ppermute | solution.py:622
  105.1 1.9 %collective-permute-start.6 = (bf16[656,128]{1,0:T(8,128)(2,1)S(1)}, bf16[656,128]{1,0:T(8,128)(2,1)S(1)}, u32[]{:S(2)}, u32[]{:S(2)}) collective-permute-start(bf16[656,128]{1,0:T(8,128)(2,1)S(1)} %slice.16), channel_id=1, source_target_pairs={{0,480},{32,0},{64,32},{96,64},{128,96},{160,128},{192,160},{224,1... | collective-permute-start | bytes 503816 | tf_op jit(solution)/shard_map/ppermute | solution.py:622
  107.0 3.4 %collective-permute-start.5 = (bf16[592,128]{1,0:T(8,128)(2,1)S(1)}, bf16[592,128]{1,0:T(8,128)(2,1)S(1)}, u32[]{:S(2)}, u32[]{:S(2)}) collective-permute-start(bf16[592,128]{1,0:T(8,128)(2,1)S(1)} %slice.15), channel_id=1, source_target_pairs={{0,32},{32,64},{64,96},{96,128},{128,160},{160,192},{192,224},{224... | collective-permute-start | bytes 454664 | tf_op jit(solution)/shard_map/ppermute | solution.py:622
  110.4 3.8 %collective-permute-done.5.refs_3_ = bf16[592,128]{1,0:T(8,128)(2,1)S(1)} collective-permute-done((bf16[592,128]{1,0:T(8,128)(2,1)S(1)}, bf16[592,128]{1,0:T(8,128)(2,1)S(1)}, u32[]{:S(2)}, u32[]{:S(2)}) %collective-permute-start.5) | collective-permute-done | bytes 151584 | tf_op jit(solution)/shard_map/ppermute | solution.py:622
  114.2 0.9 hot_sum.1
  115.0 10.2 %all-to-all-start.3 = ((bf16[32,64,128]{2,1,0:T(8,128)(2,1)}), bf16[32,64,128]{2,1,0:T(8,128)(2,1)S(1)}, u32[]{:S(2)}, u32[]{:S(2)}) async-start(bf16[32,64,128]{2,1,0:T(8,128)(2,1)} %hot_sum.1), calls=%async_computation.3 | async-start | bytes 1048576 | tf_op jit(solution)/shard_map/all_to_all | solution.py:661
  125.2 7.8 %cold_scatter.1 = bf16[4096,128]{1,0:T(8,128)(2,1)} custom-call(bf16[1248,128]{1,0:T(8,128)(2,1)S(1)} %pack.1.refs_0_, bf16[1248,128]{1,0:T(8,128)(2,1)S(1)} %collective-permute-done.3.refs_1_, bf16[1248,128]{1,0:T(8,128)(2,1)S(1)} %collective-permute-done.4.refs_2_, bf16[592,128]{1,0:T(8,128)(2,1)S(1)} %collective-permute-done.5.refs_3_, ...), custom_call_target="tpu_custom_call" | custom-call | tf_op jit(solution)/shard_map/cold_scatter/pallas_call | solution.py:599
  133.1 3.6 %all-to-all-done.3 = bf16[32,64,128]{2,1,0:T(8,128)(2,1)S(1)} async-done(((bf16[32,64,128]{2,1,0:T(8,128)(2,1)}), bf16[32,64,128]{2,1,0:T(8,128)(2,1)S(1)}, u32[]{:S(2)}, u32[]{:S(2)}) %all-to-all-start.3) | async-done | bytes 524320 | tf_op jit(solution)/shard_map/all_to_all | solution.py:661
  136.7 0.8 copy.16
  (22 shorter events, 0.1 us)
Async XLA Ops:
  0.6 19.7 %copy-start = (bf16[4096,128]{1,0:T(8,128)(2,1)S(1)}, bf16[4096,128]{1,0:T(8,128)(2,1)}, u32[]{:S(2)}) copy-start(bf16[4096,128]{1,0:T(8,128)(2,1)} %param.17) | copy-start | bytes 3145732
  0.6 26.0 %copy-start.2 = (bf16[100,3900]{1,0:T(8,128)(2,1)S(1)}, bf16[100,3900]{1,0:T(8,128)(2,1)}, u32[]{:S(2)}) copy-start(bf16[100,3900]{1,0:T(8,128)(2,1)} %refs_2_.1) | copy-start | bytes 2340004
  0.7 26.0 %copy-start.1 = (bf16[100,3900]{1,0:T(8,128)(2,1)S(1)}, bf16[100,3900]{1,0:T(8,128)(2,1)}, u32[]{:S(2)}) copy-start(bf16[100,3900]{1,0:T(8,128)(2,1)} %refs_1_.1) | copy-start | bytes 2340004
  2.9 17.3 %all-to-all-start = ((s32[32,1,128]{2,1,0:T(1,128)}), s32[32,1,128]{2,1,0:T(1,128)S(1)}, u32[]{:S(2)}, u32[]{:S(2)}) async-start(s32[32,1,128]{2,1,0:T(1,128)} %bitcast.1), calls=%async_computation | async-start | bytes 32768 | tf_op jit(solution)/shard_map/all_to_all | solution.py:646
  13.2 1.0 copy-start.3
  14.3 0.7 copy-start.5
  15.0 0.7 copy-start.7
  15.7 11.0 %copy-start.4 = (bf16[100,1521]{1,0:T(8,128)(2,1)S(1)}, bf16[100,1521]{1,0:T(8,128)(2,1)}, u32[]{:S(2)}) copy-start(bf16[100,1521]{1,0:T(8,128)(2,1)} %refs_0_.1) | copy-start | bytes 912604
  15.7 11.0 %copy-start.6 = (f32[3,100]{1,0:T(4,128)S(1)}, f32[3,100]{1,0:T(4,128)}, u32[]{:S(2)}) copy-start(f32[3,100]{1,0:T(4,128)} %scale_ref.1) | copy-start | bytes 3604
  22.2 12.0 %copy-start.8 = (f32[8]{0:T(128)S(1)}, f32[8]{0:T(128)}, u32[]{:S(2)}) copy-start(f32[8]{0:T(128)} %gl_ref.1) | copy-start | bytes 100
  22.2 12.0 %all-to-all-start.1 = ((bf16[32,16,128]{2,1,0:T(8,128)(2,1)}), bf16[32,16,128]{2,1,0:T(8,128)(2,1)S(1)}, u32[]{:S(2)}, u32[]{:S(2)}) async-start(bf16[32,16,128]{2,1,0:T(8,128)(2,1)} %bitcast.3), calls=%async_computation.1 | async-start | bytes 262144 | tf_op jit(solution)/shard_map/all_to_all | solution.py:650
  63.3 22.8 %collective-permute-start.2 = (bf16[360,128]{1,0:T(8,128)(2,1)S(1)}, bf16[360,128]{1,0:T(8,128)(2,1)S(1)}, u32[]{:S(2)}, u32[]{:S(2)}) collective-permute-start(bf16[360,128]{1,0:T(8,128)(2,1)S(1)} %bitcast.10), channel_id=1, source_target_pairs={{0,256},{32,288},{64,320},{96,352},{128,384},{160,416},{192,448},{... | collective-permute-start | bytes 276488 | tf_op jit(solution)/shard_map/ppermute | solution.py:622
  76.9 17.3 %collective-permute-start.1 = (bf16[360,128]{1,0:T(8,128)(2,1)S(1)}, bf16[360,128]{1,0:T(8,128)(2,1)S(1)}, u32[]{:S(2)}, u32[]{:S(2)}) collective-permute-start(bf16[360,128]{1,0:T(8,128)(2,1)S(1)} %bitcast.11), channel_id=1, source_target_pairs={{0,384},{32,416},{64,448},{96,480},{128,0},{160,32},{192,64},{224,... | collective-permute-start | bytes 276488 | tf_op jit(solution)/shard_map/ppermute | solution.py:622
  78.8 15.4 %collective-permute-start = (bf16[360,128]{1,0:T(8,128)(2,1)S(1)}, bf16[360,128]{1,0:T(8,128)(2,1)S(1)}, u32[]{:S(2)}, u32[]{:S(2)}) collective-permute-start(bf16[360,128]{1,0:T(8,128)(2,1)S(1)} %bitcast.12), channel_id=1, source_target_pairs={{0,128},{32,160},{64,192},{96,224},{128,256},{160,288},{192,320},{... | collective-permute-start | bytes 276488 | tf_op jit(solution)/shard_map/ppermute | solution.py:622
  94.3 10.8 %collective-permute-start.4 = (bf16[1248,128]{1,0:T(8,128)(2,1)S(1)}, bf16[1248,128]{1,0:T(8,128)(2,1)S(1)}, u32[]{:S(2)}, u32[]{:S(2)}) collective-permute-start(bf16[1248,128]{1,0:T(8,128)(2,1)S(1)} %pack.1.refs_0_), channel_id=1, source_target_pairs={{0,480},{32,0},{64,32},{96,64},{128,96},{160,128},{192,160},{224,1... | collective-permute-start | bytes 958472 | tf_op jit(solution)/shard_map/ppermute | solution.py:622
  96.9 10.1 %collective-permute-start.3 = (bf16[1248,128]{1,0:T(8,128)(2,1)S(1)}, bf16[1248,128]{1,0:T(8,128)(2,1)S(1)}, u32[]{:S(2)}, u32[]{:S(2)}) collective-permute-start(bf16[1248,128]{1,0:T(8,128)(2,1)S(1)} %pack.1.refs_0_), channel_id=1, source_target_pairs={{0,32},{32,64},{64,96},{96,128},{128,160},{160,192},{192,224},{224... | collective-permute-start | bytes 958472 | tf_op jit(solution)/shard_map/ppermute | solution.py:622
  105.1 9.1 %collective-permute-start.6 = (bf16[656,128]{1,0:T(8,128)(2,1)S(1)}, bf16[656,128]{1,0:T(8,128)(2,1)S(1)}, u32[]{:S(2)}, u32[]{:S(2)}) collective-permute-start(bf16[656,128]{1,0:T(8,128)(2,1)S(1)} %slice.16), channel_id=1, source_target_pairs={{0,480},{32,0},{64,32},{96,64},{128,96},{160,128},{192,160},{224,1... | collective-permute-start | bytes 503816 | tf_op jit(solution)/shard_map/ppermute | solution.py:622
  107.0 7.1 %collective-permute-start.5 = (bf16[592,128]{1,0:T(8,128)(2,1)S(1)}, bf16[592,128]{1,0:T(8,128)(2,1)S(1)}, u32[]{:S(2)}, u32[]{:S(2)}) collective-permute-start(bf16[592,128]{1,0:T(8,128)(2,1)S(1)} %slice.15), channel_id=1, source_target_pairs={{0,32},{32,64},{64,96},{96,128},{128,160},{160,192},{192,224},{224... | collective-permute-start | bytes 454664 | tf_op jit(solution)/shard_map/ppermute | solution.py:622
  115.0 21.6 %all-to-all-start.3 = ((bf16[32,64,128]{2,1,0:T(8,128)(2,1)}), bf16[32,64,128]{2,1,0:T(8,128)(2,1)S(1)}, u32[]{:S(2)}, u32[]{:S(2)}) async-start(bf16[32,64,128]{2,1,0:T(8,128)(2,1)} %hot_sum.1), calls=%async_computation.3 | async-start | bytes 1048576 | tf_op jit(solution)/shard_map/all_to_all | solution.py:661

commit v7 on v6

--- a/solution.py
+++ b/solution.py
@@ -289,7 +289,7 @@
 
 
 def call_hot_rows(hot_row, is_cold, hot_table):
-    samples, fields = hot_row.shape
+    samples, _ = hot_row.shape
     total = samples * FP
     return pl.pallas_call(
         hot_rows_kernel,
@@ -625,7 +625,8 @@
     far = [move(block, apart), move(block, -apart), move(block, 2 * apart)]
     mine = call_pack([far[0], block, far[1], far[2]], rows)
     up, down = move(mine, 1), move(mine, -1)
-    up_half = move(up[: 2 * rows], 1)
+    up_tail = up[: 2 * rows]
+    up_half = move(up_tail, 1)
     down_half = move(down[rows : 3 * rows + share], -1)
     whole = (0, rows, 2 * rows, 3 * rows + share)
     sources = [(n, top) for n in range(3) for top in whole]
@@ -637,8 +638,7 @@
     hot_row, cold_row, cold_owner, is_cold, grad_logit, hot_table, cold_table,
     first_weight, second_weight, third_weight, out_weight,
 ):
-    samples, fields = hot_row.shape
-    breadth = hot_table.shape[1]
+    _, fields = hot_row.shape
     owners = lax.axis_size("shard")
     *forms, mix = call_prep((first_weight, second_weight), third_weight, out_weight, fields)
     ask, slot = call_route(cold_row, cold_owner, is_cold, owners)
@@ -658,10 +658,10 @@
     tall = rows + 8
     block = call_merge(incoming, ask_in, 1)[0]
     parts, places = exchange(block, tall)
-    hot_out = lax.all_to_all(
-        call_hot(parts, (3 * tall,) * 3 + (None, 2 * tall), owners, share),
-        "shard", split_axis=0, concat_axis=0, tiled=True,
+    hot_part = call_hot(
+        (*parts[0:3], parts[4]), (3 * tall,) * 3 + (2 * tall,), owners, share
     )
+    hot_out = lax.all_to_all(hot_part, "shard", split_axis=0, concat_axis=0, tiled=True)
     cold_total = call_scatter(parts, places, rows, cold_table.shape[0])
     hot_grad = hot_out.reshape(hot_table.shape)
     return (hot_grad, cold_total, logits)

time: 138 us -> 139 us (level)
  waiting for transfers between devices: 29 us -> 31.9 us
  starting transfers between devices: 58.5 us -> 56.1 us
    ppermute x7, waiting for transfers between devices: 17.1 us -> 23.5 us  [move(): lax.ppermute(x, 'group', [(i, (i + hop) % groups) for i in range(groups)])]
    all_to_all x1, waiting for transfers between devices: 3.6 us -> 0.01 us  [local(): lax.all_to_all(hot_part, 'shard', split_axis=0, concat_axis=0, tiled=True)]
    all_to_all x1, starting transfers between devices: 10.2 us -> 7.8 us  [local(): lax.all_to_all(hot_part, 'shard', split_axis=0, concat_axis=0, tiled=True)]
where the time goes in v7:
time: 139 us; the launch traced here: 138 us
  starting transfers between devices  56.1 us (40%)
  waiting for transfers between devices  31.9 us (23%)
  Pallas kernels  27.3 us (20%)
  blocking collectives  16.5 us (12%)
  local copies, waits for them, and re-layouts  5.24 us (4%)
    ppermute x7, starting transfers between devices, move(): lax.ppermute(x, 'group', [(i, (i + hop) % groups) for i in range(groups)])  33.6 us
    ppermute x7, waiting for transfers between devices, move(): lax.ppermute(x, 'group', [(i, (i + hop) % groups) for i in range(groups)])  23.5 us
    all_to_all x1, blocking collectives, local(): lax.all_to_all(outgoing, 'shard', split_axis=0, concat_axis=0, tiled=True)  16.5 us
    pallas_call x1, Pallas kernels, call_cin(): pl.pallas_call(cin_kernel, out_shape=(jax.ShapeDtypeStruct((samples,), F3...  12.4 us
    all_to_all x1, starting transfers between devices, local(): lax.all_to_all(ask, 'shard', split_axis=0, concat_axis=0, tiled=True)  10.3 us
    pallas_call x1, Pallas kernels, call_scatter(): pl.pallas_call(functools.partial(scatter_kernel, places, rows), out_shape...  7.83 us
    all_to_all x1, starting transfers between devices, local(): lax.all_to_all(hot_part, 'shard', split_axis=0, concat_axis=0, tiled=True)  7.8 us
    all_to_all x1, waiting for transfers between devices, local(): lax.all_to_all(found, 'shard', split_axis=0, concat_axis=0, tiled=True)  5.05 us
  transfers between devices with their start and end apart: 10, of which 6 were waited for; matrix products, arithmetic and copies ran while one was open for 0% of the time, Pallas kernels for 8%

profile of v7, /device:TPU:1, one launch (start us, length us, event | category | flops | bytes accessed | tf_op | source)
XLA Modules:
  0.0 137.9 jit_solution(3545308931840519573)
XLA Ops:
  0.6 0.0 copy-start
  0.7 2.2 %route.1 = (s32[32,128]{1,0:T(8,128)}, s32[320,128]{1,0:T(8,128)S(1)}) custom-call(s32[8,39]{1,0:T(8,128)} %row_hbm.1, s32[8,39]{1,0:T(8,128)} %owner_hbm.1, s32[8,39]{1,0:T(8,128)} %cold_ref.1), custom_call_target="tpu_custom_call" | custom-call | tf_op jit(solution)/shard_map/route/pallas_call | solution.py:251
  2.9 10.3 %all-to-all-start = ((s32[32,1,128]{2,1,0:T(1,128)}), s32[32,1,128]{2,1,0:T(1,128)S(1)}, u32[]{:S(2)}, u32[]{:S(2)}) async-start(s32[32,1,128]{2,1,0:T(1,128)} %bitcast.1), calls=%async_computation | async-start | bytes 32768 | tf_op jit(solution)/shard_map/all_to_all | solution.py:646
  13.2 0.0 copy-start.3
  13.2 1.0 copy-done.3
  14.3 0.7 copy-done.5
  15.0 0.7 copy-done.7
  15.7 1.3 hot_rows.1
  16.9 3.3 %all-to-all-done = s32[32,1,128]{2,1,0:T(1,128)S(1)} async-done(((s32[32,1,128]{2,1,0:T(1,128)}), s32[32,1,128]{2,1,0:T(1,128)S(1)}, u32[]{:S(2)}, u32[]{:S(2)}) %all-to-all-start) | async-done | bytes 16416 | tf_op jit(solution)/shard_map/all_to_all | solution.py:646
  20.2 0.1 reshape.18
  20.3 1.9 %gather_fusion = bf16[512,128]{1,0:T(8,128)(2,1)} fusion(bf16[4096,128]{1,0:T(8,128)(2,1)S(1)} %copy-done, s32[1024]{0:T(1024)S(1)} %pad_clamp_fusion), kind=kCustom, calls=%fused_computation | custom fusion | bytes 264192 | tf_op jit(solution)/shard_map/gather | solution.py:649
  22.2 4.3 %all-to-all-start.1 = ((bf16[32,16,128]{2,1,0:T(8,128)(2,1)}), bf16[32,16,128]{2,1,0:T(8,128)(2,1)S(1)}, u32[]{:S(2)}, u32[]{:S(2)}) async-start(bf16[32,16,128]{2,1,0:T(8,128)(2,1)} %bitcast.3), calls=%async_computation.1 | async-start | bytes 262144 | tf_op jit(solution)/shard_map/all_to_all | solution.py:650
  26.6 2.5 %prep.1 = (bf16[112,1872]{1,0:T(8,128)(2,1)}, bf16[1872,128]{1,0:T(8,128)(2,1)}, bf16[112,4368]{1,0:T(8,128)(2,1)}, bf16[4368,128]{1,0:T(8,128)(2,1)}, f32[112,128]{1,0:T(8,128)S(1)}) custom-call(bf16[100,1521]{1,0:T(8,128)(2,1)S(1)} %copy-done.4, bf16[100,3900]{1,0:T(8,128)(2,1)S(1)} %copy-done.1, bf16[100,3900]{1,0:T(8,128)(2,1)S(1)} %copy-done.2, ...), custom_call_target="tpu_custom_call" | custom-call | tf_op jit(solution)/shard_map/prep/pallas_call | solution.py:375
  29.2 5.1 %all-to-all-done.1 = bf16[32,16,128]{2,1,0:T(8,128)(2,1)S(1)} async-done(((bf16[32,16,128]{2,1,0:T(8,128)(2,1)}), bf16[32,16,128]{2,1,0:T(8,128)(2,1)S(1)}, u32[]{:S(2)}, u32[]{:S(2)}) %all-to-all-start.1) | async-done | bytes 131104 | tf_op jit(solution)/shard_map/all_to_all | solution.py:650
  34.3 12.4 %cin.1 = (f32[8]{0:T(128)}, bf16[32,80,128]{2,1,0:T(8,128)(2,1)S(1)}) custom-call(f32[8]{0:T(128)S(1)} %copy-done.8, s32[8,320]{1,0:T(8,128)S(1)} %get-tuple-element.18.hot_line_ref, s32[320,128]{1,0:T(8,128)S(1)} %get-tuple-element.19.slot_ref, bf16[512,128]{1,0:T(8,128)(2,1)S(1)} %bitcast.9, f32[3,100]{1,0:T(4,128)S(1)} %copy-done.6, ...), custom_call_target="tpu_custom_call" | custom-call | tf_op jit(solution)/shard_map/cin/pallas_call | solution.py:403
  46.6 16.5 %all_to_all.26.in_ref = bf16[32,80,128]{2,1,0:T(8,128)(2,1)S(1)} all-to-all(bf16[32,80,128]{2,1,0:T(8,128)(2,1)S(1)} %get-tuple-element.27), channel_id=1, replica_groups=mesh['group'=16,'shard'=32] {'shard'}, dimensions={0} | all-to-all | bytes 1310720 | tf_op jit(solution)/shard_map/all_to_all | solution.py:655
  63.1 0.2 merge.1
  63.3 13.6 %collective-permute-start.2 = (bf16[360,128]{1,0:T(8,128)(2,1)S(1)}, bf16[360,128]{1,0:T(8,128)(2,1)S(1)}, u32[]{:S(2)}, u32[]{:S(2)}) collective-permute-start(bf16[360,128]{1,0:T(8,128)(2,1)S(1)} %bitcast.10), channel_id=1, source_target_pairs={{0,256},{32,288},{64,320},{96,352},{128,384},{160,416},{192,448},{... | collective-permute-start | bytes 276488 | tf_op jit(solution)/shard_map/ppermute | solution.py:622
  76.9 1.9 %collective-permute-start.1 = (bf16[360,128]{1,0:T(8,128)(2,1)S(1)}, bf16[360,128]{1,0:T(8,128)(2,1)S(1)}, u32[]{:S(2)}, u32[]{:S(2)}) collective-permute-start(bf16[360,128]{1,0:T(8,128)(2,1)S(1)} %bitcast.11), channel_id=1, source_target_pairs={{0,384},{32,416},{64,448},{96,480},{128,0},{160,32},{192,64},{224,... | collective-permute-start | bytes 276488 | tf_op jit(solution)/shard_map/ppermute | solution.py:622
  78.8 7.3 %collective-permute-start = (bf16[360,128]{1,0:T(8,128)(2,1)S(1)}, bf16[360,128]{1,0:T(8,128)(2,1)S(1)}, u32[]{:S(2)}, u32[]{:S(2)}) collective-permute-start(bf16[360,128]{1,0:T(8,128)(2,1)S(1)} %bitcast.12), channel_id=1, source_target_pairs={{0,128},{32,160},{64,192},{96,224},{128,256},{160,288},{192,320},{... | collective-permute-start | bytes 276488 | tf_op jit(solution)/shard_map/ppermute | solution.py:622
  86.1 8.1 %collective-permute-done.1.refs_2_ = bf16[360,128]{1,0:T(8,128)(2,1)S(1)} collective-permute-done((bf16[360,128]{1,0:T(8,128)(2,1)S(1)}, bf16[360,128]{1,0:T(8,128)(2,1)S(1)}, u32[]{:S(2)}, u32[]{:S(2)}) %collective-permute-start.1) | collective-permute-done | bytes 92192 | tf_op jit(solution)/shard_map/ppermute | solution.py:622
  94.3 2.6 %collective-permute-start.4 = (bf16[1248,128]{1,0:T(8,128)(2,1)S(1)}, bf16[1248,128]{1,0:T(8,128)(2,1)S(1)}, u32[]{:S(2)}, u32[]{:S(2)}) collective-permute-start(bf16[1248,128]{1,0:T(8,128)(2,1)S(1)} %pack.1.refs_0_), channel_id=1, source_target_pairs={{0,480},{32,0},{64,32},{96,64},{128,96},{160,128},{192,160},{224,1... | collective-permute-start | bytes 958472 | tf_op jit(solution)/shard_map/ppermute | solution.py:622
  96.9 3.0 %collective-permute-start.3 = (bf16[1248,128]{1,0:T(8,128)(2,1)S(1)}, bf16[1248,128]{1,0:T(8,128)(2,1)S(1)}, u32[]{:S(2)}, u32[]{:S(2)}) collective-permute-start(bf16[1248,128]{1,0:T(8,128)(2,1)S(1)} %pack.1.refs_0_), channel_id=1, source_target_pairs={{0,32},{32,64},{64,96},{96,128},{128,160},{160,192},{192,224},{224... | collective-permute-start | bytes 958472 | tf_op jit(solution)/shard_map/ppermute | solution.py:622
  99.9 5.1 %collective-permute-done.4.refs_2_ = bf16[1248,128]{1,0:T(8,128)(2,1)S(1)} collective-permute-done((bf16[1248,128]{1,0:T(8,128)(2,1)S(1)}, bf16[1248,128]{1,0:T(8,128)(2,1)S(1)}, u32[]{:S(2)}, u32[]{:S(2)}) %collective-permute-start.4) | collective-permute-done | bytes 319520 | tf_op jit(solution)/shard_map/ppermute | solution.py:622
  105.1 3.2 %collective-permute-start.5 = (bf16[656,128]{1,0:T(8,128)(2,1)S(1)}, bf16[656,128]{1,0:T(8,128)(2,1)S(1)}, u32[]{:S(2)}, u32[]{:S(2)}) collective-permute-start(bf16[656,128]{1,0:T(8,128)(2,1)S(1)} %slice.15), channel_id=1, source_target_pairs={{0,480},{32,0},{64,32},{96,64},{128,96},{160,128},{192,160},{224,1... | collective-permute-start | bytes 503816 | tf_op jit(solution)/shard_map/ppermute | solution.py:622
  108.3 2.9 %collective-permute-done.5.refs_3_.refs_4_ = bf16[656,128]{1,0:T(8,128)(2,1)S(1)} collective-permute-done((bf16[656,128]{1,0:T(8,128)(2,1)S(1)}, bf16[656,128]{1,0:T(8,128)(2,1)S(1)}, u32[]{:S(2)}, u32[]{:S(2)}) %collective-permute-start.5) | collective-permute-done | bytes 167968 | tf_op jit(solution)/shard_map/ppermute | solution.py:622
  111.2 0.9 hot_sum.1
  112.0 7.8 %all-to-all-start.3 = ((bf16[32,64,128]{2,1,0:T(8,128)(2,1)}), bf16[32,64,128]{2,1,0:T(8,128)(2,1)S(1)}, u32[]{:S(2)}, u32[]{:S(2)}) async-start(bf16[32,64,128]{2,1,0:T(8,128)(2,1)} %hot_sum.1), calls=%async_computation.3 | async-start | bytes 1048576 | tf_op jit(solution)/shard_map/all_to_all | solution.py:664
  119.9 2.0 %collective-permute-start.6 = (bf16[592,128]{1,0:T(8,128)(2,1)S(1)}, bf16[592,128]{1,0:T(8,128)(2,1)S(1)}, u32[]{:S(2)}, u32[]{:S(2)}) collective-permute-start(bf16[592,128]{1,0:T(8,128)(2,1)S(1)} %slice.16), channel_id=1, source_target_pairs={{0,32},{32,64},{64,96},{96,128},{128,160},{160,192},{192,224},{224... | collective-permute-start | bytes 454664 | tf_op jit(solution)/shard_map/ppermute | solution.py:622
  121.9 7.3 %collective-permute-done.6.refs_3_ = bf16[592,128]{1,0:T(8,128)(2,1)S(1)} collective-permute-done((bf16[592,128]{1,0:T(8,128)(2,1)S(1)}, bf16[592,128]{1,0:T(8,128)(2,1)S(1)}, u32[]{:S(2)}, u32[]{:S(2)}) %collective-permute-start.6) | collective-permute-done | bytes 151584 | tf_op jit(solution)/shard_map/ppermute | solution.py:622
  129.2 7.8 %cold_scatter.1 = bf16[4096,128]{1,0:T(8,128)(2,1)} custom-call(bf16[1248,128]{1,0:T(8,128)(2,1)S(1)} %pack.1.refs_0_, bf16[1248,128]{1,0:T(8,128)(2,1)S(1)} %collective-permute-done.3.refs_1_, bf16[1248,128]{1,0:T(8,128)(2,1)S(1)} %collective-permute-done.4.refs_2_, bf16[592,128]{1,0:T(8,128)(2,1)S(1)} %collective-permute-done.6.refs_3_, ...), custom_call_target="tpu_custom_call" | custom-call | tf_op jit(solution)/shard_map/cold_scatter/pallas_call | solution.py:599
  137.1 0.8 copy.16
  (22 shorter events, 0.1 us)
Async XLA Ops:
  0.6 19.7 %copy-start = (bf16[4096,128]{1,0:T(8,128)(2,1)S(1)}, bf16[4096,128]{1,0:T(8,128)(2,1)}, u32[]{:S(2)}) copy-start(bf16[4096,128]{1,0:T(8,128)(2,1)} %param.17) | copy-start | bytes 3145732
  0.6 26.0 %copy-start.2 = (bf16[100,3900]{1,0:T(8,128)(2,1)S(1)}, bf16[100,3900]{1,0:T(8,128)(2,1)}, u32[]{:S(2)}) copy-start(bf16[100,3900]{1,0:T(8,128)(2,1)} %refs_2_.1) | copy-start | bytes 2340004
  0.7 26.0 %copy-start.1 = (bf16[100,3900]{1,0:T(8,128)(2,1)S(1)}, bf16[100,3900]{1,0:T(8,128)(2,1)}, u32[]{:S(2)}) copy-start(bf16[100,3900]{1,0:T(8,128)(2,1)} %refs_1_.1) | copy-start | bytes 2340004
  2.9 17.3 %all-to-all-start = ((s32[32,1,128]{2,1,0:T(1,128)}), s32[32,1,128]{2,1,0:T(1,128)S(1)}, u32[]{:S(2)}, u32[]{:S(2)}) async-start(s32[32,1,128]{2,1,0:T(1,128)} %bitcast.1), calls=%async_computation | async-start | bytes 32768 | tf_op jit(solution)/shard_map/all_to_all | solution.py:646
  13.2 1.0 copy-start.3
  14.3 0.7 copy-start.5
  15.0 0.7 copy-start.7
  15.7 11.0 %copy-start.4 = (bf16[100,1521]{1,0:T(8,128)(2,1)S(1)}, bf16[100,1521]{1,0:T(8,128)(2,1)}, u32[]{:S(2)}) copy-start(bf16[100,1521]{1,0:T(8,128)(2,1)} %refs_0_.1) | copy-start | bytes 912604
  15.7 11.0 %copy-start.6 = (f32[3,100]{1,0:T(4,128)S(1)}, f32[3,100]{1,0:T(4,128)}, u32[]{:S(2)}) copy-start(f32[3,100]{1,0:T(4,128)} %scale_ref.1) | copy-start | bytes 3604
  22.2 12.0 %copy-start.8 = (f32[8]{0:T(128)S(1)}, f32[8]{0:T(128)}, u32[]{:S(2)}) copy-start(f32[8]{0:T(128)} %gl_ref.1) | copy-start | bytes 100
  22.2 12.0 %all-to-all-start.1 = ((bf16[32,16,128]{2,1,0:T(8,128)(2,1)}), bf16[32,16,128]{2,1,0:T(8,128)(2,1)S(1)}, u32[]{:S(2)}, u32[]{:S(2)}) async-start(bf16[32,16,128]{2,1,0:T(8,128)(2,1)} %bitcast.3), calls=%async_computation.1 | async-start | bytes 262144 | tf_op jit(solution)/shard_map/all_to_all | solution.py:650
  63.3 22.8 %collective-permute-start.2 = (bf16[360,128]{1,0:T(8,128)(2,1)S(1)}, bf16[360,128]{1,0:T(8,128)(2,1)S(1)}, u32[]{:S(2)}, u32[]{:S(2)}) collective-permute-start(bf16[360,128]{1,0:T(8,128)(2,1)S(1)} %bitcast.10), channel_id=1, source_target_pairs={{0,256},{32,288},{64,320},{96,352},{128,384},{160,416},{192,448},{... | collective-permute-start | bytes 276488 | tf_op jit(solution)/shard_map/ppermute | solution.py:622
  76.9 17.4 %collective-permute-start.1 = (bf16[360,128]{1,0:T(8,128)(2,1)S(1)}, bf16[360,128]{1,0:T(8,128)(2,1)S(1)}, u32[]{:S(2)}, u32[]{:S(2)}) collective-permute-start(bf16[360,128]{1,0:T(8,128)(2,1)S(1)} %bitcast.11), channel_id=1, source_target_pairs={{0,384},{32,416},{64,448},{96,480},{128,0},{160,32},{192,64},{224,... | collective-permute-start | bytes 276488 | tf_op jit(solution)/shard_map/ppermute | solution.py:622
  78.8 15.4 %collective-permute-start = (bf16[360,128]{1,0:T(8,128)(2,1)S(1)}, bf16[360,128]{1,0:T(8,128)(2,1)S(1)}, u32[]{:S(2)}, u32[]{:S(2)}) collective-permute-start(bf16[360,128]{1,0:T(8,128)(2,1)S(1)} %bitcast.12), channel_id=1, source_target_pairs={{0,128},{32,160},{64,192},{96,224},{128,256},{160,288},{192,320},{... | collective-permute-start | bytes 276488 | tf_op jit(solution)/shard_map/ppermute | solution.py:622
  94.3 10.8 %collective-permute-start.4 = (bf16[1248,128]{1,0:T(8,128)(2,1)S(1)}, bf16[1248,128]{1,0:T(8,128)(2,1)S(1)}, u32[]{:S(2)}, u32[]{:S(2)}) collective-permute-start(bf16[1248,128]{1,0:T(8,128)(2,1)S(1)} %pack.1.refs_0_), channel_id=1, source_target_pairs={{0,480},{32,0},{64,32},{96,64},{128,96},{160,128},{192,160},{224,1... | collective-permute-start | bytes 958472 | tf_op jit(solution)/shard_map/ppermute | solution.py:622
  96.9 11.4 %collective-permute-start.3 = (bf16[1248,128]{1,0:T(8,128)(2,1)S(1)}, bf16[1248,128]{1,0:T(8,128)(2,1)S(1)}, u32[]{:S(2)}, u32[]{:S(2)}) collective-permute-start(bf16[1248,128]{1,0:T(8,128)(2,1)S(1)} %pack.1.refs_0_), channel_id=1, source_target_pairs={{0,32},{32,64},{64,96},{96,128},{128,160},{160,192},{192,224},{224... | collective-permute-start | bytes 958472 | tf_op jit(solution)/shard_map/ppermute | solution.py:622
  105.1 6.1 %collective-permute-start.5 = (bf16[656,128]{1,0:T(8,128)(2,1)S(1)}, bf16[656,128]{1,0:T(8,128)(2,1)S(1)}, u32[]{:S(2)}, u32[]{:S(2)}) collective-permute-start(bf16[656,128]{1,0:T(8,128)(2,1)S(1)} %slice.15), channel_id=1, source_target_pairs={{0,480},{32,0},{64,32},{96,64},{128,96},{160,128},{192,160},{224,1... | collective-permute-start | bytes 503816 | tf_op jit(solution)/shard_map/ppermute | solution.py:622
  112.0 25.0 %all-to-all-start.3 = ((bf16[32,64,128]{2,1,0:T(8,128)(2,1)}), bf16[32,64,128]{2,1,0:T(8,128)(2,1)S(1)}, u32[]{:S(2)}, u32[]{:S(2)}) async-start(bf16[32,64,128]{2,1,0:T(8,128)(2,1)} %hot_sum.1), calls=%async_computation.3 | async-start | bytes 1048576 | tf_op jit(solution)/shard_map/all_to_all | solution.py:664
  119.9 9.4 %collective-permute-start.6 = (bf16[592,128]{1,0:T(8,128)(2,1)S(1)}, bf16[592,128]{1,0:T(8,128)(2,1)S(1)}, u32[]{:S(2)}, u32[]{:S(2)}) collective-permute-start(bf16[592,128]{1,0:T(8,128)(2,1)S(1)} %slice.16), channel_id=1, source_target_pairs={{0,32},{32,64},{64,96},{96,128},{128,160},{160,192},{192,224},{224... | collective-permute-start | bytes 454664 | tf_op jit(solution)/shard_map/ppermute | solution.py:622
